TPU v7x, 32 devices: a whole 2x2x4 slice. The times are simulated.
32 devices in a mesh: ctx: 8 (over y, x, core), tp: 4 (over z).
Axes of the slice: x: 2, y: 2, z: 4, core: 2. Of those that a mesh axis runs over, the one named last changes fastest.
Arguments:
- queries: bfloat16 [1024, 32, 128], P('ctx', 'tp'), may hold values from -8 to 8
- window_keys: bfloat16 [1024, 4, 128], P('ctx', 'tp'), may hold values from -8 to 8
- window_values: bfloat16 [1024, 4, 128], P('ctx', 'tp'), may hold values from -6 to 6
- anchor_keys: bfloat16 [512, 4, 128], P('ctx', 'tp'), may hold values from -8 to 8
- anchor_values: bfloat16 [512, 4, 128], P('ctx', 'tp'), may hold values from -6 to 6
- passing_rows: int32 [8, 32], replicated, may hold values from 0 to 127, as said below
- block_of_device: int32 [8], replicated, may hold values from 0 to 7, each once
- out_weight: bfloat16 [4096, 4096], P(None, 'tp'), may hold values from -0.09375 to 0.09375
Outputs:
- mixed: bfloat16 [4096, 1024], P('tp', 'ctx')
Inputs may be any that keep to these rules, and one draw needn't show every extreme that they name: `passing_rows`: each row holds 32 different positions. `block_of_device`: every block number appears once.
All inputs are finite; a program needn't handle non-finite values.
Results may differ from a plain program's by a relative error of at most 0.013.
Values may be sent and summed in bfloat16 or wider, within the bound.
No kernel may reach another device: no remote copies, remote signals or barrier semaphores. Data moves between devices by JAX's collectives and lax.ppermute only.
A program may use at most 128 MiB of HBM per device.

v0:
```python
import functools
import math

import jax
import jax.numpy as jnp
from jax import lax
from jax.experimental import pallas as pl
from jax.experimental.pallas import tpu as pltpu
from jax.sharding import PartitionSpec as P


BF16 = jnp.bfloat16
F32 = jnp.float32
HIDDEN = -1e30
VMEM = pl.BlockSpec(memory_space=pltpu.VMEM)
HBM = pl.BlockSpec(memory_space=pltpu.HBM)
DMA = pltpu.SemaphoreType.DMA
PAIR = 2


def dot(a, b, a_dim, b_dim):
    return lax.dot_general(a, b, (((a_dim,), (b_dim,)), ((), ())), preferred_element_type=F32)


def call(kernel, inputs, out_shape, flops, in_specs=None, scratch=()):
    if in_specs:
        inputs = [pltpu.with_memory_space_constraint(x, pltpu.HBM) if s is HBM else x for x, s in zip(inputs, in_specs)]
    moved = sum(x.size * x.dtype.itemsize for x in inputs)
    return pl.pallas_call(
        kernel,
        out_shape=out_shape,
        in_specs=in_specs or [VMEM] * len(inputs),
        out_specs=jax.tree.map(lambda _: VMEM, out_shape),
        scratch_shapes=scratch,
        compiler_params=pltpu.CompilerParams(vmem_limit_bytes=32 << 20),
        cost_estimate=pl.CostEstimate(flops=flops, bytes_accessed=moved, transcendentals=0),
    )(*inputs)


def fetch(pairs, sems):
    copies = [pltpu.make_async_copy(a, b, sems.at[i]) for i, (a, b) in enumerate(pairs)]
    for copy in copies:
        copy.start()
    return copies


def wait(copies):
    for copy in copies:
        copy.wait()


def pack_kernel(rows_hbm, wk_hbm, wv_hbm, ak_hbm, av_hbm, out_ref, rows_ref, wk_ref, wv_ref, sems):
    anchors, retained = ak_hbm.shape[0], rows_ref.shape[1]
    first = 2 * anchors
    pairs = [
        (rows_hbm, rows_ref),
        (wk_hbm, wk_ref),
        (wv_hbm, wv_ref),
        (ak_hbm, out_ref.at[0:anchors, :]),
        (av_hbm, out_ref.at[anchors:first, :]),
    ]
    wait(fetch(pairs, sems))
    slot = lax.axis_index("ctx")
    chosen = rows_ref[pl.ds(slot, 1), :]
    places = lax.broadcasted_iota(jnp.int32, (wk_ref.shape[0], retained), 0)
    one_hot = (places == chosen).astype(BF16)
    out_ref[first : first + retained, :] = dot(one_hot, wk_ref[...], 0, 0).astype(BF16)
    out_ref[first + retained :, :] = dot(one_hot, wv_ref[...], 0, 0).astype(BF16)


def fold(q, before, groups, value_cols, factor):
    scores = jnp.concatenate([mask(dot(keys, q, 1, 1)) for keys, mask in groups], axis=0)
    top = jnp.max(scores, axis=0, keepdims=True)
    if before is not None:
        top = jnp.maximum(top, before[0])
    weights = jnp.exp2((scores - top) * factor)
    total = jnp.sum(weights, axis=0, keepdims=True)
    summed = dot(value_cols, weights.astype(BF16), 1, 0)
    if before is not None:
        fade = jnp.exp2((before[0] - top) * factor)
        total = total + before[1] * fade
        summed = summed + before[2] * fade
    return top, total, summed


def factor_of(size):
    return size ** (-0.5) * math.log2(math.e)


def chunk_of(w_hbm, at, rows):
    chunk = order_of(lax.axis_index("tp"))[at]
    return w_hbm.at[pl.ds(pl.multiple_of(chunk * rows, 16), rows), :]


def own_kernel(blocks_hbm, q_hbm, wk_hbm, wv_hbm, w_hbm, qh_ref, hide_ref, w_ref, top_ref, total_ref, summed_ref,
               blocks_ref, q_ref, wk_ref, wv_ref, qf_ref, sems):
    pairs = [(blocks_hbm, blocks_ref), (q_hbm, q_ref), (wk_hbm, wk_ref), (wv_hbm, wv_ref)]
    pairs.append((chunk_of(w_hbm, 0, w_ref.shape[0]), w_ref))
    copies = fetch(pairs, sems)
    wait(copies[:-1])
    tok_rows, size = wk_ref.shape
    heads = q_ref.shape[0] // tok_rows
    slot = lax.axis_index("ctx")
    own_block = blocks_ref[slot]
    for j in range(blocks_ref.shape[0]):
        bias = jnp.where(blocks_ref[slot ^ j] < own_block, 0.0, HIDDEN)
        hide_ref[j : j + 1, :] = jnp.full((1, hide_ref.shape[1]), bias, F32)
    qf_ref[...] = q_ref[...].astype(F32)
    lanes = PAIR * tok_rows
    key_at = lax.broadcasted_iota(jnp.int32, (tok_rows, lanes), 0)
    row_at = lax.broadcasted_iota(jnp.int32, (tok_rows, lanes), 1) % tok_rows
    causal = key_at <= row_at
    value_cols = wv_ref[...].T
    for h in range(0, heads, PAIR):
        for j in range(h, h + PAIR):
            qh_ref[j * tok_rows : (j + 1) * tok_rows, :] = qf_ref[
                pl.ds(j, tok_rows, stride=heads), :
            ].astype(BF16)
        cols = slice(h * tok_rows, (h + PAIR) * tok_rows)
        groups = [(wk_ref[...], lambda s: jnp.where(causal, s, HIDDEN))]
        state = fold(qh_ref[cols, :], None, groups, value_cols, factor_of(size))
        top_ref[:, cols], total_ref[:, cols], summed_ref[:, cols] = state
    wait(copies[-1:])


def rows_of(block_ref, anchors, retained):
    slots, _, size = block_ref.shape
    first = 2 * anchors
    take = lambda a, n: block_ref[:, a : a + n, :].reshape(slots * n, size)
    seen, past = take(0, anchors), take(first, retained)
    values = jnp.concatenate([take(anchors, anchors), take(first + retained, retained)], axis=0)
    return seen, past, values.T


def hidden_rows(hide_ref, order, retained, lanes):
    width = hide_ref.shape[1]
    rows = [jnp.broadcast_to(hide_ref[j : j + 1, :], (retained, width)) for j in order]
    column = jnp.concatenate(rows, axis=0)
    return jnp.concatenate([column] * (lanes // width), axis=1)


def fold_blocks(order, anchors, retained, qh_ref, hide_ref, block_ref, state_refs, finish):
    top_ref, total_ref, summed_ref = state_refs
    tok_rows = hide_ref.shape[1]
    size = qh_ref.shape[1]
    heads = qh_ref.shape[0] // tok_rows
    seen, past, value_cols = rows_of(block_ref, anchors, retained)
    bias = hidden_rows(hide_ref, order, retained, PAIR * tok_rows)
    groups = [(seen, lambda s: s), (past, lambda s: s + bias)]
    for h in range(0, heads, PAIR):
        cols = slice(h * tok_rows, (h + PAIR) * tok_rows)
        before = (top_ref[:, cols], total_ref[:, cols], summed_ref[:, cols])
        finish(h, cols, fold(qh_ref[cols, :], before, groups, value_cols, factor_of(size)))


def early_kernel(order, anchors, retained, qh_ref, hide_ref, block_ref, top0, total0, summed0, w_hbm,
                 w_ref, top_ref, total_ref, summed_ref, sems):
    copies = fetch([(chunk_of(w_hbm, 1, w_ref.shape[0]), w_ref)], sems)

    def finish(h, cols, state):
        top_ref[:, cols], total_ref[:, cols], summed_ref[:, cols] = state

    fold_blocks(order, anchors, retained, qh_ref, hide_ref, block_ref, (top0, total0, summed0), finish)
    wait(copies)


def project(w_ref, att_ref, out_ref):
    rows = out_ref.shape[0]
    tile = min(256, rows)
    for start in range(0, rows, tile):
        part = dot(w_ref[start : start + tile, :], att_ref[...], 1, 0)
        out_ref[start : start + tile, :] = part.astype(out_ref.dtype)


def order_of(me):
    far = jnp.where(me % 2 == 0, 3, 0)
    second = jnp.where((me == 0) | (me == 1), 2, 1)
    third = jnp.where(me == 0, 1, jnp.where(me == 1, 3, jnp.where(me == 2, 0, 2)))
    return far, second, third, me


def late_kernel(order, anchors, retained, qh_ref, hide_ref, block_ref, top0, total0, summed0, w_ref, w_hbm,
                att_ref, first_ref, next_ref, sems):
    copies = fetch([(chunk_of(w_hbm, 2, next_ref.shape[0]), next_ref)], sems)
    tok_rows = hide_ref.shape[1]
    size = qh_ref.shape[1]

    def finish(h, cols, state):
        _, total, summed = state
        attended = (summed / total).astype(BF16)
        for j in range(PAIR):
            att_ref[(h + j) * size : (h + j + 1) * size, :] = attended[:, j * tok_rows : (j + 1) * tok_rows]

    fold_blocks(order, anchors, retained, qh_ref, hide_ref, block_ref, (top0, total0, summed0), finish)
    project(w_ref, att_ref, first_ref)
    wait(copies)


def second_kernel(att_ref, w_ref, w_hbm, out_ref, next_ref, sems):
    copies = fetch([(chunk_of(w_hbm, 3, next_ref.shape[0]), next_ref)], sems)
    project(w_ref, att_ref, out_ref)
    wait(copies)


def third_kernel(att_ref, w_ref, last_ref, out_ref, own_ref):
    project(w_ref, att_ref, out_ref)
    project(last_ref, att_ref, own_ref)


def add(*parts):
    return functools.reduce(jnp.add, [p.astype(F32) for p in parts]).astype(BF16)


def layer(queries, window_keys, window_values, anchor_keys, anchor_values, passing_rows, block_of_device, out_weight):
    tok_rows, heads, size = queries.shape
    anchors, retained = anchor_keys.shape[0], passing_rows.shape[1]
    slots = block_of_device.shape[0]
    flat = lambda x: x.reshape(x.shape[0], size)
    wk, wv = flat(window_keys), flat(window_values)
    packed = 2 * (anchors + retained)
    shape = jax.ShapeDtypeStruct
    tp = lax.axis_size("tp")
    chunk_rows = out_weight.shape[0] // tp
    features = heads * size
    row = lambda n: shape((n, size), BF16)
    chunk, weight = shape((chunk_rows, tok_rows), BF16), shape((chunk_rows, features), BF16)
    chunk_flops = 2 * chunk_rows * tok_rows * features
    block = call(
        pack_kernel,
        (passing_rows, wk, wv, flat(anchor_keys), flat(anchor_values)),
        row(packed),
        4 * retained * tok_rows * size,
        in_specs=[HBM] * 5,
        scratch=[
            pltpu.VMEM(passing_rows.shape, jnp.int32),
            pltpu.VMEM((tok_rows, size), BF16),
            pltpu.VMEM((tok_rows, size), BF16),
            DMA((5,)),
        ],
    )
    query_rows = heads * tok_rows
    stats = (
        shape((1, query_rows), F32),
        shape((1, query_rows), F32),
        shape((size, query_rows), F32),
    )
    qh, hide, w_first, *state = call(
        own_kernel,
        (block_of_device, queries.reshape(query_rows, size), wk, wv, out_weight),
        (row(query_rows), shape((slots, tok_rows), F32), weight, *stats),
        4 * query_rows * tok_rows * size,
        in_specs=[HBM] * 5,
        scratch=[
            pltpu.SMEM((slots,), jnp.int32),
            pltpu.VMEM((query_rows, size), BF16),
            pltpu.VMEM((tok_rows, size), BF16),
            pltpu.VMEM((tok_rows, size), BF16),
            pltpu.VMEM((query_rows, size), F32),
            DMA((5,)),
        ],
    )
    order = [0]
    step = slots // 2
    held = block
    while step > 1:
        other = lax.ppermute(held, "ctx", [(i, i ^ step) for i in range(slots)])
        held = jnp.concatenate([held, other], axis=0)
        order = order + [j ^ step for j in order]
        step //= 2
    other = lax.ppermute(held, "ctx", [(i, i ^ step) for i in range(slots)])
    late_order = [j ^ step for j in order]
    half = (slots // 2, packed, size)
    fold_flops = 4 * query_rows * (slots // 2) * (anchors + retained) * size
    w_second, *state = call(
        functools.partial(early_kernel, order, anchors, retained),
        (qh, hide, held.reshape(half), *state, out_weight),
        (weight, *stats),
        fold_flops,
        in_specs=[VMEM] * 6 + [HBM],
        scratch=[DMA((1,))],
    )
    att, first, w_third = call(
        functools.partial(late_kernel, late_order, anchors, retained),
        (qh, hide, other.reshape(half), *state, w_first, out_weight),
        (shape((features, tok_rows), BF16), chunk, weight),
        fold_flops + chunk_flops,
        in_specs=[VMEM] * 7 + [HBM],
        scratch=[DMA((1,))],
    )
    send = lambda x, pairs: lax.ppermute(x, "tp", pairs)
    near = send(first, [(0, 1), (1, 0), (2, 3), (3, 2)])
    second, w_own = call(
        second_kernel,
        (att, w_second, out_weight),
        (chunk, weight),
        chunk_flops,
        in_specs=[VMEM, VMEM, HBM],
        scratch=[DMA((1,))],
    )
    middle = send(second, [(1, 2), (2, 1)])
    far = send(second, [(0, 2), (3, 1)])
    third, own = call(third_kernel, (att, w_third, w_own), (chunk, chunk), 2 * chunk_flops)
    end = send(third, [(0, 1), (3, 2)])
    relay = send(add(third, near), [(1, 3), (2, 0)])
    me = lax.axis_index("tp")
    at_end = (me == 0) | (me == tp - 1)
    return jnp.where(at_end, add(own, near, relay), add(own, middle, far, end))


def solution(mesh):
    placed = (
        P("ctx", "tp", None),
        P("ctx", "tp", None),
        P("ctx", "tp", None),
        P("ctx", "tp", None),
        P("ctx", "tp", None),
        P(),
        P(),
        P(None, "tp"),
    )
    return jax.shard_map(layer, mesh=mesh, in_specs=placed, out_specs=P("tp", "ctx"), check_vma=False)
```

profile of v0, /device:TPU:0, one launch (start us, length us, event | category | flops | bytes accessed | tf_op | source)
XLA Modules:
  0.0 46.8 jit_solution(12650150595343365134)
XLA Ops:
  0.0 1.0 %shard_map.83 = bf16[192,128]{1,0:T(8,128)(2,1)S(1)} custom-call(s32[8,32]{1,0:T(8,128)} %rows_hbm.1, bf16[128,128]{1,0:T(8,128)(2,1)} %bitcast.10, bf16[128,128]{1,0:T(8,128)(2,1)} %bitcast.12, bf16[64,128]{1,0:T(8,128)(2,1)} %bitcast.14, bf16[64,128]{1,0:T(8,128)(2,1)} %bitcast.15), custom_call_target="tpu_custom_call" | custom-call | flops 2097152 | bytes 99328 | tf_op jit(solution)/shard_map/pallas_call | solution.py:29
  1.0 3.1 %collective-permute-start = (bf16[192,128]{1,0:T(8,128)(2,1)S(1)}, bf16[192,128]{1,0:T(8,128)(2,1)S(1)}, u32[]{:S(2)}, u32[]{:S(2)}) collective-permute-start(bf16[192,128]{1,0:T(8,128)(2,1)S(1)} %shard_map.83), channel_id=1, source_target_pairs={{0,16},{4,20},{8,24},{12,28},{16,0},{20,4},{24,8},{28,12},{1,17},{... | collective-permute-start | bytes 147464 | tf_op jit(solution)/shard_map/ppermute | solution.py:266
  4.1 2.1 %collective-permute-done = bf16[192,128]{1,0:T(8,128)(2,1)S(1)} collective-permute-done((bf16[192,128]{1,0:T(8,128)(2,1)S(1)}, bf16[192,128]{1,0:T(8,128)(2,1)S(1)}, u32[]{:S(2)}, u32[]{:S(2)}) %collective-permute-start) | collective-permute-done | bytes 49184 | tf_op jit(solution)/shard_map/ppermute | solution.py:266
  6.2 2.1 %collective-permute-start.1 = (bf16[384,128]{1,0:T(8,128)(2,1)S(1)}, bf16[384,128]{1,0:T(8,128)(2,1)S(1)}, u32[]{:S(2)}, u32[]{:S(2)}) collective-permute-start(bf16[384,128]{1,0:T(8,128)(2,1)S(1)} %pad_maximum_fusion.1), channel_id=1, source_target_pairs={{0,8},{4,12},{8,0},{12,4},{16,24},{20,28},{24,16},{28,20},{1,9},{5... | collective-permute-start | bytes 294920 | tf_op jit(solution)/shard_map/ppermute | solution.py:266
  8.2 2.6 %collective-permute-done.1 = bf16[384,128]{1,0:T(8,128)(2,1)S(1)} collective-permute-done((bf16[384,128]{1,0:T(8,128)(2,1)S(1)}, bf16[384,128]{1,0:T(8,128)(2,1)S(1)}, u32[]{:S(2)}, u32[]{:S(2)}) %collective-permute-start.1) | collective-permute-done | bytes 98336 | tf_op jit(solution)/shard_map/ppermute | solution.py:266
  10.9 0.1 collective-permute-start.2
  10.9 1.8 %shard_map.82 = (bf16[1024,128]{1,0:T(8,128)(2,1)S(1)}, f32[8,128]{1,0:T(8,128)S(1)}, bf16[1024,1024]{1,0:T(8,128)(2,1)S(1)}, f32[1,1024]{1,0:T(1,128)S(1)}, f32...) custom-call(s32[8]{0:T(128)} %blocks_hbm.1, bf16[1024,128]{1,0:T(8,128)(2,1)} %bitcast.9, bf16[128,128]{1,0:T(8,128)(2,1)} %bitcast.11, ...), custom_call_target="tpu_custom_call" | custom-call | flops 67108864 | bytes 8716320 | tf_op jit(solution)/shard_map/pallas_call | solution.py:29
  12.7 2.9 %shard_map.84 = (bf16[1024,1024]{1,0:T(8,128)(2,1)S(1)}, f32[1,1024]{1,0:T(1,128)S(1)}, f32[1,1024]{1,0:T(1,128)S(1)}, f32[128,1024]{1,0:T(8,128)S(1)}) custom-call(bf16[1024,128]{1,0:T(8,128)(2,1)S(1)} %get-tuple-element.22.qh_ref, f32[8,128]{1,0:T(8,128)S(1)} %get-tuple-element.23.hide_ref, bf16[4,192,128]{2,1,0:T(8,128)(2,1)S(1)} %bitcast.7, ...), custom_call_target="tpu_custom_call" | custom-call | flops 201326592 | bytes 9383936 | tf_op jit(solution)/shard_map/pallas_call | solution.py:29
  15.6 0.0 collective-permute-done.2
  15.6 3.5 %shard_map.85 = (bf16[1024,128]{1,0:T(8,128)(2,1)S(1)}, bf16[1024,128]{1,0:T(8,128)(2,1)S(1)}, bf16[1024,1024]{1,0:T(8,128)(2,1)S(1)}) custom-call(bf16[1024,128]{1,0:T(8,128)(2,1)S(1)} %get-tuple-element.22.qh_ref, f32[8,128]{1,0:T(8,128)S(1)} %get-tuple-element.23.hide_ref, bf16[4,192,128]{2,1,0:T(8,128)(2,1)S(1)} %bitcast.8, ...), custom_call_target="tpu_custom_call" | custom-call | flops 469762048 | bytes 11481088 | tf_op jit(solution)/shard_map/pallas_call | solution.py:29
  19.1 2.1 %collective-permute-start.3 = (bf16[1024,128]{1,0:T(8,128)(2,1)S(1)}, bf16[1024,128]{1,0:T(8,128)(2,1)S(1)}, u32[]{:S(2)}, u32[]{:S(2)}) collective-permute-start(bf16[1024,128]{1,0:T(8,128)(2,1)S(1)} %get-tuple-element.36), channel_id=1, source_target_pairs={{0,1},{1,0},{2,3},{3,2},{4,5},{5,4},{6,7},{7,6},{8,9},{9,8},{10,11... | collective-permute-start | bytes 786440 | tf_op jit(solution)/shard_map/ppermute | solution.py:290
  21.3 2.2 %shard_map.86 = (bf16[1024,128]{1,0:T(8,128)(2,1)S(1)}, bf16[1024,1024]{1,0:T(8,128)(2,1)S(1)}) custom-call(bf16[1024,128]{1,0:T(8,128)(2,1)S(1)} %get-tuple-element.31.att_ref, bf16[1024,1024]{1,0:T(8,128)(2,1)S(1)} %get-tuple-element.33.w_ref, bf16[4096,1024]{1,0:T(8,128)(2,1)} %w_hbm.7), custom_call_target="tpu_custom_call" | custom-call | flops 268435456 | bytes 10747904 | tf_op jit(solution)/shard_map/pallas_call | solution.py:29
  23.5 0.7 %collective-permute-start.5 = (bf16[1024,128]{1,0:T(8,128)(2,1)S(1)}, bf16[1024,128]{1,0:T(8,128)(2,1)S(1)}, u32[]{:S(2)}, u32[]{:S(2)}) collective-permute-start(bf16[1024,128]{1,0:T(8,128)(2,1)S(1)} %get-tuple-element.38), channel_id=1, source_target_pairs={{1,2},{2,1},{5,6},{6,5},{9,10},{10,9},{13,14},{14,13},{17,18},{18,... | collective-permute-start | bytes 786440 | tf_op jit(solution)/shard_map/ppermute | solution.py:290
  24.2 5.7 %collective-permute-start.6 = (bf16[1024,128]{1,0:T(8,128)(2,1)S(1)}, bf16[1024,128]{1,0:T(8,128)(2,1)S(1)}, u32[]{:S(2)}, u32[]{:S(2)}) collective-permute-start(bf16[1024,128]{1,0:T(8,128)(2,1)S(1)} %get-tuple-element.38), channel_id=1, source_target_pairs={{0,2},{3,1},{4,6},{7,5},{8,10},{11,9},{12,14},{15,13},{16,18},{19,... | collective-permute-start | bytes 786440 | tf_op jit(solution)/shard_map/ppermute | solution.py:290
  29.9 1.3 %shard_map.87 = (bf16[1024,128]{1,0:T(8,128)(2,1)S(1)}, bf16[1024,128]{1,0:T(8,128)(2,1)S(1)}) custom-call(bf16[1024,128]{1,0:T(8,128)(2,1)S(1)} %get-tuple-element.31.att_ref, bf16[1024,1024]{1,0:T(8,128)(2,1)S(1)} %get-tuple-element.32.w_ref, bf16[1024,1024]{1,0:T(8,128)(2,1)S(1)} %get-tuple-element.34.last_ref), custom_call_target="tpu_custom_call" | custom-call | flops 536870912 | bytes 4456448 | tf_op jit(solution)/shard_map/pallas_call | solution.py:29
  31.2 1.8 %collective-permute-start.7 = (bf16[1024,128]{1,0:T(8,128)(2,1)S(1)}, bf16[1024,128]{1,0:T(8,128)(2,1)S(1)}, u32[]{:S(2)}, u32[]{:S(2)}) collective-permute-start(bf16[1024,128]{1,0:T(8,128)(2,1)S(1)} %get-tuple-element.37), channel_id=1, source_target_pairs={{0,1},{3,2},{4,5},{7,6},{8,9},{11,10},{12,13},{15,14},{16,17},{19,... | collective-permute-start | bytes 786440 | tf_op jit(solution)/shard_map/ppermute | solution.py:290
  33.1 0.0 collective-permute-done.3
  33.1 0.1 fusion.5
  33.1 1.3 %collective-permute-start.4 = (bf16[1024,128]{1,0:T(8,128)(2,1)S(1)}, bf16[1024,128]{1,0:T(8,128)(2,1)S(1)}, u32[]{:S(2)}, u32[]{:S(2)}) collective-permute-start(bf16[1024,128]{1,0:T(8,128)(2,1)S(1)} %fusion.5), channel_id=1, source_target_pairs={{1,3},{2,0},{5,7},{6,4},{9,11},{10,8},{13,15},{14,12},{17,19},{18,... | collective-permute-start | bytes 786440 | tf_op jit(solution)/shard_map/ppermute | solution.py:290
  34.5 7.0 %collective-permute-done.7 = bf16[1024,128]{1,0:T(8,128)(2,1)S(1)} collective-permute-done((bf16[1024,128]{1,0:T(8,128)(2,1)S(1)}, bf16[1024,128]{1,0:T(8,128)(2,1)S(1)}, u32[]{:S(2)}, u32[]{:S(2)}) %collective-permute-start.7) | collective-permute-done | bytes 262176 | tf_op jit(solution)/shard_map/ppermute | solution.py:290
  41.5 0.0 collective-permute-done.5
  41.5 0.0 collective-permute-done.6
  41.5 4.4 %collective-permute-done.4 = bf16[1024,128]{1,0:T(8,128)(2,1)S(1)} collective-permute-done((bf16[1024,128]{1,0:T(8,128)(2,1)S(1)}, bf16[1024,128]{1,0:T(8,128)(2,1)S(1)}, u32[]{:S(2)}, u32[]{:S(2)}) %collective-permute-start.4) | collective-permute-done | bytes 262176 | tf_op jit(solution)/shard_map/ppermute | solution.py:290
  45.9 0.9 %fusion.6 = bf16[1024,128]{1,0:T(8,128)(2,1)} fusion(bf16[1024,128]{1,0:T(8,128)(2,1)S(1)} %collective-permute-done.4, bf16[1024,128]{1,0:T(8,128)(2,1)S(1)} %collective-permute-done.3, bf16[1024,128]{1,0:T(8,128)(2,1)S(1)} %get-tuple-element.35, bf16[1024,128]{1,0:T(8,128)(2,1)S(1)} %collective-permute-done.7, ...), kind=kLoop, calls=%fused_computation.9 | loop fusion | flops 1835008 | bytes 1835009 | tf_op jit(solution)/shard_map/jit(_where)/select_n | solution.py:307
  (2 shorter events, 0.0 us)
Async XLA Ops:
  1.0 5.1 %collective-permute-start = (bf16[192,128]{1,0:T(8,128)(2,1)S(1)}, bf16[192,128]{1,0:T(8,128)(2,1)S(1)}, u32[]{:S(2)}, u32[]{:S(2)}) collective-permute-start(bf16[192,128]{1,0:T(8,128)(2,1)S(1)} %shard_map.83), channel_id=1, source_target_pairs={{0,16},{4,20},{8,24},{12,28},{16,0},{20,4},{24,8},{28,12},{1,17},{... | collective-permute-start | bytes 147464 | tf_op jit(solution)/shard_map/ppermute | solution.py:266
  6.2 4.7 %collective-permute-start.1 = (bf16[384,128]{1,0:T(8,128)(2,1)S(1)}, bf16[384,128]{1,0:T(8,128)(2,1)S(1)}, u32[]{:S(2)}, u32[]{:S(2)}) collective-permute-start(bf16[384,128]{1,0:T(8,128)(2,1)S(1)} %pad_maximum_fusion.1), channel_id=1, source_target_pairs={{0,8},{4,12},{8,0},{12,4},{16,24},{20,28},{24,16},{28,20},{1,9},{5... | collective-permute-start | bytes 294920 | tf_op jit(solution)/shard_map/ppermute | solution.py:266
  10.9 4.7 %collective-permute-start.2 = (bf16[768,128]{1,0:T(8,128)(2,1)S(1)}, bf16[768,128]{1,0:T(8,128)(2,1)S(1)}, u32[]{:S(2)}, u32[]{:S(2)}) collective-permute-start(bf16[768,128]{1,0:T(8,128)(2,1)S(1)} %pad_maximum_fusion), channel_id=1, source_target_pairs={{0,4},{4,0},{8,12},{12,8},{16,20},{20,16},{24,28},{28,24},{1,5},{5... | collective-permute-start | bytes 589832 | tf_op jit(solution)/shard_map/ppermute | solution.py:270
  19.1 13.9 %collective-permute-start.3 = (bf16[1024,128]{1,0:T(8,128)(2,1)S(1)}, bf16[1024,128]{1,0:T(8,128)(2,1)S(1)}, u32[]{:S(2)}, u32[]{:S(2)}) collective-permute-start(bf16[1024,128]{1,0:T(8,128)(2,1)S(1)} %get-tuple-element.36), channel_id=1, source_target_pairs={{0,1},{1,0},{2,3},{3,2},{4,5},{5,4},{6,7},{7,6},{8,9},{9,8},{10,11... | collective-permute-start | bytes 786440 | tf_op jit(solution)/shard_map/ppermute | solution.py:290
  23.5 18.0 %collective-permute-start.5 = (bf16[1024,128]{1,0:T(8,128)(2,1)S(1)}, bf16[1024,128]{1,0:T(8,128)(2,1)S(1)}, u32[]{:S(2)}, u32[]{:S(2)}) collective-permute-start(bf16[1024,128]{1,0:T(8,128)(2,1)S(1)} %get-tuple-element.38), channel_id=1, source_target_pairs={{1,2},{2,1},{5,6},{6,5},{9,10},{10,9},{13,14},{14,13},{17,18},{18,... | collective-permute-start | bytes 786440 | tf_op jit(solution)/shard_map/ppermute | solution.py:290
  24.2 17.3 %collective-permute-start.6 = (bf16[1024,128]{1,0:T(8,128)(2,1)S(1)}, bf16[1024,128]{1,0:T(8,128)(2,1)S(1)}, u32[]{:S(2)}, u32[]{:S(2)}) collective-permute-start(bf16[1024,128]{1,0:T(8,128)(2,1)S(1)} %get-tuple-element.38), channel_id=1, source_target_pairs={{0,2},{3,1},{4,6},{7,5},{8,10},{11,9},{12,14},{15,13},{16,18},{19,... | collective-permute-start | bytes 786440 | tf_op jit(solution)/shard_map/ppermute | solution.py:290
  31.2 10.3 %collective-permute-start.7 = (bf16[1024,128]{1,0:T(8,128)(2,1)S(1)}, bf16[1024,128]{1,0:T(8,128)(2,1)S(1)}, u32[]{:S(2)}, u32[]{:S(2)}) collective-permute-start(bf16[1024,128]{1,0:T(8,128)(2,1)S(1)} %get-tuple-element.37), channel_id=1, source_target_pairs={{0,1},{3,2},{4,5},{7,6},{8,9},{11,10},{12,13},{15,14},{16,17},{19,... | collective-permute-start | bytes 786440 | tf_op jit(solution)/shard_map/ppermute | solution.py:290
  33.1 12.7 %collective-permute-start.4 = (bf16[1024,128]{1,0:T(8,128)(2,1)S(1)}, bf16[1024,128]{1,0:T(8,128)(2,1)S(1)}, u32[]{:S(2)}, u32[]{:S(2)}) collective-permute-start(bf16[1024,128]{1,0:T(8,128)(2,1)S(1)} %fusion.5), channel_id=1, source_target_pairs={{1,3},{2,0},{5,7},{6,4},{9,11},{10,8},{13,15},{14,12},{17,19},{18,... | collective-permute-start | bytes 786440 | tf_op jit(solution)/shard_map/ppermute | solution.py:290
where the time goes:
time: 47.2 us; the launch traced here: 46.8 us
  starting transfers between devices  16.9 us (36%)
  waiting for transfers between devices  16.1 us (34%)
  Pallas kernels  12.6 us (27%)
  other arithmetic  1.02 us (2%)
    pallas_call x6, Pallas kernels, call(): pl.pallas_call(kernel, out_shape=out_shape, in_specs=in_specs or [VMEM] *...  12.6 us
    ppermute x5, starting transfers between devices, layer(): send = lambda x, pairs: lax.ppermute(x, 'tp', pairs)  11.7 us
    ppermute x5, waiting for transfers between devices, layer(): send = lambda x, pairs: lax.ppermute(x, 'tp', pairs)  11.4 us
    ppermute x3, starting transfers between devices, layer(): other = lax.ppermute(held, 'ctx', [(i, i ^ step) for i in range(slots)])  5.19 us
    ppermute x3, waiting for transfers between devices, layer(): other = lax.ppermute(held, 'ctx', [(i, i ^ step) for i in range(slots)])  4.7 us
  transfers between devices with their start and end apart: 8, of which 4 were waited for; matrix products, arithmetic and copies ran while one was open for 0% of the time, Pallas kernels for 17%

commit v1 on v0

--- a/solution.py
+++ b/solution.py
@@ -16,6 +16,7 @@
 HBM = pl.BlockSpec(memory_space=pltpu.HBM)
 DMA = pltpu.SemaphoreType.DMA
 PAIR = 2
+PARTS = 4
 
 
 def dot(a, b, a_dim, b_dim):
@@ -87,17 +88,21 @@
     return size ** (-0.5) * math.log2(math.e)
 
 
-def chunk_of(w_hbm, at, rows):
+def parts_of(w_hbm, at, w_ref):
+    rows = w_ref.shape[0]
     chunk = order_of(lax.axis_index("tp"))[at]
-    return w_hbm.at[pl.ds(pl.multiple_of(chunk * rows, 16), rows), :]
+    part = rows // PARTS
+    return [
+        (w_hbm.at[pl.ds(pl.multiple_of(chunk * rows + i * part, 16), part), :], w_ref.at[i * part : (i + 1) * part, :])
+        for i in range(PARTS)
+    ]
 
 
 def own_kernel(blocks_hbm, q_hbm, wk_hbm, wv_hbm, w_hbm, qh_ref, hide_ref, w_ref, top_ref, total_ref, summed_ref,
                blocks_ref, q_ref, wk_ref, wv_ref, qf_ref, sems):
     pairs = [(blocks_hbm, blocks_ref), (q_hbm, q_ref), (wk_hbm, wk_ref), (wv_hbm, wv_ref)]
-    pairs.append((chunk_of(w_hbm, 0, w_ref.shape[0]), w_ref))
-    copies = fetch(pairs, sems)
-    wait(copies[:-1])
+    copies = fetch(pairs + parts_of(w_hbm, 0, w_ref), sems)
+    wait(copies[: len(pairs)])
     tok_rows, size = wk_ref.shape
     heads = q_ref.shape[0] // tok_rows
     slot = lax.axis_index("ctx")
@@ -120,7 +125,7 @@
         groups = [(wk_ref[...], lambda s: jnp.where(causal, s, HIDDEN))]
         state = fold(qh_ref[cols, :], None, groups, value_cols, factor_of(size))
         top_ref[:, cols], total_ref[:, cols], summed_ref[:, cols] = state
-    wait(copies[-1:])
+    wait(copies[len(pairs) :])
 
 
 def rows_of(block_ref, anchors, retained):
@@ -153,15 +158,16 @@
         finish(h, cols, fold(qh_ref[cols, :], before, groups, value_cols, factor_of(size)))
 
 
-def early_kernel(order, anchors, retained, qh_ref, hide_ref, block_ref, top0, total0, summed0, w_hbm,
-                 w_ref, top_ref, total_ref, summed_ref, sems):
-    copies = fetch([(chunk_of(w_hbm, 1, w_ref.shape[0]), w_ref)], sems)
-
+def early_kernel(order, anchors, retained, qh_ref, hide_ref, block_ref, top0, total0, summed0,
+                 top_ref, total_ref, summed_ref):
     def finish(h, cols, state):
         top_ref[:, cols], total_ref[:, cols], summed_ref[:, cols] = state
 
     fold_blocks(order, anchors, retained, qh_ref, hide_ref, block_ref, (top0, total0, summed0), finish)
-    wait(copies)
+
+
+def fetch_kernel(held_ref, w_hbm, second_ref, third_ref, sems):
+    wait(fetch(parts_of(w_hbm, 1, second_ref) + parts_of(w_hbm, 2, third_ref), sems))
 
 
 def project(w_ref, att_ref, out_ref):
@@ -179,9 +185,8 @@
     return far, second, third, me
 
 
-def late_kernel(order, anchors, retained, qh_ref, hide_ref, block_ref, top0, total0, summed0, w_ref, w_hbm,
-                att_ref, first_ref, next_ref, sems):
-    copies = fetch([(chunk_of(w_hbm, 2, next_ref.shape[0]), next_ref)], sems)
+def late_kernel(order, anchors, retained, qh_ref, hide_ref, block_ref, top0, total0, summed0, w_ref,
+                att_ref, first_ref):
     tok_rows = hide_ref.shape[1]
     size = qh_ref.shape[1]
 
@@ -193,17 +198,16 @@
 
     fold_blocks(order, anchors, retained, qh_ref, hide_ref, block_ref, (top0, total0, summed0), finish)
     project(w_ref, att_ref, first_ref)
-    wait(copies)
-
-
-def second_kernel(att_ref, w_ref, w_hbm, out_ref, next_ref, sems):
-    copies = fetch([(chunk_of(w_hbm, 3, next_ref.shape[0]), next_ref)], sems)
+
+
+def second_kernel(att_ref, w_ref, out_ref):
+    project(w_ref, att_ref, out_ref)
+
+
+def third_kernel(att_ref, w_ref, w_hbm, out_ref, own_ref, last_ref, sems):
+    copies = fetch(parts_of(w_hbm, 3, last_ref), sems)
     project(w_ref, att_ref, out_ref)
     wait(copies)
-
-
-def third_kernel(att_ref, w_ref, last_ref, out_ref, own_ref):
-    project(w_ref, att_ref, out_ref)
     project(last_ref, att_ref, own_ref)
 
 
@@ -256,7 +260,7 @@
             pltpu.VMEM((tok_rows, size), BF16),
             pltpu.VMEM((tok_rows, size), BF16),
             pltpu.VMEM((query_rows, size), F32),
-            DMA((5,)),
+            DMA((4 + PARTS,)),
         ],
     )
     order = [0]
@@ -267,39 +271,38 @@
         held = jnp.concatenate([held, other], axis=0)
         order = order + [j ^ step for j in order]
         step //= 2
+    w_second, w_third = call(
+        fetch_kernel, (hide, out_weight), (weight, weight), 0, in_specs=[VMEM, HBM], scratch=[DMA((2 * PARTS,))]
+    )
     other = lax.ppermute(held, "ctx", [(i, i ^ step) for i in range(slots)])
     late_order = [j ^ step for j in order]
     half = (slots // 2, packed, size)
     fold_flops = 4 * query_rows * (slots // 2) * (anchors + retained) * size
-    w_second, *state = call(
+    state = call(
         functools.partial(early_kernel, order, anchors, retained),
-        (qh, hide, held.reshape(half), *state, out_weight),
-        (weight, *stats),
+        (qh, hide, held.reshape(half), *state),
+        stats,
         fold_flops,
-        in_specs=[VMEM] * 6 + [HBM],
-        scratch=[DMA((1,))],
-    )
-    att, first, w_third = call(
+    )
+    att, first = call(
         functools.partial(late_kernel, late_order, anchors, retained),
-        (qh, hide, other.reshape(half), *state, w_first, out_weight),
-        (shape((features, tok_rows), BF16), chunk, weight),
+        (qh, hide, other.reshape(half), *state, w_first),
+        (shape((features, tok_rows), BF16), chunk),
         fold_flops + chunk_flops,
-        in_specs=[VMEM] * 7 + [HBM],
-        scratch=[DMA((1,))],
     )
     send = lambda x, pairs: lax.ppermute(x, "tp", pairs)
     near = send(first, [(0, 1), (1, 0), (2, 3), (3, 2)])
-    second, w_own = call(
-        second_kernel,
-        (att, w_second, out_weight),
-        (chunk, weight),
-        chunk_flops,
-        in_specs=[VMEM, VMEM, HBM],
-        scratch=[DMA((1,))],
-    )
+    second = call(second_kernel, (att, w_second), chunk, chunk_flops)
     middle = send(second, [(1, 2), (2, 1)])
     far = send(second, [(0, 2), (3, 1)])
-    third, own = call(third_kernel, (att, w_third, w_own), (chunk, chunk), 2 * chunk_flops)
+    third, own = call(
+        third_kernel,
+        (att, w_third, out_weight),
+        (chunk, chunk),
+        2 * chunk_flops,
+        in_specs=[VMEM, VMEM, HBM],
+        scratch=[pltpu.VMEM((chunk_rows, features), BF16), DMA((PARTS,))],
+    )
     end = send(third, [(0, 1), (3, 2)])
     relay = send(add(third, near), [(1, 3), (2, 0)])
     me = lax.axis_index("tp")

time: 47.2 us -> 44.9 us (0.951)
  waiting for transfers between devices: 16.1 us -> 14.5 us
  Pallas kernels: 12.6 us -> 12 us
    ppermute x5, waiting for transfers between devices: 11.4 us -> 9.84 us  [layer(): send = lambda x, pairs: lax.ppermute(x, 'tp', pairs)]
    pallas_call x6 -> x7, Pallas kernels: 12.6 us -> 12 us  [call(): pl.pallas_call(kernel, out_shape=out_shape, in_specs=in_specs or [VMEM] *...]
  transfers between devices with their start and end apart: 8 -> 8, of which waited for: 4 -> 5; matrix products, arithmetic and copies ran while one was open for 0% -> 0% of each run, Pallas kernels for 17% -> 20%
where the time goes in v1:
time: 44.9 us; the launch traced here: 44.6 us
  starting transfers between devices  16.9 us (38%)
  waiting for transfers between devices  14.5 us (32%)
  Pallas kernels  12 us (27%)
  other arithmetic  1.02 us (2%)
    pallas_call x7, Pallas kernels, call(): pl.pallas_call(kernel, out_shape=out_shape, in_specs=in_specs or [VMEM] *...  12 us
    ppermute x5, starting transfers between devices, layer(): send = lambda x, pairs: lax.ppermute(x, 'tp', pairs)  11.7 us
    ppermute x5, waiting for transfers between devices, layer(): send = lambda x, pairs: lax.ppermute(x, 'tp', pairs)  9.84 us
    ppermute x3, starting transfers between devices, layer(): other = lax.ppermute(held, 'ctx', [(i, i ^ step) for i in range(slots)])  5.19 us
    ppermute x3, waiting for transfers between devices, layer(): other = lax.ppermute(held, 'ctx', [(i, i ^ step) for i in range(slots)])  4.7 us
    select_n x1, other arithmetic, layer(): return jnp.where(at_end, add(own, near, relay), add(own, middle, far, end))  0.93 us
  transfers between devices with their start and end apart: 8, of which 5 were waited for; matrix products, arithmetic and copies ran while one was open for 0% of the time, Pallas kernels for 20%

profile of v1, /device:TPU:0, one launch (start us, length us, event | category | flops | bytes accessed | tf_op | source)
XLA Modules:
  0.0 44.6 jit_solution(16882508726590936499)
XLA Ops:
  0.0 1.0 %shard_map.83 = bf16[192,128]{1,0:T(8,128)(2,1)S(1)} custom-call(s32[8,32]{1,0:T(8,128)} %rows_hbm.1, bf16[128,128]{1,0:T(8,128)(2,1)} %bitcast.10, bf16[128,128]{1,0:T(8,128)(2,1)} %bitcast.12, bf16[64,128]{1,0:T(8,128)(2,1)} %bitcast.14, bf16[64,128]{1,0:T(8,128)(2,1)} %bitcast.15), custom_call_target="tpu_custom_call" | custom-call | flops 2097152 | bytes 99328 | tf_op jit(solution)/shard_map/pallas_call | solution.py:30
  1.0 3.1 %collective-permute-start = (bf16[192,128]{1,0:T(8,128)(2,1)S(1)}, bf16[192,128]{1,0:T(8,128)(2,1)S(1)}, u32[]{:S(2)}, u32[]{:S(2)}) collective-permute-start(bf16[192,128]{1,0:T(8,128)(2,1)S(1)} %shard_map.83), channel_id=1, source_target_pairs={{0,16},{4,20},{8,24},{12,28},{16,0},{20,4},{24,8},{28,12},{1,17},{... | collective-permute-start | bytes 147464 | tf_op jit(solution)/shard_map/ppermute | solution.py:270
  4.1 2.1 %collective-permute-done = bf16[192,128]{1,0:T(8,128)(2,1)S(1)} collective-permute-done((bf16[192,128]{1,0:T(8,128)(2,1)S(1)}, bf16[192,128]{1,0:T(8,128)(2,1)S(1)}, u32[]{:S(2)}, u32[]{:S(2)}) %collective-permute-start) | collective-permute-done | bytes 49184 | tf_op jit(solution)/shard_map/ppermute | solution.py:270
  6.2 2.1 %collective-permute-start.1 = (bf16[384,128]{1,0:T(8,128)(2,1)S(1)}, bf16[384,128]{1,0:T(8,128)(2,1)S(1)}, u32[]{:S(2)}, u32[]{:S(2)}) collective-permute-start(bf16[384,128]{1,0:T(8,128)(2,1)S(1)} %pad_maximum_fusion.1), channel_id=1, source_target_pairs={{0,8},{4,12},{8,0},{12,4},{16,24},{20,28},{24,16},{28,20},{1,9},{5... | collective-permute-start | bytes 294920 | tf_op jit(solution)/shard_map/ppermute | solution.py:270
  8.2 2.6 %collective-permute-done.1 = bf16[384,128]{1,0:T(8,128)(2,1)S(1)} collective-permute-done((bf16[384,128]{1,0:T(8,128)(2,1)S(1)}, bf16[384,128]{1,0:T(8,128)(2,1)S(1)}, u32[]{:S(2)}, u32[]{:S(2)}) %collective-permute-start.1) | collective-permute-done | bytes 98336 | tf_op jit(solution)/shard_map/ppermute | solution.py:270
  10.9 0.1 collective-permute-start.2
  10.9 1.8 %shard_map.82 = (bf16[1024,128]{1,0:T(8,128)(2,1)S(1)}, f32[8,128]{1,0:T(8,128)S(1)}, bf16[1024,1024]{1,0:T(8,128)(2,1)S(1)}, f32[1,1024]{1,0:T(1,128)S(1)}, f32...) custom-call(s32[8]{0:T(128)} %blocks_hbm.1, bf16[1024,128]{1,0:T(8,128)(2,1)} %bitcast.9, bf16[128,128]{1,0:T(8,128)(2,1)} %bitcast.11, ...), custom_call_target="tpu_custom_call" | custom-call | flops 67108864 | bytes 8716320 | tf_op jit(solution)/shard_map/pallas_call | solution.py:30
  12.7 1.4 %shard_map.84 = (f32[1,1024]{1,0:T(1,128)S(1)}, f32[1,1024]{1,0:T(1,128)S(1)}, f32[128,1024]{1,0:T(8,128)S(1)}) custom-call(bf16[1024,128]{1,0:T(8,128)(2,1)S(1)} %get-tuple-element.20.qh_ref, f32[8,128]{1,0:T(8,128)S(1)} %get-tuple-element.21.hide_ref.held_ref, bf16[4,192,128]{2,1,0:T(8,128)(2,1)S(1)} %bitcast.7, f32[1,1024]{1,0:T(1,128)S(1)} %get-tuple-element.22.top0, ...), custom_call_target="tpu_custom_call" | custom-call | flops 201326592 | bytes 995328 | tf_op jit(solution)/shard_map/pallas_call | solution.py:30
  14.1 0.0 collective-permute-done.2
  14.1 2.0 %shard_map.85 = (bf16[1024,128]{1,0:T(8,128)(2,1)S(1)}, bf16[1024,128]{1,0:T(8,128)(2,1)S(1)}) custom-call(bf16[1024,128]{1,0:T(8,128)(2,1)S(1)} %get-tuple-element.20.qh_ref, f32[8,128]{1,0:T(8,128)S(1)} %get-tuple-element.21.hide_ref.held_ref, bf16[4,192,128]{2,1,0:T(8,128)(2,1)S(1)} %bitcast.8, f32[1,1024]{1,0:T(1,128)S(1)} %get-tuple-element.25.top0, ...), custom_call_target="tpu_custom_call" | custom-call | flops 469762048 | bytes 3092480 | tf_op jit(solution)/shard_map/pallas_call | solution.py:30
  16.2 2.1 %collective-permute-start.3 = (bf16[1024,128]{1,0:T(8,128)(2,1)S(1)}, bf16[1024,128]{1,0:T(8,128)(2,1)S(1)}, u32[]{:S(2)}, u32[]{:S(2)}) collective-permute-start(bf16[1024,128]{1,0:T(8,128)(2,1)S(1)} %get-tuple-element.32), channel_id=1, source_target_pairs={{0,1},{1,0},{2,3},{3,2},{4,5},{5,4},{6,7},{7,6},{8,9},{9,8},{10,11... | collective-permute-start | bytes 786440 | tf_op jit(solution)/shard_map/ppermute | solution.py:293
  18.3 2.2 %shard_map.86 = (bf16[1024,1024]{1,0:T(8,128)(2,1)S(1)}, bf16[1024,1024]{1,0:T(8,128)(2,1)S(1)}) custom-call(f32[8,128]{1,0:T(8,128)S(1)} %get-tuple-element.21.hide_ref.held_ref, bf16[4096,1024]{1,0:T(8,128)(2,1)} %w_hbm.5), custom_call_target="tpu_custom_call" | custom-call | bytes 8392704 | tf_op jit(solution)/shard_map/pallas_call | solution.py:30
  20.5 0.7 %shard_map.88 = bf16[1024,128]{1,0:T(8,128)(2,1)S(1)} custom-call(bf16[1024,128]{1,0:T(8,128)(2,1)S(1)} %get-tuple-element.29.att_ref, bf16[1024,1024]{1,0:T(8,128)(2,1)S(1)} %get-tuple-element.34.w_ref), custom_call_target="tpu_custom_call" | custom-call | flops 268435456 | bytes 2359296 | tf_op jit(solution)/shard_map/pallas_call | solution.py:30
  21.2 0.7 %collective-permute-start.5 = (bf16[1024,128]{1,0:T(8,128)(2,1)S(1)}, bf16[1024,128]{1,0:T(8,128)(2,1)S(1)}, u32[]{:S(2)}, u32[]{:S(2)}) collective-permute-start(bf16[1024,128]{1,0:T(8,128)(2,1)S(1)} %shard_map.88), channel_id=1, source_target_pairs={{1,2},{2,1},{5,6},{6,5},{9,10},{10,9},{13,14},{14,13},{17,18},{18,... | collective-permute-start | bytes 786440 | tf_op jit(solution)/shard_map/ppermute | solution.py:293
  21.9 5.8 %collective-permute-start.6 = (bf16[1024,128]{1,0:T(8,128)(2,1)S(1)}, bf16[1024,128]{1,0:T(8,128)(2,1)S(1)}, u32[]{:S(2)}, u32[]{:S(2)}) collective-permute-start(bf16[1024,128]{1,0:T(8,128)(2,1)S(1)} %shard_map.88), channel_id=1, source_target_pairs={{0,2},{3,1},{4,6},{7,5},{8,10},{11,9},{12,14},{15,13},{16,18},{19,... | collective-permute-start | bytes 786440 | tf_op jit(solution)/shard_map/ppermute | solution.py:293
  27.7 2.9 %shard_map.87 = (bf16[1024,128]{1,0:T(8,128)(2,1)S(1)}, bf16[1024,128]{1,0:T(8,128)(2,1)S(1)}) custom-call(bf16[1024,128]{1,0:T(8,128)(2,1)S(1)} %get-tuple-element.29.att_ref, bf16[1024,1024]{1,0:T(8,128)(2,1)S(1)} %get-tuple-element.30.w_ref, bf16[4096,1024]{1,0:T(8,128)(2,1)} %w_hbm.5), custom_call_target="tpu_custom_call" | custom-call | flops 536870912 | bytes 10747904 | tf_op jit(solution)/shard_map/pallas_call | solution.py:30
  30.5 1.8 %collective-permute-start.7 = (bf16[1024,128]{1,0:T(8,128)(2,1)S(1)}, bf16[1024,128]{1,0:T(8,128)(2,1)S(1)}, u32[]{:S(2)}, u32[]{:S(2)}) collective-permute-start(bf16[1024,128]{1,0:T(8,128)(2,1)S(1)} %get-tuple-element.33), channel_id=1, source_target_pairs={{0,1},{3,2},{4,5},{7,6},{8,9},{11,10},{12,13},{15,14},{16,17},{19,... | collective-permute-start | bytes 786440 | tf_op jit(solution)/shard_map/ppermute | solution.py:293
  32.4 0.0 collective-permute-done.3
  32.4 0.1 fusion.5
  32.5 1.3 %collective-permute-start.4 = (bf16[1024,128]{1,0:T(8,128)(2,1)S(1)}, bf16[1024,128]{1,0:T(8,128)(2,1)S(1)}, u32[]{:S(2)}, u32[]{:S(2)}) collective-permute-start(bf16[1024,128]{1,0:T(8,128)(2,1)S(1)} %fusion.5), channel_id=1, source_target_pairs={{1,3},{2,0},{5,7},{6,4},{9,11},{10,8},{13,15},{14,12},{17,19},{18,... | collective-permute-start | bytes 786440 | tf_op jit(solution)/shard_map/ppermute | solution.py:293
  33.8 0.0 collective-permute-done.5
  33.8 0.6 %collective-permute-done.6 = bf16[1024,128]{1,0:T(8,128)(2,1)S(1)} collective-permute-done((bf16[1024,128]{1,0:T(8,128)(2,1)S(1)}, bf16[1024,128]{1,0:T(8,128)(2,1)S(1)}, u32[]{:S(2)}, u32[]{:S(2)}) %collective-permute-start.6) | collective-permute-done | bytes 262176 | tf_op jit(solution)/shard_map/ppermute | solution.py:293
  34.4 4.9 %collective-permute-done.7 = bf16[1024,128]{1,0:T(8,128)(2,1)S(1)} collective-permute-done((bf16[1024,128]{1,0:T(8,128)(2,1)S(1)}, bf16[1024,128]{1,0:T(8,128)(2,1)S(1)}, u32[]{:S(2)}, u32[]{:S(2)}) %collective-permute-start.7) | collective-permute-done | bytes 262176 | tf_op jit(solution)/shard_map/ppermute | solution.py:293
  39.3 4.4 %collective-permute-done.4 = bf16[1024,128]{1,0:T(8,128)(2,1)S(1)} collective-permute-done((bf16[1024,128]{1,0:T(8,128)(2,1)S(1)}, bf16[1024,128]{1,0:T(8,128)(2,1)S(1)}, u32[]{:S(2)}, u32[]{:S(2)}) %collective-permute-start.4) | collective-permute-done | bytes 262176 | tf_op jit(solution)/shard_map/ppermute | solution.py:293
  43.6 0.9 %fusion.6 = bf16[1024,128]{1,0:T(8,128)(2,1)} fusion(bf16[1024,128]{1,0:T(8,128)(2,1)S(1)} %collective-permute-done.4, bf16[1024,128]{1,0:T(8,128)(2,1)S(1)} %collective-permute-done.3, bf16[1024,128]{1,0:T(8,128)(2,1)S(1)} %get-tuple-element.31, bf16[1024,128]{1,0:T(8,128)(2,1)S(1)} %collective-permute-done.7, ...), kind=kLoop, calls=%fused_computation.9 | loop fusion | flops 1835008 | bytes 1835009 | tf_op jit(solution)/shard_map/jit(_where)/select_n | solution.py:310
  (2 shorter events, 0.0 us)
Async XLA Ops:
  1.0 5.1 %collective-permute-start = (bf16[192,128]{1,0:T(8,128)(2,1)S(1)}, bf16[192,128]{1,0:T(8,128)(2,1)S(1)}, u32[]{:S(2)}, u32[]{:S(2)}) collective-permute-start(bf16[192,128]{1,0:T(8,128)(2,1)S(1)} %shard_map.83), channel_id=1, source_target_pairs={{0,16},{4,20},{8,24},{12,28},{16,0},{20,4},{24,8},{28,12},{1,17},{... | collective-permute-start | bytes 147464 | tf_op jit(solution)/shard_map/ppermute | solution.py:270
  6.2 4.7 %collective-permute-start.1 = (bf16[384,128]{1,0:T(8,128)(2,1)S(1)}, bf16[384,128]{1,0:T(8,128)(2,1)S(1)}, u32[]{:S(2)}, u32[]{:S(2)}) collective-permute-start(bf16[384,128]{1,0:T(8,128)(2,1)S(1)} %pad_maximum_fusion.1), channel_id=1, source_target_pairs={{0,8},{4,12},{8,0},{12,4},{16,24},{20,28},{24,16},{28,20},{1,9},{5... | collective-permute-start | bytes 294920 | tf_op jit(solution)/shard_map/ppermute | solution.py:270
  10.9 3.2 %collective-permute-start.2 = (bf16[768,128]{1,0:T(8,128)(2,1)S(1)}, bf16[768,128]{1,0:T(8,128)(2,1)S(1)}, u32[]{:S(2)}, u32[]{:S(2)}) collective-permute-start(bf16[768,128]{1,0:T(8,128)(2,1)S(1)} %pad_maximum_fusion), channel_id=1, source_target_pairs={{0,4},{4,0},{8,12},{12,8},{16,20},{20,16},{24,28},{28,24},{1,5},{5... | collective-permute-start | bytes 589832 | tf_op jit(solution)/shard_map/ppermute | solution.py:277
  16.2 16.2 %collective-permute-start.3 = (bf16[1024,128]{1,0:T(8,128)(2,1)S(1)}, bf16[1024,128]{1,0:T(8,128)(2,1)S(1)}, u32[]{:S(2)}, u32[]{:S(2)}) collective-permute-start(bf16[1024,128]{1,0:T(8,128)(2,1)S(1)} %get-tuple-element.32), channel_id=1, source_target_pairs={{0,1},{1,0},{2,3},{3,2},{4,5},{5,4},{6,7},{7,6},{8,9},{9,8},{10,11... | collective-permute-start | bytes 786440 | tf_op jit(solution)/shard_map/ppermute | solution.py:293
  21.2 12.6 %collective-permute-start.5 = (bf16[1024,128]{1,0:T(8,128)(2,1)S(1)}, bf16[1024,128]{1,0:T(8,128)(2,1)S(1)}, u32[]{:S(2)}, u32[]{:S(2)}) collective-permute-start(bf16[1024,128]{1,0:T(8,128)(2,1)S(1)} %shard_map.88), channel_id=1, source_target_pairs={{1,2},{2,1},{5,6},{6,5},{9,10},{10,9},{13,14},{14,13},{17,18},{18,... | collective-permute-start | bytes 786440 | tf_op jit(solution)/shard_map/ppermute | solution.py:293
  21.9 12.5 %collective-permute-start.6 = (bf16[1024,128]{1,0:T(8,128)(2,1)S(1)}, bf16[1024,128]{1,0:T(8,128)(2,1)S(1)}, u32[]{:S(2)}, u32[]{:S(2)}) collective-permute-start(bf16[1024,128]{1,0:T(8,128)(2,1)S(1)} %shard_map.88), channel_id=1, source_target_pairs={{0,2},{3,1},{4,6},{7,5},{8,10},{11,9},{12,14},{15,13},{16,18},{19,... | collective-permute-start | bytes 786440 | tf_op jit(solution)/shard_map/ppermute | solution.py:293
  30.5 8.7 %collective-permute-start.7 = (bf16[1024,128]{1,0:T(8,128)(2,1)S(1)}, bf16[1024,128]{1,0:T(8,128)(2,1)S(1)}, u32[]{:S(2)}, u32[]{:S(2)}) collective-permute-start(bf16[1024,128]{1,0:T(8,128)(2,1)S(1)} %get-tuple-element.33), channel_id=1, source_target_pairs={{0,1},{3,2},{4,5},{7,6},{8,9},{11,10},{12,13},{15,14},{16,17},{19,... | collective-permute-start | bytes 786440 | tf_op jit(solution)/shard_map/ppermute | solution.py:293
  32.5 11.2 %collective-permute-start.4 = (bf16[1024,128]{1,0:T(8,128)(2,1)S(1)}, bf16[1024,128]{1,0:T(8,128)(2,1)S(1)}, u32[]{:S(2)}, u32[]{:S(2)}) collective-permute-start(bf16[1024,128]{1,0:T(8,128)(2,1)S(1)} %fusion.5), channel_id=1, source_target_pairs={{1,3},{2,0},{5,7},{6,4},{9,11},{10,8},{13,15},{14,12},{17,19},{18,... | collective-permute-start | bytes 786440 | tf_op jit(solution)/shard_map/ppermute | solution.py:293

commit v2 on v1

--- a/solution.py
+++ b/solution.py
@@ -17,6 +17,7 @@
 DMA = pltpu.SemaphoreType.DMA
 PAIR = 2
 PARTS = 4
+RELAY_PARTS, ALL_PARTS = 5, 8
 
 
 def dot(a, b, a_dim, b_dim):
@@ -88,20 +89,20 @@
     return size ** (-0.5) * math.log2(math.e)
 
 
-def parts_of(w_hbm, at, w_ref):
+def parts_of(w_hbm, mask, w_ref):
     rows = w_ref.shape[0]
-    chunk = order_of(lax.axis_index("tp"))[at]
+    begin = (lax.axis_index("tp") ^ mask) * rows
     part = rows // PARTS
     return [
-        (w_hbm.at[pl.ds(pl.multiple_of(chunk * rows + i * part, 16), part), :], w_ref.at[i * part : (i + 1) * part, :])
-        for i in range(PARTS)
+        (w_hbm.at[pl.ds(pl.multiple_of(begin + i, 16), part), :], w_ref.at[i : i + part, :])
+        for i in range(0, rows, part)
     ]
 
 
 def own_kernel(blocks_hbm, q_hbm, wk_hbm, wv_hbm, w_hbm, qh_ref, hide_ref, w_ref, top_ref, total_ref, summed_ref,
                blocks_ref, q_ref, wk_ref, wv_ref, qf_ref, sems):
     pairs = [(blocks_hbm, blocks_ref), (q_hbm, q_ref), (wk_hbm, wk_ref), (wv_hbm, wv_ref)]
-    copies = fetch(pairs + parts_of(w_hbm, 0, w_ref), sems)
+    copies = fetch(pairs + parts_of(w_hbm, 3, w_ref), sems)
     wait(copies[: len(pairs)])
     tok_rows, size = wk_ref.shape
     heads = q_ref.shape[0] // tok_rows
@@ -166,23 +167,16 @@
     fold_blocks(order, anchors, retained, qh_ref, hide_ref, block_ref, (top0, total0, summed0), finish)
 
 
-def fetch_kernel(held_ref, w_hbm, second_ref, third_ref, sems):
-    wait(fetch(parts_of(w_hbm, 1, second_ref) + parts_of(w_hbm, 2, third_ref), sems))
-
-
-def project(w_ref, att_ref, out_ref):
+def fetch_kernel(hide_ref, w_hbm, far_ref, near_ref, sems):
+    wait(fetch(parts_of(w_hbm, 2, far_ref) + parts_of(w_hbm, 1, near_ref), sems))
+
+
+def project(w_ref, first, att_ref, out_ref):
     rows = out_ref.shape[0]
-    tile = min(256, rows)
+    tile = math.gcd(256, rows)
     for start in range(0, rows, tile):
-        part = dot(w_ref[start : start + tile, :], att_ref[...], 1, 0)
+        part = dot(w_ref[first + start : first + start + tile, :], att_ref[...], 1, 0)
         out_ref[start : start + tile, :] = part.astype(out_ref.dtype)
-
-
-def order_of(me):
-    far = jnp.where(me % 2 == 0, 3, 0)
-    second = jnp.where((me == 0) | (me == 1), 2, 1)
-    third = jnp.where(me == 0, 1, jnp.where(me == 1, 3, jnp.where(me == 2, 0, 2)))
-    return far, second, third, me
 
 
 def late_kernel(order, anchors, retained, qh_ref, hide_ref, block_ref, top0, total0, summed0, w_ref,
@@ -197,18 +191,22 @@
             att_ref[(h + j) * size : (h + j + 1) * size, :] = attended[:, j * tok_rows : (j + 1) * tok_rows]
 
     fold_blocks(order, anchors, retained, qh_ref, hide_ref, block_ref, (top0, total0, summed0), finish)
-    project(w_ref, att_ref, first_ref)
-
-
-def second_kernel(att_ref, w_ref, out_ref):
-    project(w_ref, att_ref, out_ref)
-
-
-def third_kernel(att_ref, w_ref, w_hbm, out_ref, own_ref, last_ref, sems):
-    copies = fetch(parts_of(w_hbm, 3, last_ref), sems)
-    project(w_ref, att_ref, out_ref)
-    wait(copies)
-    project(last_ref, att_ref, own_ref)
+    project(w_ref, 0, att_ref, first_ref)
+
+
+def direct_kernel(att_ref, farther_w, far_w, farther_ref, far_ref):
+    for w_ref, out_ref in ((farther_w, farther_ref), (far_w, far_ref)):
+        project(w_ref, w_ref.shape[0] - out_ref.shape[0], att_ref, out_ref)
+
+
+def later_kernel(att_ref, far_w, near_w, across_ref, near_ref):
+    project(far_w, 0, att_ref, across_ref)
+    project(near_w, 0, att_ref, near_ref)
+
+
+def own_chunk_kernel(att_ref, w_hbm, out_ref, w_ref, sems):
+    wait(fetch(parts_of(w_hbm, 0, w_ref), sems))
+    project(w_ref, 0, att_ref, out_ref)
 
 
 def add(*parts):
@@ -228,6 +226,9 @@
     features = heads * size
     row = lambda n: shape((n, size), BF16)
     chunk, weight = shape((chunk_rows, tok_rows), BF16), shape((chunk_rows, features), BF16)
+    relay_rows = chunk_rows * RELAY_PARTS // ALL_PARTS
+    relayed = shape((relay_rows, tok_rows), BF16)
+    direct = shape((chunk_rows - relay_rows, tok_rows), BF16)
     chunk_flops = 2 * chunk_rows * tok_rows * features
     block = call(
         pack_kernel,
@@ -248,7 +249,7 @@
         shape((1, query_rows), F32),
         shape((size, query_rows), F32),
     )
-    qh, hide, w_first, *state = call(
+    qh, hide, w_farther, *state = call(
         own_kernel,
         (block_of_device, queries.reshape(query_rows, size), wk, wv, out_weight),
         (row(query_rows), shape((slots, tok_rows), F32), weight, *stats),
@@ -266,15 +267,22 @@
     order = [0]
     step = slots // 2
     held = block
-    while step > 1:
-        other = lax.ppermute(held, "ctx", [(i, i ^ step) for i in range(slots)])
-        held = jnp.concatenate([held, other], axis=0)
+
+    def exchange(mask):
+        return lax.ppermute(held, "ctx", [(i, i ^ mask) for i in range(slots)])
+
+    while step > 4:
+        held = jnp.concatenate([held, exchange(step)], axis=0)
         order = order + [j ^ step for j in order]
         step //= 2
-    w_second, w_third = call(
+    masks = (6, 4, 2)
+    held = jnp.concatenate([held] + [exchange(mask) for mask in masks], axis=0)
+    order = [j ^ mask for mask in (0, *masks) for j in order]
+    w_far, w_near = call(
         fetch_kernel, (hide, out_weight), (weight, weight), 0, in_specs=[VMEM, HBM], scratch=[DMA((2 * PARTS,))]
     )
-    other = lax.ppermute(held, "ctx", [(i, i ^ step) for i in range(slots)])
+    step = 1
+    other = exchange(step)
     late_order = [j ^ step for j in order]
     half = (slots // 2, packed, size)
     fold_flops = 4 * query_rows * (slots // 2) * (anchors + retained) * size
@@ -286,28 +294,32 @@
     )
     att, first = call(
         functools.partial(late_kernel, late_order, anchors, retained),
-        (qh, hide, other.reshape(half), *state, w_first),
-        (shape((features, tok_rows), BF16), chunk),
-        fold_flops + chunk_flops,
-    )
-    send = lambda x, pairs: lax.ppermute(x, "tp", pairs)
-    near = send(first, [(0, 1), (1, 0), (2, 3), (3, 2)])
-    second = call(second_kernel, (att, w_second), chunk, chunk_flops)
-    middle = send(second, [(1, 2), (2, 1)])
-    far = send(second, [(0, 2), (3, 1)])
-    third, own = call(
-        third_kernel,
-        (att, w_third, out_weight),
-        (chunk, chunk),
-        2 * chunk_flops,
-        in_specs=[VMEM, VMEM, HBM],
+        (qh, hide, other.reshape(half), *state, w_farther),
+        (shape((features, tok_rows), BF16), relayed),
+        fold_flops + chunk_flops // 2,
+    )
+
+    def send(x, mask):
+        return lax.ppermute(x, "tp", [(i, i ^ mask) for i in range(tp)])
+
+    relay = send(first, 1)
+    farther, far = call(direct_kernel, (att, w_farther, w_far), (direct, direct), chunk_flops)
+    farther = send(farther, 3)
+    far = send(far, 2)
+    across, near = call(later_kernel, (att, w_far, w_near), (relayed, chunk), chunk_flops)
+    across = send(add(across, relay), 2)
+    near = send(near, 1)
+    own = call(
+        own_chunk_kernel,
+        (att, out_weight),
+        chunk,
+        chunk_flops,
+        in_specs=[VMEM, HBM],
         scratch=[pltpu.VMEM((chunk_rows, features), BF16), DMA((PARTS,))],
     )
-    end = send(third, [(0, 1), (3, 2)])
-    relay = send(add(third, near), [(1, 3), (2, 0)])
-    me = lax.axis_index("tp")
-    at_end = (me == 0) | (me == tp - 1)
-    return jnp.where(at_end, add(own, near, relay), add(own, middle, far, end))
+    top = add(own[:relay_rows], near[:relay_rows], across)
+    low = add(own[relay_rows:], near[relay_rows:], far, farther)
+    return jnp.concatenate([top, low], axis=0)
 
 
 def solution(mesh):

time: 44.9 us -> 43.2 us (0.962)
  starting transfers between devices: 16.9 us -> 13.5 us
  waiting for transfers between devices: 14.5 us -> 16.4 us
    ppermute x8 -> x9, starting transfers between devices: 16.9 us -> 13.5 us  [the longest x5 8.82 us: send(): return lax.ppermute(x, 'tp', [(i, i ^ mask) for i in range(tp)])]
    ppermute x8 -> x9, waiting for transfers between devices: 14.5 us -> 16.4 us  [the longest x5 11.4 us: send(): return lax.ppermute(x, 'tp', [(i, i ^ mask) for i in range(tp)])]
    select_n x1 -> x0, other arithmetic: 0.93 us -> none  [layer(): return jnp.where(at_end, add(own, near, relay), add(own, middle, far, end))]
    concatenate x2, other arithmetic: 0.02 us -> 0.73 us  [the longest x1 0.72 us: layer(): return jnp.concatenate([top, low], axis=0)]
    pallas_call x7 -> x8, Pallas kernels: 12 us -> 12.1 us  [call(): pl.pallas_call(kernel, out_shape=out_shape, in_specs=in_specs or [VMEM] *...]
  transfers between devices with their start and end apart: 8 -> 9, of which waited for: 5 -> 5; matrix products, arithmetic and copies ran while one was open for 0% -> 0% of each run, Pallas kernels for 20% -> 21%
where the time goes in v2:
time: 43.2 us; the launch traced here: 42.9 us
  waiting for transfers between devices  16.4 us (38%)
  starting transfers between devices  13.5 us (31%)
  Pallas kernels  12.1 us (28%)
  other arithmetic  0.91 us (2%)
    pallas_call x8, Pallas kernels, call(): pl.pallas_call(kernel, out_shape=out_shape, in_specs=in_specs or [VMEM] *...  12.1 us
    ppermute x5, waiting for transfers between devices, send(): return lax.ppermute(x, 'tp', [(i, i ^ mask) for i in range(tp)])  11.4 us
    ppermute x5, starting transfers between devices, send(): return lax.ppermute(x, 'tp', [(i, i ^ mask) for i in range(tp)])  8.82 us
    ppermute x4, waiting for transfers between devices, exchange(): return lax.ppermute(held, 'ctx', [(i, i ^ mask) for i in range(slots)])  4.97 us
    ppermute x4, starting transfers between devices, exchange(): return lax.ppermute(held, 'ctx', [(i, i ^ mask) for i in range(slots)])  4.64 us
  transfers between devices with their start and end apart: 9, of which 5 were waited for; matrix products, arithmetic and copies ran while one was open for 0% of the time, Pallas kernels for 21%

profile of v2, /device:TPU:0, one launch (start us, length us, event | category | flops | bytes accessed | tf_op | source)
XLA Modules:
  0.0 42.9 jit_solution(8664602423430069308)
XLA Ops:
  0.0 1.0 %shard_map.83 = bf16[192,128]{1,0:T(8,128)(2,1)S(1)} custom-call(s32[8,32]{1,0:T(8,128)} %rows_hbm.1, bf16[128,128]{1,0:T(8,128)(2,1)} %bitcast.10, bf16[128,128]{1,0:T(8,128)(2,1)} %bitcast.12, bf16[64,128]{1,0:T(8,128)(2,1)} %bitcast.14, bf16[64,128]{1,0:T(8,128)(2,1)} %bitcast.15), custom_call_target="tpu_custom_call" | custom-call | flops 2097152 | bytes 99328 | tf_op jit(solution)/shard_map/pallas_call | solution.py:31
  1.0 3.0 %collective-permute-start.2 = (bf16[192,128]{1,0:T(8,128)(2,1)S(1)}, bf16[192,128]{1,0:T(8,128)(2,1)S(1)}, u32[]{:S(2)}, u32[]{:S(2)}) collective-permute-start(bf16[192,128]{1,0:T(8,128)(2,1)S(1)} %shard_map.83), channel_id=1, source_target_pairs={{0,8},{4,12},{8,0},{12,4},{16,24},{20,28},{24,16},{28,20},{1,9},{5... | collective-permute-start | bytes 147464 | tf_op jit(solution)/shard_map/ppermute | solution.py:272
  4.1 1.5 %collective-permute-start.1 = (bf16[192,128]{1,0:T(8,128)(2,1)S(1)}, bf16[192,128]{1,0:T(8,128)(2,1)S(1)}, u32[]{:S(2)}, u32[]{:S(2)}) collective-permute-start(bf16[192,128]{1,0:T(8,128)(2,1)S(1)} %shard_map.83), channel_id=1, source_target_pairs={{0,16},{4,20},{8,24},{12,28},{16,0},{20,4},{24,8},{28,12},{1,17},{... | collective-permute-start | bytes 147464 | tf_op jit(solution)/shard_map/ppermute | solution.py:272
  5.6 0.0 collective-permute-start
  5.6 0.5 %collective-permute-done.2 = bf16[192,128]{1,0:T(8,128)(2,1)S(1)} collective-permute-done((bf16[192,128]{1,0:T(8,128)(2,1)S(1)}, bf16[192,128]{1,0:T(8,128)(2,1)S(1)}, u32[]{:S(2)}, u32[]{:S(2)}) %collective-permute-start.2) | collective-permute-done | bytes 49184 | tf_op jit(solution)/shard_map/ppermute | solution.py:272
  6.1 2.0 %collective-permute-done.1 = bf16[192,128]{1,0:T(8,128)(2,1)S(1)} collective-permute-done((bf16[192,128]{1,0:T(8,128)(2,1)S(1)}, bf16[192,128]{1,0:T(8,128)(2,1)S(1)}, u32[]{:S(2)}, u32[]{:S(2)}) %collective-permute-start.1) | collective-permute-done | bytes 49184 | tf_op jit(solution)/shard_map/ppermute | solution.py:272
  8.2 2.4 %collective-permute-done = bf16[192,128]{1,0:T(8,128)(2,1)S(1)} collective-permute-done((bf16[192,128]{1,0:T(8,128)(2,1)S(1)}, bf16[192,128]{1,0:T(8,128)(2,1)S(1)}, u32[]{:S(2)}, u32[]{:S(2)}) %collective-permute-start) | collective-permute-done | bytes 49184 | tf_op jit(solution)/shard_map/ppermute | solution.py:272
  10.6 0.1 collective-permute-start.3
  10.7 1.8 %shard_map.82 = (bf16[1024,128]{1,0:T(8,128)(2,1)S(1)}, f32[8,128]{1,0:T(8,128)S(1)}, bf16[1024,1024]{1,0:T(8,128)(2,1)S(1)}, f32[1,1024]{1,0:T(1,128)S(1)}, f32...) custom-call(s32[8]{0:T(128)} %blocks_hbm.1, bf16[1024,128]{1,0:T(8,128)(2,1)} %bitcast.9, bf16[128,128]{1,0:T(8,128)(2,1)} %bitcast.11, ...), custom_call_target="tpu_custom_call" | custom-call | flops 67108864 | bytes 8716320 | tf_op jit(solution)/shard_map/pallas_call | solution.py:31
  12.4 1.4 %shard_map.84 = (f32[1,1024]{1,0:T(1,128)S(1)}, f32[1,1024]{1,0:T(1,128)S(1)}, f32[128,1024]{1,0:T(8,128)S(1)}) custom-call(bf16[1024,128]{1,0:T(8,128)(2,1)S(1)} %get-tuple-element.22.qh_ref, f32[8,128]{1,0:T(8,128)S(1)} %get-tuple-element.23.hide_ref, bf16[4,192,128]{2,1,0:T(8,128)(2,1)S(1)} %bitcast.7, f32[1,1024]{1,0:T(1,128)S(1)} %get-tuple-element.24.top0, ...), custom_call_target="tpu_custom_call" | custom-call | flops 201326592 | bytes 995328 | tf_op jit(solution)/shard_map/pallas_call | solution.py:31
  13.8 0.0 collective-permute-done.3
  13.8 1.9 %shard_map.85 = (bf16[1024,128]{1,0:T(8,128)(2,1)S(1)}, bf16[640,128]{1,0:T(8,128)(2,1)S(1)}) custom-call(bf16[1024,128]{1,0:T(8,128)(2,1)S(1)} %get-tuple-element.22.qh_ref, f32[8,128]{1,0:T(8,128)S(1)} %get-tuple-element.23.hide_ref, bf16[4,192,128]{2,1,0:T(8,128)(2,1)S(1)} %bitcast.8, f32[1,1024]{1,0:T(1,128)S(1)} %get-tuple-element.27.top0, ...), custom_call_target="tpu_custom_call" | custom-call | flops 335544320 | bytes 3092480 | tf_op jit(solution)/shard_map/pallas_call | solution.py:31
  15.7 1.6 %collective-permute-start.5 = (bf16[640,128]{1,0:T(8,128)(2,1)S(1)}, bf16[640,128]{1,0:T(8,128)(2,1)S(1)}, u32[]{:S(2)}, u32[]{:S(2)}) collective-permute-start(bf16[640,128]{1,0:T(8,128)(2,1)S(1)} %get-tuple-element.36), channel_id=1, source_target_pairs={{0,1},{1,0},{2,3},{3,2},{4,5},{5,4},{6,7},{7,6},{8,9},{9,8},{10,11... | collective-permute-start | bytes 491528 | tf_op jit(solution)/shard_map/ppermute | solution.py:303
  17.4 2.2 %shard_map.87 = (bf16[1024,1024]{1,0:T(8,128)(2,1)S(1)}, bf16[1024,1024]{1,0:T(8,128)(2,1)S(1)}) custom-call(f32[8,128]{1,0:T(8,128)S(1)} %get-tuple-element.23.hide_ref, bf16[4096,1024]{1,0:T(8,128)(2,1)} %w_hbm.5), custom_call_target="tpu_custom_call" | custom-call | bytes 8392704 | tf_op jit(solution)/shard_map/pallas_call | solution.py:31
  19.6 1.0 %shard_map.88 = (bf16[640,128]{1,0:T(8,128)(2,1)S(1)}, bf16[1024,128]{1,0:T(8,128)(2,1)S(1)}) custom-call(bf16[1024,128]{1,0:T(8,128)(2,1)S(1)} %get-tuple-element.31.att_ref, bf16[1024,1024]{1,0:T(8,128)(2,1)S(1)} %get-tuple-element.32.far_w, bf16[1024,1024]{1,0:T(8,128)(2,1)S(1)} %get-tuple-element.33.near_w), custom_call_target="tpu_custom_call" | custom-call | flops 268435456 | bytes 4456448 | tf_op jit(solution)/shard_map/pallas_call | solution.py:31
  20.6 0.5 %collective-permute-start.4 = (bf16[1024,128]{1,0:T(8,128)(2,1)S(1)}, bf16[1024,128]{1,0:T(8,128)(2,1)S(1)}, u32[]{:S(2)}, u32[]{:S(2)}) collective-permute-start(bf16[1024,128]{1,0:T(8,128)(2,1)S(1)} %get-tuple-element.34), channel_id=1, source_target_pairs={{0,1},{1,0},{2,3},{3,2},{4,5},{5,4},{6,7},{7,6},{8,9},{9,8},{10,11... | collective-permute-start | bytes 786440 | tf_op jit(solution)/shard_map/ppermute | solution.py:303
  21.1 0.6 %shard_map.89 = (bf16[384,128]{1,0:T(8,128)(2,1)S(1)}, bf16[384,128]{1,0:T(8,128)(2,1)S(1)}) custom-call(bf16[1024,128]{1,0:T(8,128)(2,1)S(1)} %get-tuple-element.31.att_ref, bf16[1024,1024]{1,0:T(8,128)(2,1)S(1)} %get-tuple-element.30.w_ref.farther_w, bf16[1024,1024]{1,0:T(8,128)(2,1)S(1)} %get-tuple-element.32.far_w), custom_call_target="tpu_custom_call" | custom-call | flops 268435456 | bytes 4456448 | tf_op jit(solution)/shard_map/pallas_call | solution.py:31
  21.7 3.7 %collective-permute-start.8 = (bf16[384,128]{1,0:T(8,128)(2,1)S(1)}, bf16[384,128]{1,0:T(8,128)(2,1)S(1)}, u32[]{:S(2)}, u32[]{:S(2)}) collective-permute-start(bf16[384,128]{1,0:T(8,128)(2,1)S(1)} %get-tuple-element.38), channel_id=1, source_target_pairs={{0,3},{1,2},{2,1},{3,0},{4,7},{5,6},{6,5},{7,4},{8,11},{9,10},{10,... | collective-permute-start | bytes 294920 | tf_op jit(solution)/shard_map/ppermute | solution.py:303
  25.4 0.0 collective-permute-start.7
  25.4 2.2 %shard_map.86 = bf16[1024,128]{1,0:T(8,128)(2,1)S(1)} custom-call(bf16[1024,128]{1,0:T(8,128)(2,1)S(1)} %get-tuple-element.31.att_ref, bf16[4096,1024]{1,0:T(8,128)(2,1)} %w_hbm.5), custom_call_target="tpu_custom_call" | custom-call | flops 268435456 | bytes 8650752 | tf_op jit(solution)/shard_map/pallas_call | solution.py:31
  27.6 0.0 collective-permute-done.5
  27.7 3.0 %collective-permute-start.6 = (bf16[640,128]{1,0:T(8,128)(2,1)S(1)}, bf16[640,128]{1,0:T(8,128)(2,1)S(1)}, u32[]{:S(2)}, u32[]{:S(2)}) collective-permute-start(bf16[640,128]{1,0:T(8,128)(2,1)S(1)} %add_convert_fusion.1), channel_id=1, source_target_pairs={{0,2},{1,3},{2,0},{3,1},{4,6},{5,7},{6,4},{7,5},{8,10},{9,11},{10,... | collective-permute-start | bytes 491528 | tf_op jit(solution)/shard_map/ppermute | solution.py:303
  30.7 3.4 %collective-permute-done.8 = bf16[384,128]{1,0:T(8,128)(2,1)S(1)} collective-permute-done((bf16[384,128]{1,0:T(8,128)(2,1)S(1)}, bf16[384,128]{1,0:T(8,128)(2,1)S(1)}, u32[]{:S(2)}, u32[]{:S(2)}) %collective-permute-start.8) | collective-permute-done | bytes 98336 | tf_op jit(solution)/shard_map/ppermute | solution.py:303
  34.1 0.0 collective-permute-done.7
  34.1 0.0 collective-permute-done.4
  34.1 0.1 add_convert_fusion.2
  34.2 8.0 %collective-permute-done.6 = bf16[640,128]{1,0:T(8,128)(2,1)S(1)} collective-permute-done((bf16[640,128]{1,0:T(8,128)(2,1)S(1)}, bf16[640,128]{1,0:T(8,128)(2,1)S(1)}, u32[]{:S(2)}, u32[]{:S(2)}) %collective-permute-start.6) | collective-permute-done | bytes 163872 | tf_op jit(solution)/shard_map/ppermute | solution.py:303
  42.1 0.1 add_convert_fusion
  42.2 0.7 %pad_maximum_fusion = bf16[1024,128]{1,0:T(8,128)(2,1)} fusion(bf16[384,128]{1,0:T(8,128)(2,1)S(1)} %add_convert_fusion.2, bf16[640,128]{1,0:T(8,128)(2,1)S(1)} %add_convert_fusion), kind=kLoop, calls=%fused_computation.2 | loop fusion | flops 524288 | bytes 524288 | tf_op jit(solution)/shard_map/concatenate | solution.py:322
  (2 shorter events, 0.1 us)
Async XLA Ops:
  1.0 5.1 %collective-permute-start.2 = (bf16[192,128]{1,0:T(8,128)(2,1)S(1)}, bf16[192,128]{1,0:T(8,128)(2,1)S(1)}, u32[]{:S(2)}, u32[]{:S(2)}) collective-permute-start(bf16[192,128]{1,0:T(8,128)(2,1)S(1)} %shard_map.83), channel_id=1, source_target_pairs={{0,8},{4,12},{8,0},{12,4},{16,24},{20,28},{24,16},{28,20},{1,9},{5... | collective-permute-start | bytes 147464 | tf_op jit(solution)/shard_map/ppermute | solution.py:272
  4.1 4.1 %collective-permute-start.1 = (bf16[192,128]{1,0:T(8,128)(2,1)S(1)}, bf16[192,128]{1,0:T(8,128)(2,1)S(1)}, u32[]{:S(2)}, u32[]{:S(2)}) collective-permute-start(bf16[192,128]{1,0:T(8,128)(2,1)S(1)} %shard_map.83), channel_id=1, source_target_pairs={{0,16},{4,20},{8,24},{12,28},{16,0},{20,4},{24,8},{28,12},{1,17},{... | collective-permute-start | bytes 147464 | tf_op jit(solution)/shard_map/ppermute | solution.py:272
  5.6 5.0 %collective-permute-start = (bf16[192,128]{1,0:T(8,128)(2,1)S(1)}, bf16[192,128]{1,0:T(8,128)(2,1)S(1)}, u32[]{:S(2)}, u32[]{:S(2)}) collective-permute-start(bf16[192,128]{1,0:T(8,128)(2,1)S(1)} %shard_map.83), channel_id=1, source_target_pairs={{0,24},{4,28},{8,16},{12,20},{16,8},{20,12},{24,0},{28,4},{1,25},{... | collective-permute-start | bytes 147464 | tf_op jit(solution)/shard_map/ppermute | solution.py:272
  10.6 3.2 %collective-permute-start.3 = (bf16[768,128]{1,0:T(8,128)(2,1)S(1)}, bf16[768,128]{1,0:T(8,128)(2,1)S(1)}, u32[]{:S(2)}, u32[]{:S(2)}) collective-permute-start(bf16[768,128]{1,0:T(8,128)(2,1)S(1)} %pad_maximum_fusion.1), channel_id=1, source_target_pairs={{0,4},{4,0},{8,12},{12,8},{16,20},{20,16},{24,28},{28,24},{1,5},{5... | collective-permute-start | bytes 589832 | tf_op jit(solution)/shard_map/ppermute | solution.py:272
  15.7 11.9 %collective-permute-start.5 = (bf16[640,128]{1,0:T(8,128)(2,1)S(1)}, bf16[640,128]{1,0:T(8,128)(2,1)S(1)}, u32[]{:S(2)}, u32[]{:S(2)}) collective-permute-start(bf16[640,128]{1,0:T(8,128)(2,1)S(1)} %get-tuple-element.36), channel_id=1, source_target_pairs={{0,1},{1,0},{2,3},{3,2},{4,5},{5,4},{6,7},{7,6},{8,9},{9,8},{10,11... | collective-permute-start | bytes 491528 | tf_op jit(solution)/shard_map/ppermute | solution.py:303
  20.6 13.5 %collective-permute-start.4 = (bf16[1024,128]{1,0:T(8,128)(2,1)S(1)}, bf16[1024,128]{1,0:T(8,128)(2,1)S(1)}, u32[]{:S(2)}, u32[]{:S(2)}) collective-permute-start(bf16[1024,128]{1,0:T(8,128)(2,1)S(1)} %get-tuple-element.34), channel_id=1, source_target_pairs={{0,1},{1,0},{2,3},{3,2},{4,5},{5,4},{6,7},{7,6},{8,9},{9,8},{10,11... | collective-permute-start | bytes 786440 | tf_op jit(solution)/shard_map/ppermute | solution.py:303
  21.7 12.4 %collective-permute-start.8 = (bf16[384,128]{1,0:T(8,128)(2,1)S(1)}, bf16[384,128]{1,0:T(8,128)(2,1)S(1)}, u32[]{:S(2)}, u32[]{:S(2)}) collective-permute-start(bf16[384,128]{1,0:T(8,128)(2,1)S(1)} %get-tuple-element.38), channel_id=1, source_target_pairs={{0,3},{1,2},{2,1},{3,0},{4,7},{5,6},{6,5},{7,4},{8,11},{9,10},{10,... | collective-permute-start | bytes 294920 | tf_op jit(solution)/shard_map/ppermute | solution.py:303
  25.4 8.7 %collective-permute-start.7 = (bf16[384,128]{1,0:T(8,128)(2,1)S(1)}, bf16[384,128]{1,0:T(8,128)(2,1)S(1)}, u32[]{:S(2)}, u32[]{:S(2)}) collective-permute-start(bf16[384,128]{1,0:T(8,128)(2,1)S(1)} %get-tuple-element.37), channel_id=1, source_target_pairs={{0,2},{1,3},{2,0},{3,1},{4,6},{5,7},{6,4},{7,5},{8,10},{9,11},{10,... | collective-permute-start | bytes 294920 | tf_op jit(solution)/shard_map/ppermute | solution.py:303
  27.7 14.4 %collective-permute-start.6 = (bf16[640,128]{1,0:T(8,128)(2,1)S(1)}, bf16[640,128]{1,0:T(8,128)(2,1)S(1)}, u32[]{:S(2)}, u32[]{:S(2)}) collective-permute-start(bf16[640,128]{1,0:T(8,128)(2,1)S(1)} %add_convert_fusion.1), channel_id=1, source_target_pairs={{0,2},{1,3},{2,0},{3,1},{4,6},{5,7},{6,4},{7,5},{8,10},{9,11},{10,... | collective-permute-start | bytes 491528 | tf_op jit(solution)/shard_map/ppermute | solution.py:303

commit v3 on v2

--- a/solution.py
+++ b/solution.py
@@ -89,9 +89,9 @@
     return size ** (-0.5) * math.log2(math.e)
 
 
-def parts_of(w_hbm, mask, w_ref):
+def parts_of(w_hbm, mask, first, w_ref):
     rows = w_ref.shape[0]
-    begin = (lax.axis_index("tp") ^ mask) * rows
+    begin = (lax.axis_index("tp") ^ mask) * (w_hbm.shape[0] // lax.axis_size("tp")) + first
     part = rows // PARTS
     return [
         (w_hbm.at[pl.ds(pl.multiple_of(begin + i, 16), part), :], w_ref.at[i : i + part, :])
@@ -99,10 +99,13 @@
     ]
 
 
-def own_kernel(blocks_hbm, q_hbm, wk_hbm, wv_hbm, w_hbm, qh_ref, hide_ref, w_ref, top_ref, total_ref, summed_ref,
+def own_kernel(blocks_hbm, q_hbm, wk_hbm, wv_hbm, w_hbm,
+               qh_ref, hide_ref, farther_ref, far_ref, top_ref, total_ref, summed_ref,
                blocks_ref, q_ref, wk_ref, wv_ref, qf_ref, sems):
     pairs = [(blocks_hbm, blocks_ref), (q_hbm, q_ref), (wk_hbm, wk_ref), (wv_hbm, wv_ref)]
-    copies = fetch(pairs + parts_of(w_hbm, 3, w_ref), sems)
+    weights = parts_of(w_hbm, 3, 0, farther_ref)
+    weights += parts_of(w_hbm, 2, farther_ref.shape[0] - far_ref.shape[0], far_ref)
+    copies = fetch(pairs + weights, sems)
     wait(copies[: len(pairs)])
     tok_rows, size = wk_ref.shape
     heads = q_ref.shape[0] // tok_rows
@@ -145,30 +148,31 @@
     return jnp.concatenate([column] * (lanes // width), axis=1)
 
 
-def fold_blocks(order, anchors, retained, qh_ref, hide_ref, block_ref, state_refs, finish):
+def fold_blocks(orders, anchors, retained, qh_ref, hide_ref, block_refs, state_refs, finish):
     top_ref, total_ref, summed_ref = state_refs
     tok_rows = hide_ref.shape[1]
     size = qh_ref.shape[1]
     heads = qh_ref.shape[0] // tok_rows
-    seen, past, value_cols = rows_of(block_ref, anchors, retained)
-    bias = hidden_rows(hide_ref, order, retained, PAIR * tok_rows)
-    groups = [(seen, lambda s: s), (past, lambda s: s + bias)]
+    groups, columns = [], []
+    for order, block_ref in zip(orders, block_refs):
+        seen, past, value_cols = rows_of(block_ref, anchors, retained)
+        bias = hidden_rows(hide_ref, order, retained, PAIR * tok_rows)
+        groups += [(seen, lambda s: s), (past, lambda s, bias=bias: s + bias)]
+        columns.append(value_cols)
+    value_cols = jnp.concatenate(columns, axis=1)
     for h in range(0, heads, PAIR):
         cols = slice(h * tok_rows, (h + PAIR) * tok_rows)
         before = (top_ref[:, cols], total_ref[:, cols], summed_ref[:, cols])
         finish(h, cols, fold(qh_ref[cols, :], before, groups, value_cols, factor_of(size)))
 
 
-def early_kernel(order, anchors, retained, qh_ref, hide_ref, block_ref, top0, total0, summed0,
-                 top_ref, total_ref, summed_ref):
+def early_kernel(orders, anchors, retained, qh_ref, hide_ref, *refs):
+    block_refs, (top0, total0, summed0, top_ref, total_ref, summed_ref) = refs[: len(orders)], refs[len(orders) :]
+
     def finish(h, cols, state):
         top_ref[:, cols], total_ref[:, cols], summed_ref[:, cols] = state
 
-    fold_blocks(order, anchors, retained, qh_ref, hide_ref, block_ref, (top0, total0, summed0), finish)
-
-
-def fetch_kernel(hide_ref, w_hbm, far_ref, near_ref, sems):
-    wait(fetch(parts_of(w_hbm, 2, far_ref) + parts_of(w_hbm, 1, near_ref), sems))
+    fold_blocks(orders, anchors, retained, qh_ref, hide_ref, block_refs, (top0, total0, summed0), finish)
 
 
 def project(w_ref, first, att_ref, out_ref):
@@ -179,7 +183,7 @@
         out_ref[start : start + tile, :] = part.astype(out_ref.dtype)
 
 
-def late_kernel(order, anchors, retained, qh_ref, hide_ref, block_ref, top0, total0, summed0, w_ref,
+def late_kernel(orders, anchors, retained, qh_ref, hide_ref, block_ref, top0, total0, summed0, w_ref,
                 att_ref, first_ref):
     tok_rows = hide_ref.shape[1]
     size = qh_ref.shape[1]
@@ -190,22 +194,24 @@
         for j in range(PAIR):
             att_ref[(h + j) * size : (h + j + 1) * size, :] = attended[:, j * tok_rows : (j + 1) * tok_rows]
 
-    fold_blocks(order, anchors, retained, qh_ref, hide_ref, block_ref, (top0, total0, summed0), finish)
+    fold_blocks(orders, anchors, retained, qh_ref, hide_ref, (block_ref,), (top0, total0, summed0), finish)
     project(w_ref, 0, att_ref, first_ref)
 
 
-def direct_kernel(att_ref, farther_w, far_w, farther_ref, far_ref):
-    for w_ref, out_ref in ((farther_w, farther_ref), (far_w, far_ref)):
-        project(w_ref, w_ref.shape[0] - out_ref.shape[0], att_ref, out_ref)
-
-
-def later_kernel(att_ref, far_w, near_w, across_ref, near_ref):
+def direct_kernel(att_ref, farther_w, far_w, far_ref, farther_ref):
+    project(far_w, 0, att_ref, far_ref)
+    project(farther_w, farther_w.shape[0] - farther_ref.shape[0], att_ref, farther_ref)
+
+
+def later_kernel(att_ref, w_hbm, across_ref, near_ref, far_w, near_w, sems):
+    copies = fetch(parts_of(w_hbm, 2, 0, far_w) + parts_of(w_hbm, 1, 0, near_w), sems)
+    wait(copies)
     project(far_w, 0, att_ref, across_ref)
     project(near_w, 0, att_ref, near_ref)
 
 
 def own_chunk_kernel(att_ref, w_hbm, out_ref, w_ref, sems):
-    wait(fetch(parts_of(w_hbm, 0, w_ref), sems))
+    wait(fetch(parts_of(w_hbm, 0, 0, w_ref), sems))
     project(w_ref, 0, att_ref, out_ref)
 
 
@@ -225,7 +231,8 @@
     chunk_rows = out_weight.shape[0] // tp
     features = heads * size
     row = lambda n: shape((n, size), BF16)
-    chunk, weight = shape((chunk_rows, tok_rows), BF16), shape((chunk_rows, features), BF16)
+    chunk = shape((chunk_rows, tok_rows), BF16)
+    weights = lambda n: shape((n, features), BF16)
     relay_rows = chunk_rows * RELAY_PARTS // ALL_PARTS
     relayed = shape((relay_rows, tok_rows), BF16)
     direct = shape((chunk_rows - relay_rows, tok_rows), BF16)
@@ -249,10 +256,10 @@
         shape((1, query_rows), F32),
         shape((size, query_rows), F32),
     )
-    qh, hide, w_farther, *state = call(
+    qh, hide, w_farther, w_far, *state = call(
         own_kernel,
         (block_of_device, queries.reshape(query_rows, size), wk, wv, out_weight),
-        (row(query_rows), shape((slots, tok_rows), F32), weight, *stats),
+        (row(query_rows), shape((slots, tok_rows), F32), weights(chunk_rows), weights(chunk_rows - relay_rows), *stats),
         4 * query_rows * tok_rows * size,
         in_specs=[HBM] * 5,
         scratch=[
@@ -261,7 +268,7 @@
             pltpu.VMEM((tok_rows, size), BF16),
             pltpu.VMEM((tok_rows, size), BF16),
             pltpu.VMEM((query_rows, size), F32),
-            DMA((4 + PARTS,)),
+            DMA((4 + 2 * PARTS,)),
         ],
     )
     order = [0]
@@ -275,38 +282,49 @@
         held = jnp.concatenate([held, exchange(step)], axis=0)
         order = order + [j ^ step for j in order]
         step //= 2
-    masks = (6, 4, 2)
-    held = jnp.concatenate([held] + [exchange(mask) for mask in masks], axis=0)
-    order = [j ^ mask for mask in (0, *masks) for j in order]
-    w_far, w_near = call(
-        fetch_kernel, (hide, out_weight), (weight, weight), 0, in_specs=[VMEM, HBM], scratch=[DMA((2 * PARTS,))]
-    )
-    step = 1
-    other = exchange(step)
-    late_order = [j ^ step for j in order]
-    half = (slots // 2, packed, size)
-    fold_flops = 4 * query_rows * (slots // 2) * (anchors + retained) * size
+    pieces = [exchange(mask) for mask in (6, 4, 2)]
+    partner = exchange(1)
+    partner_order = [j ^ 1 for j in order]
+    rest_order = [j ^ mask for mask in (6, 4, 2) for j in order]
+    late_order = [j ^ 1 for j in rest_order]
+    blocks = lambda x: x.reshape(x.shape[0] // packed, packed, size)
+    fold_flops = lambda n: 4 * query_rows * n * (anchors + retained) * size
     state = call(
-        functools.partial(early_kernel, order, anchors, retained),
-        (qh, hide, held.reshape(half), *state),
+        functools.partial(early_kernel, (order, partner_order), anchors, retained),
+        (qh, hide, blocks(held), blocks(partner), *state),
         stats,
-        fold_flops,
+        fold_flops(2 * len(order)),
+    )
+    held = jnp.concatenate(pieces, axis=0)
+    other = exchange(1)
+    state = call(
+        functools.partial(early_kernel, (rest_order,), anchors, retained),
+        (qh, hide, blocks(held), *state),
+        stats,
+        fold_flops(len(rest_order)),
     )
     att, first = call(
-        functools.partial(late_kernel, late_order, anchors, retained),
-        (qh, hide, other.reshape(half), *state, w_farther),
+        functools.partial(late_kernel, (late_order,), anchors, retained),
+        (qh, hide, blocks(other), *state, w_farther),
         (shape((features, tok_rows), BF16), relayed),
-        fold_flops + chunk_flops // 2,
+        fold_flops(len(late_order)) + chunk_flops // 2,
     )
 
     def send(x, mask):
         return lax.ppermute(x, "tp", [(i, i ^ mask) for i in range(tp)])
 
     relay = send(first, 1)
-    farther, far = call(direct_kernel, (att, w_farther, w_far), (direct, direct), chunk_flops)
+    far, farther = call(direct_kernel, (att, w_farther, w_far), (direct, direct), chunk_flops)
+    far = send(far, 2)
     farther = send(farther, 3)
-    far = send(far, 2)
-    across, near = call(later_kernel, (att, w_far, w_near), (relayed, chunk), chunk_flops)
+    across, near = call(
+        later_kernel,
+        (att, out_weight),
+        (relayed, chunk),
+        chunk_flops,
+        in_specs=[VMEM, HBM],
+        scratch=[pltpu.VMEM((relay_rows, features), BF16), pltpu.VMEM((chunk_rows, features), BF16), DMA((2 * PARTS,))],
+    )
     across = send(add(across, relay), 2)
     near = send(near, 1)
     own = call(

time: 43.2 us -> 42.5 us (0.984)
  waiting for transfers between devices: 16.4 us -> 15.4 us
  Pallas kernels: 12.1 us -> 12.7 us
    ppermute x4 -> x5, waiting for transfers between devices: 4.97 us -> 3.94 us  [exchange(): return lax.ppermute(held, 'ctx', [(i, i ^ mask) for i in range(slots)])]
    ppermute x5, starting transfers between devices: 8.82 us -> 7.91 us  [send(): return lax.ppermute(x, 'tp', [(i, i ^ mask) for i in range(tp)])]
    pallas_call x8, Pallas kernels: 12.1 us -> 12.7 us  [call(): pl.pallas_call(kernel, out_shape=out_shape, in_specs=in_specs or [VMEM] *...]
    ppermute x4 -> x5, starting transfers between devices: 4.64 us -> 5.2 us  [exchange(): return lax.ppermute(held, 'ctx', [(i, i ^ mask) for i in range(slots)])]
  transfers between devices with their start and end apart: 9 -> 10, of which waited for: 5 -> 6; matrix products, arithmetic and copies ran while one was open for 0% -> 0% of each run, Pallas kernels for 21% -> 24%
where the time goes in v3:
time: 42.5 us; the launch traced here: 42.2 us
  waiting for transfers between devices  15.4 us (36%)
  starting transfers between devices  13.1 us (31%)
  Pallas kernels  12.7 us (30%)
  other arithmetic  0.89 us (2%)
    pallas_call x8, Pallas kernels, call(): pl.pallas_call(kernel, out_shape=out_shape, in_specs=in_specs or [VMEM] *...  12.7 us
    ppermute x5, waiting for transfers between devices, send(): return lax.ppermute(x, 'tp', [(i, i ^ mask) for i in range(tp)])  11.5 us
    ppermute x5, starting transfers between devices, send(): return lax.ppermute(x, 'tp', [(i, i ^ mask) for i in range(tp)])  7.91 us
    ppermute x5, starting transfers between devices, exchange(): return lax.ppermute(held, 'ctx', [(i, i ^ mask) for i in range(slots)])  5.2 us
    ppermute x5, waiting for transfers between devices, exchange(): return lax.ppermute(held, 'ctx', [(i, i ^ mask) for i in range(slots)])  3.94 us
  transfers between devices with their start and end apart: 10, of which 6 were waited for; matrix products, arithmetic and copies ran while one was open for 0% of the time, Pallas kernels for 24%

profile of v3, /device:TPU:0, one launch (start us, length us, event | category | flops | bytes accessed | tf_op | source)
XLA Modules:
  0.0 42.2 jit_solution(4188992696642411069)
XLA Ops:
  0.0 1.0 %shard_map.83 = bf16[192,128]{1,0:T(8,128)(2,1)S(1)} custom-call(s32[8,32]{1,0:T(8,128)} %rows_hbm.1, bf16[128,128]{1,0:T(8,128)(2,1)} %bitcast.14, bf16[128,128]{1,0:T(8,128)(2,1)} %bitcast.16, bf16[64,128]{1,0:T(8,128)(2,1)} %bitcast.18, bf16[64,128]{1,0:T(8,128)(2,1)} %bitcast.19), custom_call_target="tpu_custom_call" | custom-call | flops 2097152 | bytes 99328 | tf_op jit(solution)/shard_map/pallas_call | solution.py:31
  1.0 4.0 %collective-permute-start = (bf16[192,128]{1,0:T(8,128)(2,1)S(1)}, bf16[192,128]{1,0:T(8,128)(2,1)S(1)}, u32[]{:S(2)}, u32[]{:S(2)}) collective-permute-start(bf16[192,128]{1,0:T(8,128)(2,1)S(1)} %shard_map.83), channel_id=1, source_target_pairs={{0,24},{4,28},{8,16},{12,20},{16,8},{20,12},{24,0},{28,4},{1,25},{... | collective-permute-start | bytes 147464 | tf_op jit(solution)/shard_map/ppermute | solution.py:279
  5.0 0.5 %collective-permute-start.1 = (bf16[192,128]{1,0:T(8,128)(2,1)S(1)}, bf16[192,128]{1,0:T(8,128)(2,1)S(1)}, u32[]{:S(2)}, u32[]{:S(2)}) collective-permute-start(bf16[192,128]{1,0:T(8,128)(2,1)S(1)} %shard_map.83), channel_id=1, source_target_pairs={{0,16},{4,20},{8,24},{12,28},{16,0},{20,4},{24,8},{28,12},{1,17},{... | collective-permute-start | bytes 147464 | tf_op jit(solution)/shard_map/ppermute | solution.py:279
  5.5 0.1 collective-permute-start.2
  5.7 1.4 %collective-permute-done = bf16[192,128]{1,0:T(8,128)(2,1)S(1)} collective-permute-done((bf16[192,128]{1,0:T(8,128)(2,1)S(1)}, bf16[192,128]{1,0:T(8,128)(2,1)S(1)}, u32[]{:S(2)}, u32[]{:S(2)}) %collective-permute-start) | collective-permute-done | bytes 49184 | tf_op jit(solution)/shard_map/ppermute | solution.py:279
  7.1 2.0 %collective-permute-done.1 = bf16[192,128]{1,0:T(8,128)(2,1)S(1)} collective-permute-done((bf16[192,128]{1,0:T(8,128)(2,1)S(1)}, bf16[192,128]{1,0:T(8,128)(2,1)S(1)}, u32[]{:S(2)}, u32[]{:S(2)}) %collective-permute-start.1) | collective-permute-done | bytes 49184 | tf_op jit(solution)/shard_map/ppermute | solution.py:279
  9.1 0.5 %collective-permute-done.2 = bf16[192,128]{1,0:T(8,128)(2,1)S(1)} collective-permute-done((bf16[192,128]{1,0:T(8,128)(2,1)S(1)}, bf16[192,128]{1,0:T(8,128)(2,1)S(1)}, u32[]{:S(2)}, u32[]{:S(2)}) %collective-permute-start.2) | collective-permute-done | bytes 49184 | tf_op jit(solution)/shard_map/ppermute | solution.py:279
  9.6 0.1 collective-permute-start.3
  9.7 0.5 %collective-permute-start.4 = (bf16[192,128]{1,0:T(8,128)(2,1)S(1)}, bf16[192,128]{1,0:T(8,128)(2,1)S(1)}, u32[]{:S(2)}, u32[]{:S(2)}) collective-permute-start(bf16[192,128]{1,0:T(8,128)(2,1)S(1)} %shard_map.83), channel_id=1, source_target_pairs={{0,4},{4,0},{8,12},{12,8},{16,20},{20,16},{24,28},{28,24},{1,5},{5... | collective-permute-start | bytes 147464 | tf_op jit(solution)/shard_map/ppermute | solution.py:279
  10.2 2.0 %shard_map.82 = (bf16[1024,128]{1,0:T(8,128)(2,1)S(1)}, f32[8,128]{1,0:T(8,128)S(1)}, bf16[1024,1024]{1,0:T(8,128)(2,1)S(1)}, bf16[384,1024]{1,0:T(8,128)(2,1)S(...) custom-call(s32[8]{0:T(128)} %blocks_hbm.1, bf16[1024,128]{1,0:T(8,128)(2,1)} %bitcast.13, ...), custom_call_target="tpu_custom_call" | custom-call | flops 67108864 | bytes 8716320 | tf_op jit(solution)/shard_map/pallas_call | solution.py:31
  12.2 0.0 collective-permute-done.4
  12.2 1.2 %shard_map.84 = (f32[1,1024]{1,0:T(1,128)S(1)}, f32[1,1024]{1,0:T(1,128)S(1)}, f32[128,1024]{1,0:T(8,128)S(1)}) custom-call(bf16[1024,128]{1,0:T(8,128)(2,1)S(1)} %get-tuple-element.24.qh_ref, f32[8,128]{1,0:T(8,128)S(1)} %get-tuple-element.25.hide_ref, bf16[1,192,128]{2,1,0:T(8,128)(2,1)S(1)} %bitcast.10, bf16[1,192,128]{2,1,0:T(8,128)(2,1)S(1)} %bitcast.12, ...), custom_call_target="tpu_custom_call" | custom-call | flops 100663296 | bytes 897024 | tf_op jit(solution)/shard_map/pallas_call | solution.py:31
  13.4 1.1 %shard_map.85 = (f32[1,1024]{1,0:T(1,128)S(1)}, f32[1,1024]{1,0:T(1,128)S(1)}, f32[128,1024]{1,0:T(8,128)S(1)}) custom-call(bf16[1024,128]{1,0:T(8,128)(2,1)S(1)} %get-tuple-element.24.qh_ref, f32[8,128]{1,0:T(8,128)S(1)} %get-tuple-element.25.hide_ref, bf16[3,192,128]{2,1,0:T(8,128)(2,1)S(1)} %bitcast.9, f32[1,1024]{1,0:T(1,128)S(1)} %get-tuple-element.29.refs_1_, ...), custom_call_target="tpu_custom_call" | custom-call | flops 150994944 | bytes 946176 | tf_op jit(solution)/shard_map/pallas_call | solution.py:31
  14.5 0.0 collective-permute-done.3
  14.5 1.6 %shard_map.86 = (bf16[1024,128]{1,0:T(8,128)(2,1)S(1)}, bf16[640,128]{1,0:T(8,128)(2,1)S(1)}) custom-call(bf16[1024,128]{1,0:T(8,128)(2,1)S(1)} %get-tuple-element.24.qh_ref, f32[8,128]{1,0:T(8,128)S(1)} %get-tuple-element.25.hide_ref, bf16[3,192,128]{2,1,0:T(8,128)(2,1)S(1)} %bitcast.11, f32[1,1024]{1,0:T(1,128)S(1)} %get-tuple-element.32.top0, ...), custom_call_target="tpu_custom_call" | custom-call | flops 285212672 | bytes 3043328 | tf_op jit(solution)/shard_map/pallas_call | solution.py:31
  16.1 1.6 %collective-permute-start.6 = (bf16[640,128]{1,0:T(8,128)(2,1)S(1)}, bf16[640,128]{1,0:T(8,128)(2,1)S(1)}, u32[]{:S(2)}, u32[]{:S(2)}) collective-permute-start(bf16[640,128]{1,0:T(8,128)(2,1)S(1)} %get-tuple-element.39), channel_id=1, source_target_pairs={{0,1},{1,0},{2,3},{3,2},{4,5},{5,4},{6,7},{7,6},{8,9},{9,8},{10,11... | collective-permute-start | bytes 491528 | tf_op jit(solution)/shard_map/ppermute | solution.py:314
  17.7 3.0 %shard_map.88 = (bf16[640,128]{1,0:T(8,128)(2,1)S(1)}, bf16[1024,128]{1,0:T(8,128)(2,1)S(1)}) custom-call(bf16[1024,128]{1,0:T(8,128)(2,1)S(1)} %get-tuple-element.36.att_ref, bf16[4096,1024]{1,0:T(8,128)(2,1)} %w_hbm.5), custom_call_target="tpu_custom_call" | custom-call | flops 268435456 | bytes 8650752 | tf_op jit(solution)/shard_map/pallas_call | solution.py:31
  20.8 0.5 %collective-permute-start.5 = (bf16[1024,128]{1,0:T(8,128)(2,1)S(1)}, bf16[1024,128]{1,0:T(8,128)(2,1)S(1)}, u32[]{:S(2)}, u32[]{:S(2)}) collective-permute-start(bf16[1024,128]{1,0:T(8,128)(2,1)S(1)} %get-tuple-element.37), channel_id=1, source_target_pairs={{0,1},{1,0},{2,3},{3,2},{4,5},{5,4},{6,7},{7,6},{8,9},{9,8},{10,11... | collective-permute-start | bytes 786440 | tf_op jit(solution)/shard_map/ppermute | solution.py:314
  21.3 0.6 %shard_map.89 = (bf16[384,128]{1,0:T(8,128)(2,1)S(1)}, bf16[384,128]{1,0:T(8,128)(2,1)S(1)}) custom-call(bf16[1024,128]{1,0:T(8,128)(2,1)S(1)} %get-tuple-element.36.att_ref, bf16[1024,1024]{1,0:T(8,128)(2,1)S(1)} %get-tuple-element.35.w_ref.farther_w, bf16[384,1024]{1,0:T(8,128)(2,1)S(1)} %get-tuple-element.40.far_w), custom_call_target="tpu_custom_call" | custom-call | flops 268435456 | bytes 3145728 | tf_op jit(solution)/shard_map/pallas_call | solution.py:31
  21.8 2.6 %collective-permute-start.8 = (bf16[384,128]{1,0:T(8,128)(2,1)S(1)}, bf16[384,128]{1,0:T(8,128)(2,1)S(1)}, u32[]{:S(2)}, u32[]{:S(2)}) collective-permute-start(bf16[384,128]{1,0:T(8,128)(2,1)S(1)} %get-tuple-element.41), channel_id=1, source_target_pairs={{0,2},{1,3},{2,0},{3,1},{4,6},{5,7},{6,4},{7,5},{8,10},{9,11},{10,... | collective-permute-start | bytes 294920 | tf_op jit(solution)/shard_map/ppermute | solution.py:314
  24.5 1.4 %collective-permute-start.9 = (bf16[384,128]{1,0:T(8,128)(2,1)S(1)}, bf16[384,128]{1,0:T(8,128)(2,1)S(1)}, u32[]{:S(2)}, u32[]{:S(2)}) collective-permute-start(bf16[384,128]{1,0:T(8,128)(2,1)S(1)} %get-tuple-element.42), channel_id=1, source_target_pairs={{0,3},{1,2},{2,1},{3,0},{4,7},{5,6},{6,5},{7,4},{8,11},{9,10},{10,... | collective-permute-start | bytes 294920 | tf_op jit(solution)/shard_map/ppermute | solution.py:314
  25.8 2.2 %shard_map.87 = bf16[1024,128]{1,0:T(8,128)(2,1)S(1)} custom-call(bf16[1024,128]{1,0:T(8,128)(2,1)S(1)} %get-tuple-element.36.att_ref, bf16[4096,1024]{1,0:T(8,128)(2,1)} %w_hbm.5), custom_call_target="tpu_custom_call" | custom-call | flops 268435456 | bytes 8650752 | tf_op jit(solution)/shard_map/pallas_call | solution.py:31
  28.1 0.0 collective-permute-done.6
  28.2 1.7 %collective-permute-start.7 = (bf16[640,128]{1,0:T(8,128)(2,1)S(1)}, bf16[640,128]{1,0:T(8,128)(2,1)S(1)}, u32[]{:S(2)}, u32[]{:S(2)}) collective-permute-start(bf16[640,128]{1,0:T(8,128)(2,1)S(1)} %add_convert_fusion.1), channel_id=1, source_target_pairs={{0,2},{1,3},{2,0},{3,1},{4,6},{5,7},{6,4},{7,5},{8,10},{9,11},{10,... | collective-permute-start | bytes 491528 | tf_op jit(solution)/shard_map/ppermute | solution.py:314
  29.9 0.2 collective-permute-done.8
  30.1 6.2 %collective-permute-done.9 = bf16[384,128]{1,0:T(8,128)(2,1)S(1)} collective-permute-done((bf16[384,128]{1,0:T(8,128)(2,1)S(1)}, bf16[384,128]{1,0:T(8,128)(2,1)S(1)}, u32[]{:S(2)}, u32[]{:S(2)}) %collective-permute-start.9) | collective-permute-done | bytes 98336 | tf_op jit(solution)/shard_map/ppermute | solution.py:314
  36.3 0.0 collective-permute-done.5
  36.3 0.1 add_convert_fusion.2
  36.4 5.0 %collective-permute-done.7 = bf16[640,128]{1,0:T(8,128)(2,1)S(1)} collective-permute-done((bf16[640,128]{1,0:T(8,128)(2,1)S(1)}, bf16[640,128]{1,0:T(8,128)(2,1)S(1)}, u32[]{:S(2)}, u32[]{:S(2)}) %collective-permute-start.7) | collective-permute-done | bytes 163872 | tf_op jit(solution)/shard_map/ppermute | solution.py:314
  41.4 0.1 add_convert_fusion
  41.5 0.7 %pad_maximum_fusion = bf16[1024,128]{1,0:T(8,128)(2,1)} fusion(bf16[384,128]{1,0:T(8,128)(2,1)S(1)} %add_convert_fusion.2, bf16[640,128]{1,0:T(8,128)(2,1)S(1)} %add_convert_fusion), kind=kLoop, calls=%fused_computation.2 | loop fusion | flops 524288 | bytes 524288 | tf_op jit(solution)/shard_map/concatenate | solution.py:340
  (4 shorter events, 0.1 us)
Async XLA Ops:
  1.0 6.1 %collective-permute-start = (bf16[192,128]{1,0:T(8,128)(2,1)S(1)}, bf16[192,128]{1,0:T(8,128)(2,1)S(1)}, u32[]{:S(2)}, u32[]{:S(2)}) collective-permute-start(bf16[192,128]{1,0:T(8,128)(2,1)S(1)} %shard_map.83), channel_id=1, source_target_pairs={{0,24},{4,28},{8,16},{12,20},{16,8},{20,12},{24,0},{28,4},{1,25},{... | collective-permute-start | bytes 147464 | tf_op jit(solution)/shard_map/ppermute | solution.py:279
  5.0 4.1 %collective-permute-start.1 = (bf16[192,128]{1,0:T(8,128)(2,1)S(1)}, bf16[192,128]{1,0:T(8,128)(2,1)S(1)}, u32[]{:S(2)}, u32[]{:S(2)}) collective-permute-start(bf16[192,128]{1,0:T(8,128)(2,1)S(1)} %shard_map.83), channel_id=1, source_target_pairs={{0,16},{4,20},{8,24},{12,28},{16,0},{20,4},{24,8},{28,12},{1,17},{... | collective-permute-start | bytes 147464 | tf_op jit(solution)/shard_map/ppermute | solution.py:279
  5.5 4.1 %collective-permute-start.2 = (bf16[192,128]{1,0:T(8,128)(2,1)S(1)}, bf16[192,128]{1,0:T(8,128)(2,1)S(1)}, u32[]{:S(2)}, u32[]{:S(2)}) collective-permute-start(bf16[192,128]{1,0:T(8,128)(2,1)S(1)} %shard_map.83), channel_id=1, source_target_pairs={{0,8},{4,12},{8,0},{12,4},{16,24},{20,28},{24,16},{28,20},{1,9},{5... | collective-permute-start | bytes 147464 | tf_op jit(solution)/shard_map/ppermute | solution.py:279
  9.6 4.9 %collective-permute-start.3 = (bf16[576,128]{1,0:T(8,128)(2,1)S(1)}, bf16[576,128]{1,0:T(8,128)(2,1)S(1)}, u32[]{:S(2)}, u32[]{:S(2)}) collective-permute-start(bf16[576,128]{1,0:T(8,128)(2,1)S(1)} %constant_dynamic-update-slice_fusion), channel_id=1, source_target_pairs={{0,4},{4,0},{8,12},{12,8},{16,20},{20,16},{24,28},{28,24},{1,5},{5... | collective-permute-start | bytes 442376 | tf_op jit(solution)/shard_map/ppermute | solution.py:279
  9.7 2.5 %collective-permute-start.4 = (bf16[192,128]{1,0:T(8,128)(2,1)S(1)}, bf16[192,128]{1,0:T(8,128)(2,1)S(1)}, u32[]{:S(2)}, u32[]{:S(2)}) collective-permute-start(bf16[192,128]{1,0:T(8,128)(2,1)S(1)} %shard_map.83), channel_id=1, source_target_pairs={{0,4},{4,0},{8,12},{12,8},{16,20},{20,16},{24,28},{28,24},{1,5},{5... | collective-permute-start | bytes 147464 | tf_op jit(solution)/shard_map/ppermute | solution.py:279
  16.1 12.0 %collective-permute-start.6 = (bf16[640,128]{1,0:T(8,128)(2,1)S(1)}, bf16[640,128]{1,0:T(8,128)(2,1)S(1)}, u32[]{:S(2)}, u32[]{:S(2)}) collective-permute-start(bf16[640,128]{1,0:T(8,128)(2,1)S(1)} %get-tuple-element.39), channel_id=1, source_target_pairs={{0,1},{1,0},{2,3},{3,2},{4,5},{5,4},{6,7},{7,6},{8,9},{9,8},{10,11... | collective-permute-start | bytes 491528 | tf_op jit(solution)/shard_map/ppermute | solution.py:314
  20.8 15.6 %collective-permute-start.5 = (bf16[1024,128]{1,0:T(8,128)(2,1)S(1)}, bf16[1024,128]{1,0:T(8,128)(2,1)S(1)}, u32[]{:S(2)}, u32[]{:S(2)}) collective-permute-start(bf16[1024,128]{1,0:T(8,128)(2,1)S(1)} %get-tuple-element.37), channel_id=1, source_target_pairs={{0,1},{1,0},{2,3},{3,2},{4,5},{5,4},{6,7},{7,6},{8,9},{9,8},{10,11... | collective-permute-start | bytes 786440 | tf_op jit(solution)/shard_map/ppermute | solution.py:314
  21.8 8.3 %collective-permute-start.8 = (bf16[384,128]{1,0:T(8,128)(2,1)S(1)}, bf16[384,128]{1,0:T(8,128)(2,1)S(1)}, u32[]{:S(2)}, u32[]{:S(2)}) collective-permute-start(bf16[384,128]{1,0:T(8,128)(2,1)S(1)} %get-tuple-element.41), channel_id=1, source_target_pairs={{0,2},{1,3},{2,0},{3,1},{4,6},{5,7},{6,4},{7,5},{8,10},{9,11},{10,... | collective-permute-start | bytes 294920 | tf_op jit(solution)/shard_map/ppermute | solution.py:314
  24.5 11.8 %collective-permute-start.9 = (bf16[384,128]{1,0:T(8,128)(2,1)S(1)}, bf16[384,128]{1,0:T(8,128)(2,1)S(1)}, u32[]{:S(2)}, u32[]{:S(2)}) collective-permute-start(bf16[384,128]{1,0:T(8,128)(2,1)S(1)} %get-tuple-element.42), channel_id=1, source_target_pairs={{0,3},{1,2},{2,1},{3,0},{4,7},{5,6},{6,5},{7,4},{8,11},{9,10},{10,... | collective-permute-start | bytes 294920 | tf_op jit(solution)/shard_map/ppermute | solution.py:314
  28.2 13.3 %collective-permute-start.7 = (bf16[640,128]{1,0:T(8,128)(2,1)S(1)}, bf16[640,128]{1,0:T(8,128)(2,1)S(1)}, u32[]{:S(2)}, u32[]{:S(2)}) collective-permute-start(bf16[640,128]{1,0:T(8,128)(2,1)S(1)} %add_convert_fusion.1), channel_id=1, source_target_pairs={{0,2},{1,3},{2,0},{3,1},{4,6},{5,7},{6,4},{7,5},{8,10},{9,11},{10,... | collective-permute-start | bytes 491528 | tf_op jit(solution)/shard_map/ppermute | solution.py:314

commit v4 on v3

--- a/solution.py
+++ b/solution.py
@@ -15,7 +15,7 @@
 VMEM = pl.BlockSpec(memory_space=pltpu.VMEM)
 HBM = pl.BlockSpec(memory_space=pltpu.HBM)
 DMA = pltpu.SemaphoreType.DMA
-PAIR = 2
+GROUP = 8
 PARTS = 4
 RELAY_PARTS, ALL_PARTS = 5, 8
 
@@ -115,17 +115,17 @@
         bias = jnp.where(blocks_ref[slot ^ j] < own_block, 0.0, HIDDEN)
         hide_ref[j : j + 1, :] = jnp.full((1, hide_ref.shape[1]), bias, F32)
     qf_ref[...] = q_ref[...].astype(F32)
-    lanes = PAIR * tok_rows
+    lanes = GROUP * tok_rows
     key_at = lax.broadcasted_iota(jnp.int32, (tok_rows, lanes), 0)
     row_at = lax.broadcasted_iota(jnp.int32, (tok_rows, lanes), 1) % tok_rows
     causal = key_at <= row_at
     value_cols = wv_ref[...].T
-    for h in range(0, heads, PAIR):
-        for j in range(h, h + PAIR):
+    for h in range(0, heads, GROUP):
+        for j in range(h, h + GROUP):
             qh_ref[j * tok_rows : (j + 1) * tok_rows, :] = qf_ref[
                 pl.ds(j, tok_rows, stride=heads), :
             ].astype(BF16)
-        cols = slice(h * tok_rows, (h + PAIR) * tok_rows)
+        cols = slice(h * tok_rows, (h + GROUP) * tok_rows)
         groups = [(wk_ref[...], lambda s: jnp.where(causal, s, HIDDEN))]
         state = fold(qh_ref[cols, :], None, groups, value_cols, factor_of(size))
         top_ref[:, cols], total_ref[:, cols], summed_ref[:, cols] = state
@@ -156,12 +156,12 @@
     groups, columns = [], []
     for order, block_ref in zip(orders, block_refs):
         seen, past, value_cols = rows_of(block_ref, anchors, retained)
-        bias = hidden_rows(hide_ref, order, retained, PAIR * tok_rows)
+        bias = hidden_rows(hide_ref, order, retained, GROUP * tok_rows)
         groups += [(seen, lambda s: s), (past, lambda s, bias=bias: s + bias)]
         columns.append(value_cols)
     value_cols = jnp.concatenate(columns, axis=1)
-    for h in range(0, heads, PAIR):
-        cols = slice(h * tok_rows, (h + PAIR) * tok_rows)
+    for h in range(0, heads, GROUP):
+        cols = slice(h * tok_rows, (h + GROUP) * tok_rows)
         before = (top_ref[:, cols], total_ref[:, cols], summed_ref[:, cols])
         finish(h, cols, fold(qh_ref[cols, :], before, groups, value_cols, factor_of(size)))
 
@@ -183,23 +183,23 @@
         out_ref[start : start + tile, :] = part.astype(out_ref.dtype)
 
 
-def late_kernel(orders, anchors, retained, qh_ref, hide_ref, block_ref, top0, total0, summed0, w_ref,
-                att_ref, first_ref):
+def late_kernel(orders, anchors, retained, qh_ref, hide_ref, block_ref, top0, total0, summed0, w_ref, far_w,
+                att_ref, first_ref, far_ref):
     tok_rows = hide_ref.shape[1]
     size = qh_ref.shape[1]
 
     def finish(h, cols, state):
         _, total, summed = state
         attended = (summed / total).astype(BF16)
-        for j in range(PAIR):
+        for j in range(GROUP):
             att_ref[(h + j) * size : (h + j + 1) * size, :] = attended[:, j * tok_rows : (j + 1) * tok_rows]
 
     fold_blocks(orders, anchors, retained, qh_ref, hide_ref, (block_ref,), (top0, total0, summed0), finish)
     project(w_ref, 0, att_ref, first_ref)
-
-
-def direct_kernel(att_ref, farther_w, far_w, far_ref, farther_ref):
     project(far_w, 0, att_ref, far_ref)
+
+
+def direct_kernel(att_ref, farther_w, farther_ref):
     project(farther_w, farther_w.shape[0] - farther_ref.shape[0], att_ref, farther_ref)
 
 
@@ -282,31 +282,34 @@
         held = jnp.concatenate([held, exchange(step)], axis=0)
         order = order + [j ^ step for j in order]
         step //= 2
-    pieces = [exchange(mask) for mask in (6, 4, 2)]
+    diagonal, *sides = [exchange(mask) for mask in (6, 4, 2)]
     partner = exchange(1)
-    partner_order = [j ^ 1 for j in order]
-    rest_order = [j ^ mask for mask in (6, 4, 2) for j in order]
-    late_order = [j ^ 1 for j in rest_order]
+    across_chip = lambda order, mask: [j ^ mask for j in order]
+    partner_order, diagonal_order = across_chip(order, 1), across_chip(order, 6)
+    side_order = across_chip(order, 4) + across_chip(order, 2)
     blocks = lambda x: x.reshape(x.shape[0] // packed, packed, size)
     fold_flops = lambda n: 4 * query_rows * n * (anchors + retained) * size
-    state = call(
-        functools.partial(early_kernel, (order, partner_order), anchors, retained),
-        (qh, hide, blocks(held), blocks(partner), *state),
-        stats,
-        fold_flops(2 * len(order)),
-    )
-    held = jnp.concatenate(pieces, axis=0)
+
+    def attend(state, *pairs):
+        orders, arrays = zip(*pairs)
+        return call(
+            functools.partial(early_kernel, orders, anchors, retained),
+            (qh, hide, *[blocks(x) for x in arrays], *state),
+            stats,
+            fold_flops(sum(len(o) for o in orders)),
+        )
+
+    own_held, held = held, diagonal
+    diagonal_partner = exchange(1)
+    state = attend(state, (order, own_held), (partner_order, partner), (diagonal_order, diagonal))
+    held = jnp.concatenate(sides, axis=0)
     other = exchange(1)
-    state = call(
-        functools.partial(early_kernel, (rest_order,), anchors, retained),
-        (qh, hide, blocks(held), *state),
-        stats,
-        fold_flops(len(rest_order)),
-    )
-    att, first = call(
+    state = attend(state, (across_chip(diagonal_order, 1), diagonal_partner), (side_order, held))
+    late_order = across_chip(side_order, 1)
+    att, first, far = call(
         functools.partial(late_kernel, (late_order,), anchors, retained),
-        (qh, hide, blocks(other), *state, w_farther),
-        (shape((features, tok_rows), BF16), relayed),
+        (qh, hide, blocks(other), *state, w_farther, w_far),
+        (shape((features, tok_rows), BF16), relayed, direct),
         fold_flops(len(late_order)) + chunk_flops // 2,
     )
 
@@ -314,7 +317,7 @@
         return lax.ppermute(x, "tp", [(i, i ^ mask) for i in range(tp)])
 
     relay = send(first, 1)
-    far, farther = call(direct_kernel, (att, w_farther, w_far), (direct, direct), chunk_flops)
+    farther = call(direct_kernel, (att, w_farther), direct, chunk_flops)
     far = send(far, 2)
     farther = send(farther, 3)
     across, near = call(

time: 42.5 us -> 42.6 us (level)
  starting transfers between devices: 13.1 us -> 14.1 us
  Pallas kernels: 12.7 us -> 11.8 us
    ppermute x5, starting transfers between devices: 7.91 us -> 8.81 us  [send(): return lax.ppermute(x, 'tp', [(i, i ^ mask) for i in range(tp)])]
    pallas_call x8, Pallas kernels: 12.7 us -> 11.8 us  [call(): pl.pallas_call(kernel, out_shape=out_shape, in_specs=in_specs or [VMEM] *...]
    ppermute x5 -> x6, starting transfers between devices: 5.2 us -> 5.25 us  [exchange(): return lax.ppermute(held, 'ctx', [(i, i ^ mask) for i in range(slots)])]
    ppermute x5 -> x6, waiting for transfers between devices: 3.94 us -> 3.99 us  [exchange(): return lax.ppermute(held, 'ctx', [(i, i ^ mask) for i in range(slots)])]
  transfers between devices with their start and end apart: 10 -> 11, of which waited for: 6 -> 4; matrix products, arithmetic and copies ran while one was open for 0% -> 0% of each run, Pallas kernels for 24% -> 23%
where the time goes in v4:
time: 42.6 us; the launch traced here: 42.3 us
  waiting for transfers between devices  15.4 us (36%)
  starting transfers between devices  14.1 us (33%)
  Pallas kernels  11.8 us (28%)
  other arithmetic  0.89 us (2%)
    pallas_call x8, Pallas kernels, call(): pl.pallas_call(kernel, out_shape=out_shape, in_specs=in_specs or [VMEM] *...  11.8 us
    ppermute x5, waiting for transfers between devices, send(): return lax.ppermute(x, 'tp', [(i, i ^ mask) for i in range(tp)])  11.4 us
    ppermute x5, starting transfers between devices, send(): return lax.ppermute(x, 'tp', [(i, i ^ mask) for i in range(tp)])  8.81 us
    ppermute x6, starting transfers between devices, exchange(): return lax.ppermute(held, 'ctx', [(i, i ^ mask) for i in range(slots)])  5.25 us
    ppermute x6, waiting for transfers between devices, exchange(): return lax.ppermute(held, 'ctx', [(i, i ^ mask) for i in range(slots)])  3.99 us
  transfers between devices with their start and end apart: 11, of which 4 were waited for; matrix products, arithmetic and copies ran while one was open for 0% of the time, Pallas kernels for 23%

profile of v4, /device:TPU:0, one launch (start us, length us, event | category | flops | bytes accessed | tf_op | source)
XLA Modules:
  0.0 42.3 jit_solution(11068525829557260064)
XLA Ops:
  0.0 1.0 %shard_map.83 = bf16[192,128]{1,0:T(8,128)(2,1)S(1)} custom-call(s32[8,32]{1,0:T(8,128)} %rows_hbm.1, bf16[128,128]{1,0:T(8,128)(2,1)} %bitcast.18, bf16[128,128]{1,0:T(8,128)(2,1)} %bitcast.20, bf16[64,128]{1,0:T(8,128)(2,1)} %bitcast.22, bf16[64,128]{1,0:T(8,128)(2,1)} %bitcast.23), custom_call_target="tpu_custom_call" | custom-call | flops 2097152 | bytes 99328 | tf_op jit(solution)/shard_map/pallas_call | solution.py:31
  1.0 3.1 %collective-permute-start = (bf16[192,128]{1,0:T(8,128)(2,1)S(1)}, bf16[192,128]{1,0:T(8,128)(2,1)S(1)}, u32[]{:S(2)}, u32[]{:S(2)}) collective-permute-start(bf16[192,128]{1,0:T(8,128)(2,1)S(1)} %shard_map.83), channel_id=1, source_target_pairs={{0,16},{4,20},{8,24},{12,28},{16,0},{20,4},{24,8},{28,12},{1,17},{... | collective-permute-start | bytes 147464 | tf_op jit(solution)/shard_map/ppermute | solution.py:279
  4.1 1.4 %collective-permute-start.3 = (bf16[192,128]{1,0:T(8,128)(2,1)S(1)}, bf16[192,128]{1,0:T(8,128)(2,1)S(1)}, u32[]{:S(2)}, u32[]{:S(2)}) collective-permute-start(bf16[192,128]{1,0:T(8,128)(2,1)S(1)} %shard_map.83), channel_id=1, source_target_pairs={{0,24},{4,28},{8,16},{12,20},{16,8},{20,12},{24,0},{28,4},{1,25},{... | collective-permute-start | bytes 147464 | tf_op jit(solution)/shard_map/ppermute | solution.py:279
  5.5 0.1 collective-permute-start.1
  5.6 0.5 %collective-permute-done = bf16[192,128]{1,0:T(8,128)(2,1)S(1)} collective-permute-done((bf16[192,128]{1,0:T(8,128)(2,1)S(1)}, bf16[192,128]{1,0:T(8,128)(2,1)S(1)}, u32[]{:S(2)}, u32[]{:S(2)}) %collective-permute-start) | collective-permute-done | bytes 49184 | tf_op jit(solution)/shard_map/ppermute | solution.py:279
  6.2 3.4 %collective-permute-done.1 = bf16[192,128]{1,0:T(8,128)(2,1)S(1)} collective-permute-done((bf16[192,128]{1,0:T(8,128)(2,1)S(1)}, bf16[192,128]{1,0:T(8,128)(2,1)S(1)}, u32[]{:S(2)}, u32[]{:S(2)}) %collective-permute-start.1) | collective-permute-done | bytes 49184 | tf_op jit(solution)/shard_map/ppermute | solution.py:279
  9.6 0.1 collective-permute-start.2
  9.7 0.5 %collective-permute-start.5 = (bf16[192,128]{1,0:T(8,128)(2,1)S(1)}, bf16[192,128]{1,0:T(8,128)(2,1)S(1)}, u32[]{:S(2)}, u32[]{:S(2)}) collective-permute-start(bf16[192,128]{1,0:T(8,128)(2,1)S(1)} %shard_map.83), channel_id=1, source_target_pairs={{0,4},{4,0},{8,12},{12,8},{16,20},{20,16},{24,28},{28,24},{1,5},{5... | collective-permute-start | bytes 147464 | tf_op jit(solution)/shard_map/ppermute | solution.py:279
  10.2 0.0 collective-permute-done.3
  10.2 0.1 collective-permute-start.4
  10.3 2.0 %shard_map.82 = (bf16[1024,128]{1,0:T(8,128)(2,1)S(1)}, f32[8,128]{1,0:T(8,128)S(1)}, bf16[1024,1024]{1,0:T(8,128)(2,1)S(1)}, bf16[384,1024]{1,0:T(8,128)(2,1)S(...) custom-call(s32[8]{0:T(128)} %blocks_hbm.1, bf16[1024,128]{1,0:T(8,128)(2,1)} %bitcast.17, ...), custom_call_target="tpu_custom_call" | custom-call | flops 67108864 | bytes 8716320 | tf_op jit(solution)/shard_map/pallas_call | solution.py:31
  12.2 0.0 collective-permute-done.5
  12.3 1.1 %shard_map.84 = (f32[1,1024]{1,0:T(1,128)S(1)}, f32[1,1024]{1,0:T(1,128)S(1)}, f32[128,1024]{1,0:T(8,128)S(1)}) custom-call(bf16[1024,128]{1,0:T(8,128)(2,1)S(1)} %get-tuple-element.23.qh_ref, f32[8,128]{1,0:T(8,128)S(1)} %get-tuple-element.24.hide_ref, bf16[1,192,128]{2,1,0:T(8,128)(2,1)S(1)} %bitcast.12, bf16[1,192,128]{2,1,0:T(8,128)(2,1)S(1)} %bitcast.16, ...), custom_call_target="tpu_custom_call" | custom-call | flops 150994944 | bytes 946176 | tf_op jit(solution)/shard_map/pallas_call | solution.py:31
  13.3 0.0 collective-permute-done.4
  13.3 0.9 %shard_map.85 = (f32[1,1024]{1,0:T(1,128)S(1)}, f32[1,1024]{1,0:T(1,128)S(1)}, f32[128,1024]{1,0:T(8,128)S(1)}) custom-call(bf16[1024,128]{1,0:T(8,128)(2,1)S(1)} %get-tuple-element.23.qh_ref, f32[8,128]{1,0:T(8,128)S(1)} %get-tuple-element.24.hide_ref, bf16[1,192,128]{2,1,0:T(8,128)(2,1)S(1)} %bitcast.15, bf16[2,192,128]{2,1,0:T(8,128)(2,1)S(1)} %bitcast.11, ...), custom_call_target="tpu_custom_call" | custom-call | flops 150994944 | bytes 946176 | tf_op jit(solution)/shard_map/pallas_call | solution.py:31
  14.3 0.0 collective-permute-done.2
  14.3 1.2 %shard_map.86 = (bf16[1024,128]{1,0:T(8,128)(2,1)S(1)}, bf16[640,128]{1,0:T(8,128)(2,1)S(1)}, bf16[384,128]{1,0:T(8,128)(2,1)S(1)}) custom-call(bf16[1024,128]{1,0:T(8,128)(2,1)S(1)} %get-tuple-element.23.qh_ref, f32[8,128]{1,0:T(8,128)S(1)} %get-tuple-element.24.hide_ref, bf16[2,192,128]{2,1,0:T(8,128)(2,1)S(1)} %bitcast.13, ...), custom_call_target="tpu_custom_call" | custom-call | flops 234881024 | bytes 3780608 | tf_op jit(solution)/shard_map/pallas_call | solution.py:31
  15.5 1.6 %collective-permute-start.7 = (bf16[640,128]{1,0:T(8,128)(2,1)S(1)}, bf16[640,128]{1,0:T(8,128)(2,1)S(1)}, u32[]{:S(2)}, u32[]{:S(2)}) collective-permute-start(bf16[640,128]{1,0:T(8,128)(2,1)S(1)} %get-tuple-element.39), channel_id=1, source_target_pairs={{0,1},{1,0},{2,3},{3,2},{4,5},{5,4},{6,7},{7,6},{8,9},{9,8},{10,11... | collective-permute-start | bytes 491528 | tf_op jit(solution)/shard_map/ppermute | solution.py:317
  17.2 3.0 %shard_map.88 = (bf16[640,128]{1,0:T(8,128)(2,1)S(1)}, bf16[1024,128]{1,0:T(8,128)(2,1)S(1)}) custom-call(bf16[1024,128]{1,0:T(8,128)(2,1)S(1)} %get-tuple-element.36.att_ref, bf16[4096,1024]{1,0:T(8,128)(2,1)} %w_hbm.5), custom_call_target="tpu_custom_call" | custom-call | flops 268435456 | bytes 8650752 | tf_op jit(solution)/shard_map/pallas_call | solution.py:31
  20.2 0.5 %collective-permute-start.6 = (bf16[1024,128]{1,0:T(8,128)(2,1)S(1)}, bf16[1024,128]{1,0:T(8,128)(2,1)S(1)}, u32[]{:S(2)}, u32[]{:S(2)}) collective-permute-start(bf16[1024,128]{1,0:T(8,128)(2,1)S(1)} %get-tuple-element.37), channel_id=1, source_target_pairs={{0,1},{1,0},{2,3},{3,2},{4,5},{5,4},{6,7},{7,6},{8,9},{9,8},{10,11... | collective-permute-start | bytes 786440 | tf_op jit(solution)/shard_map/ppermute | solution.py:317
  20.7 0.4 shard_map.89
  21.1 3.7 %collective-permute-start.10 = (bf16[384,128]{1,0:T(8,128)(2,1)S(1)}, bf16[384,128]{1,0:T(8,128)(2,1)S(1)}, u32[]{:S(2)}, u32[]{:S(2)}) collective-permute-start(bf16[384,128]{1,0:T(8,128)(2,1)S(1)} %shard_map.89), channel_id=1, source_target_pairs={{0,3},{1,2},{2,1},{3,0},{4,7},{5,6},{6,5},{7,4},{8,11},{9,10},{10,... | collective-permute-start | bytes 294920 | tf_op jit(solution)/shard_map/ppermute | solution.py:317
  24.8 0.0 collective-permute-start.9
  24.8 2.3 %shard_map.87 = bf16[1024,128]{1,0:T(8,128)(2,1)S(1)} custom-call(bf16[1024,128]{1,0:T(8,128)(2,1)S(1)} %get-tuple-element.36.att_ref, bf16[4096,1024]{1,0:T(8,128)(2,1)} %w_hbm.5), custom_call_target="tpu_custom_call" | custom-call | flops 268435456 | bytes 8650752 | tf_op jit(solution)/shard_map/pallas_call | solution.py:31
  27.0 0.0 collective-permute-done.7
  27.1 3.0 %collective-permute-start.8 = (bf16[640,128]{1,0:T(8,128)(2,1)S(1)}, bf16[640,128]{1,0:T(8,128)(2,1)S(1)}, u32[]{:S(2)}, u32[]{:S(2)}) collective-permute-start(bf16[640,128]{1,0:T(8,128)(2,1)S(1)} %add_convert_fusion.1), channel_id=1, source_target_pairs={{0,2},{1,3},{2,0},{3,1},{4,6},{5,7},{6,4},{7,5},{8,10},{9,11},{10,... | collective-permute-start | bytes 491528 | tf_op jit(solution)/shard_map/ppermute | solution.py:317
  30.1 3.6 %collective-permute-done.10 = bf16[384,128]{1,0:T(8,128)(2,1)S(1)} collective-permute-done((bf16[384,128]{1,0:T(8,128)(2,1)S(1)}, bf16[384,128]{1,0:T(8,128)(2,1)S(1)}, u32[]{:S(2)}, u32[]{:S(2)}) %collective-permute-start.10) | collective-permute-done | bytes 98336 | tf_op jit(solution)/shard_map/ppermute | solution.py:317
  33.7 0.0 collective-permute-done.9
  33.7 0.0 collective-permute-done.6
  33.7 0.1 add_convert_fusion.2
  33.8 7.8 %collective-permute-done.8 = bf16[640,128]{1,0:T(8,128)(2,1)S(1)} collective-permute-done((bf16[640,128]{1,0:T(8,128)(2,1)S(1)}, bf16[640,128]{1,0:T(8,128)(2,1)S(1)}, u32[]{:S(2)}, u32[]{:S(2)}) %collective-permute-start.8) | collective-permute-done | bytes 163872 | tf_op jit(solution)/shard_map/ppermute | solution.py:317
  41.5 0.1 add_convert_fusion
  41.6 0.7 %pad_maximum_fusion = bf16[1024,128]{1,0:T(8,128)(2,1)} fusion(bf16[384,128]{1,0:T(8,128)(2,1)S(1)} %add_convert_fusion.2, bf16[640,128]{1,0:T(8,128)(2,1)S(1)} %add_convert_fusion), kind=kLoop, calls=%fused_computation.2 | loop fusion | flops 524288 | bytes 524288 | tf_op jit(solution)/shard_map/concatenate | solution.py:343
  (3 shorter events, 0.1 us)
Async XLA Ops:
  1.0 5.1 %collective-permute-start = (bf16[192,128]{1,0:T(8,128)(2,1)S(1)}, bf16[192,128]{1,0:T(8,128)(2,1)S(1)}, u32[]{:S(2)}, u32[]{:S(2)}) collective-permute-start(bf16[192,128]{1,0:T(8,128)(2,1)S(1)} %shard_map.83), channel_id=1, source_target_pairs={{0,16},{4,20},{8,24},{12,28},{16,0},{20,4},{24,8},{28,12},{1,17},{... | collective-permute-start | bytes 147464 | tf_op jit(solution)/shard_map/ppermute | solution.py:279
  4.1 6.1 %collective-permute-start.3 = (bf16[192,128]{1,0:T(8,128)(2,1)S(1)}, bf16[192,128]{1,0:T(8,128)(2,1)S(1)}, u32[]{:S(2)}, u32[]{:S(2)}) collective-permute-start(bf16[192,128]{1,0:T(8,128)(2,1)S(1)} %shard_map.83), channel_id=1, source_target_pairs={{0,24},{4,28},{8,16},{12,20},{16,8},{20,12},{24,0},{28,4},{1,25},{... | collective-permute-start | bytes 147464 | tf_op jit(solution)/shard_map/ppermute | solution.py:279
  5.5 4.1 %collective-permute-start.1 = (bf16[192,128]{1,0:T(8,128)(2,1)S(1)}, bf16[192,128]{1,0:T(8,128)(2,1)S(1)}, u32[]{:S(2)}, u32[]{:S(2)}) collective-permute-start(bf16[192,128]{1,0:T(8,128)(2,1)S(1)} %shard_map.83), channel_id=1, source_target_pairs={{0,8},{4,12},{8,0},{12,4},{16,24},{20,28},{24,16},{28,20},{1,9},{5... | collective-permute-start | bytes 147464 | tf_op jit(solution)/shard_map/ppermute | solution.py:279
  9.6 4.6 %collective-permute-start.2 = (bf16[384,128]{1,0:T(8,128)(2,1)S(1)}, bf16[384,128]{1,0:T(8,128)(2,1)S(1)}, u32[]{:S(2)}, u32[]{:S(2)}) collective-permute-start(bf16[384,128]{1,0:T(8,128)(2,1)S(1)} %constant_dynamic-update-slice_fusion), channel_id=1, source_target_pairs={{0,4},{4,0},{8,12},{12,8},{16,20},{20,16},{24,28},{28,24},{1,5},{5... | collective-permute-start | bytes 294920 | tf_op jit(solution)/shard_map/ppermute | solution.py:279
  9.7 2.5 %collective-permute-start.5 = (bf16[192,128]{1,0:T(8,128)(2,1)S(1)}, bf16[192,128]{1,0:T(8,128)(2,1)S(1)}, u32[]{:S(2)}, u32[]{:S(2)}) collective-permute-start(bf16[192,128]{1,0:T(8,128)(2,1)S(1)} %shard_map.83), channel_id=1, source_target_pairs={{0,4},{4,0},{8,12},{12,8},{16,20},{20,16},{24,28},{28,24},{1,5},{5... | collective-permute-start | bytes 147464 | tf_op jit(solution)/shard_map/ppermute | solution.py:279
  10.2 3.1 %collective-permute-start.4 = (bf16[192,128]{1,0:T(8,128)(2,1)S(1)}, bf16[192,128]{1,0:T(8,128)(2,1)S(1)}, u32[]{:S(2)}, u32[]{:S(2)}) collective-permute-start(bf16[192,128]{1,0:T(8,128)(2,1)S(1)} %collective-permute-done.3), channel_id=1, source_target_pairs={{0,4},{4,0},{8,12},{12,8},{16,20},{20,16},{24,28},{28,24},{1,5},{5... | collective-permute-start | bytes 147464 | tf_op jit(solution)/shard_map/ppermute | solution.py:279
  15.5 11.5 %collective-permute-start.7 = (bf16[640,128]{1,0:T(8,128)(2,1)S(1)}, bf16[640,128]{1,0:T(8,128)(2,1)S(1)}, u32[]{:S(2)}, u32[]{:S(2)}) collective-permute-start(bf16[640,128]{1,0:T(8,128)(2,1)S(1)} %get-tuple-element.39), channel_id=1, source_target_pairs={{0,1},{1,0},{2,3},{3,2},{4,5},{5,4},{6,7},{7,6},{8,9},{9,8},{10,11... | collective-permute-start | bytes 491528 | tf_op jit(solution)/shard_map/ppermute | solution.py:317
  20.2 13.5 %collective-permute-start.6 = (bf16[1024,128]{1,0:T(8,128)(2,1)S(1)}, bf16[1024,128]{1,0:T(8,128)(2,1)S(1)}, u32[]{:S(2)}, u32[]{:S(2)}) collective-permute-start(bf16[1024,128]{1,0:T(8,128)(2,1)S(1)} %get-tuple-element.37), channel_id=1, source_target_pairs={{0,1},{1,0},{2,3},{3,2},{4,5},{5,4},{6,7},{7,6},{8,9},{9,8},{10,11... | collective-permute-start | bytes 786440 | tf_op jit(solution)/shard_map/ppermute | solution.py:317
  21.1 12.6 %collective-permute-start.10 = (bf16[384,128]{1,0:T(8,128)(2,1)S(1)}, bf16[384,128]{1,0:T(8,128)(2,1)S(1)}, u32[]{:S(2)}, u32[]{:S(2)}) collective-permute-start(bf16[384,128]{1,0:T(8,128)(2,1)S(1)} %shard_map.89), channel_id=1, source_target_pairs={{0,3},{1,2},{2,1},{3,0},{4,7},{5,6},{6,5},{7,4},{8,11},{9,10},{10,... | collective-permute-start | bytes 294920 | tf_op jit(solution)/shard_map/ppermute | solution.py:317
  24.8 8.9 %collective-permute-start.9 = (bf16[384,128]{1,0:T(8,128)(2,1)S(1)}, bf16[384,128]{1,0:T(8,128)(2,1)S(1)}, u32[]{:S(2)}, u32[]{:S(2)}) collective-permute-start(bf16[384,128]{1,0:T(8,128)(2,1)S(1)} %get-tuple-element.40), channel_id=1, source_target_pairs={{0,2},{1,3},{2,0},{3,1},{4,6},{5,7},{6,4},{7,5},{8,10},{9,11},{10,... | collective-permute-start | bytes 294920 | tf_op jit(solution)/shard_map/ppermute | solution.py:317
  27.1 14.4 %collective-permute-start.8 = (bf16[640,128]{1,0:T(8,128)(2,1)S(1)}, bf16[640,128]{1,0:T(8,128)(2,1)S(1)}, u32[]{:S(2)}, u32[]{:S(2)}) collective-permute-start(bf16[640,128]{1,0:T(8,128)(2,1)S(1)} %add_convert_fusion.1), channel_id=1, source_target_pairs={{0,2},{1,3},{2,0},{3,1},{4,6},{5,7},{6,4},{7,5},{8,10},{9,11},{10,... | collective-permute-start | bytes 491528 | tf_op jit(solution)/shard_map/ppermute | solution.py:317

commit v5 on v4

--- a/solution.py
+++ b/solution.py
@@ -17,7 +17,7 @@
 DMA = pltpu.SemaphoreType.DMA
 GROUP = 8
 PARTS = 4
-RELAY_PARTS, ALL_PARTS = 5, 8
+RELAY_PARTS, ALL_PARTS = 10, 16
 
 
 def dot(a, b, a_dim, b_dim):
@@ -177,10 +177,10 @@
 
 def project(w_ref, first, att_ref, out_ref):
     rows = out_ref.shape[0]
-    tile = math.gcd(256, rows)
-    for start in range(0, rows, tile):
-        part = dot(w_ref[first + start : first + start + tile, :], att_ref[...], 1, 0)
-        out_ref[start : start + tile, :] = part.astype(out_ref.dtype)
+    for start in range(0, rows, 256):
+        stop = min(start + 256, rows)
+        part = dot(w_ref[first + start : first + stop, :], att_ref[...], 1, 0)
+        out_ref[start:stop, :] = part.astype(out_ref.dtype)
 
 
 def late_kernel(orders, anchors, retained, qh_ref, hide_ref, block_ref, top0, total0, summed0, w_ref, far_w,
@@ -203,11 +203,12 @@
     project(farther_w, farther_w.shape[0] - farther_ref.shape[0], att_ref, farther_ref)
 
 
-def later_kernel(att_ref, w_hbm, across_ref, near_ref, far_w, near_w, sems):
+def later_kernel(att_ref, w_hbm, across_ref, near_top_ref, near_low_ref, far_w, near_w, sems):
     copies = fetch(parts_of(w_hbm, 2, 0, far_w) + parts_of(w_hbm, 1, 0, near_w), sems)
     wait(copies)
     project(far_w, 0, att_ref, across_ref)
-    project(near_w, 0, att_ref, near_ref)
+    project(near_w, 0, att_ref, near_top_ref)
+    project(near_w, near_top_ref.shape[0], att_ref, near_low_ref)
 
 
 def own_chunk_kernel(att_ref, w_hbm, out_ref, w_ref, sems):
@@ -320,16 +321,17 @@
     farther = call(direct_kernel, (att, w_farther), direct, chunk_flops)
     far = send(far, 2)
     farther = send(farther, 3)
-    across, near = call(
+    across, near_top, near_low = call(
         later_kernel,
         (att, out_weight),
-        (relayed, chunk),
+        (relayed, relayed, direct),
         chunk_flops,
         in_specs=[VMEM, HBM],
         scratch=[pltpu.VMEM((relay_rows, features), BF16), pltpu.VMEM((chunk_rows, features), BF16), DMA((2 * PARTS,))],
     )
+    near_low = send(near_low, 1)
     across = send(add(across, relay), 2)
-    near = send(near, 1)
+    near_top = send(near_top, 1)
     own = call(
         own_chunk_kernel,
         (att, out_weight),
@@ -338,8 +340,8 @@
         in_specs=[VMEM, HBM],
         scratch=[pltpu.VMEM((chunk_rows, features), BF16), DMA((PARTS,))],
     )
-    top = add(own[:relay_rows], near[:relay_rows], across)
-    low = add(own[relay_rows:], near[relay_rows:], far, farther)
+    top = add(own[:relay_rows], near_top, across)
+    low = add(own[relay_rows:], near_low, far, farther)
     return jnp.concatenate([top, low], axis=0)
 
 

time: 42.6 us -> 43 us (level)
    ppermute x5 -> x6, starting transfers between devices: 8.81 us -> 9.26 us  [send(): return lax.ppermute(x, 'tp', [(i, i ^ mask) for i in range(tp)])]
    ppermute x5 -> x6, waiting for transfers between devices: 11.4 us -> 11.4 us  [send(): return lax.ppermute(x, 'tp', [(i, i ^ mask) for i in range(tp)])]
  transfers between devices with their start and end apart: 11 -> 12, of which waited for: 4 -> 5; matrix products, arithmetic and copies ran while one was open for 0% -> 0% of each run, Pallas kernels for 23% -> 22%
where the time goes in v5:
time: 43 us; the launch traced here: 42.7 us
  waiting for transfers between devices  15.4 us (36%)
  starting transfers between devices  14.5 us (34%)
  Pallas kernels  11.9 us (28%)
  other arithmetic  0.89 us (2%)
    pallas_call x8, Pallas kernels, call(): pl.pallas_call(kernel, out_shape=out_shape, in_specs=in_specs or [VMEM] *...  11.9 us
    ppermute x6, waiting for transfers between devices, send(): return lax.ppermute(x, 'tp', [(i, i ^ mask) for i in range(tp)])  11.4 us
    ppermute x6, starting transfers between devices, send(): return lax.ppermute(x, 'tp', [(i, i ^ mask) for i in range(tp)])  9.26 us
    ppermute x6, starting transfers between devices, exchange(): return lax.ppermute(held, 'ctx', [(i, i ^ mask) for i in range(slots)])  5.25 us
    ppermute x6, waiting for transfers between devices, exchange(): return lax.ppermute(held, 'ctx', [(i, i ^ mask) for i in range(slots)])  3.99 us
  transfers between devices with their start and end apart: 12, of which 5 were waited for; matrix products, arithmetic and copies ran while one was open for 0% of the time, Pallas kernels for 22%

profile of v5, /device:TPU:0, one launch (start us, length us, event | category | flops | bytes accessed | tf_op | source)
XLA Modules:
  0.0 42.7 jit_solution(11077551952995008990)
XLA Ops:
  0.0 1.0 %shard_map.83 = bf16[192,128]{1,0:T(8,128)(2,1)S(1)} custom-call(s32[8,32]{1,0:T(8,128)} %rows_hbm.1, bf16[128,128]{1,0:T(8,128)(2,1)} %bitcast.18, bf16[128,128]{1,0:T(8,128)(2,1)} %bitcast.20, bf16[64,128]{1,0:T(8,128)(2,1)} %bitcast.22, bf16[64,128]{1,0:T(8,128)(2,1)} %bitcast.23), custom_call_target="tpu_custom_call" | custom-call | flops 2097152 | bytes 99328 | tf_op jit(solution)/shard_map/pallas_call | solution.py:31
  1.0 3.1 %collective-permute-start = (bf16[192,128]{1,0:T(8,128)(2,1)S(1)}, bf16[192,128]{1,0:T(8,128)(2,1)S(1)}, u32[]{:S(2)}, u32[]{:S(2)}) collective-permute-start(bf16[192,128]{1,0:T(8,128)(2,1)S(1)} %shard_map.83), channel_id=1, source_target_pairs={{0,16},{4,20},{8,24},{12,28},{16,0},{20,4},{24,8},{28,12},{1,17},{... | collective-permute-start | bytes 147464 | tf_op jit(solution)/shard_map/ppermute | solution.py:280
  4.1 1.4 %collective-permute-start.3 = (bf16[192,128]{1,0:T(8,128)(2,1)S(1)}, bf16[192,128]{1,0:T(8,128)(2,1)S(1)}, u32[]{:S(2)}, u32[]{:S(2)}) collective-permute-start(bf16[192,128]{1,0:T(8,128)(2,1)S(1)} %shard_map.83), channel_id=1, source_target_pairs={{0,24},{4,28},{8,16},{12,20},{16,8},{20,12},{24,0},{28,4},{1,25},{... | collective-permute-start | bytes 147464 | tf_op jit(solution)/shard_map/ppermute | solution.py:280
  5.5 0.1 collective-permute-start.1
  5.6 0.5 %collective-permute-done = bf16[192,128]{1,0:T(8,128)(2,1)S(1)} collective-permute-done((bf16[192,128]{1,0:T(8,128)(2,1)S(1)}, bf16[192,128]{1,0:T(8,128)(2,1)S(1)}, u32[]{:S(2)}, u32[]{:S(2)}) %collective-permute-start) | collective-permute-done | bytes 49184 | tf_op jit(solution)/shard_map/ppermute | solution.py:280
  6.2 3.4 %collective-permute-done.1 = bf16[192,128]{1,0:T(8,128)(2,1)S(1)} collective-permute-done((bf16[192,128]{1,0:T(8,128)(2,1)S(1)}, bf16[192,128]{1,0:T(8,128)(2,1)S(1)}, u32[]{:S(2)}, u32[]{:S(2)}) %collective-permute-start.1) | collective-permute-done | bytes 49184 | tf_op jit(solution)/shard_map/ppermute | solution.py:280
  9.6 0.1 collective-permute-start.2
  9.7 0.5 %collective-permute-start.5 = (bf16[192,128]{1,0:T(8,128)(2,1)S(1)}, bf16[192,128]{1,0:T(8,128)(2,1)S(1)}, u32[]{:S(2)}, u32[]{:S(2)}) collective-permute-start(bf16[192,128]{1,0:T(8,128)(2,1)S(1)} %shard_map.83), channel_id=1, source_target_pairs={{0,4},{4,0},{8,12},{12,8},{16,20},{20,16},{24,28},{28,24},{1,5},{5... | collective-permute-start | bytes 147464 | tf_op jit(solution)/shard_map/ppermute | solution.py:280
  10.2 0.0 collective-permute-done.3
  10.2 0.1 collective-permute-start.4
  10.3 2.0 %shard_map.82 = (bf16[1024,128]{1,0:T(8,128)(2,1)S(1)}, f32[8,128]{1,0:T(8,128)S(1)}, bf16[1024,1024]{1,0:T(8,128)(2,1)S(1)}, bf16[384,1024]{1,0:T(8,128)(2,1)S(...) custom-call(s32[8]{0:T(128)} %blocks_hbm.1, bf16[1024,128]{1,0:T(8,128)(2,1)} %bitcast.17, ...), custom_call_target="tpu_custom_call" | custom-call | flops 67108864 | bytes 8716320 | tf_op jit(solution)/shard_map/pallas_call | solution.py:31
  12.2 0.0 collective-permute-done.5
  12.3 1.1 %shard_map.84 = (f32[1,1024]{1,0:T(1,128)S(1)}, f32[1,1024]{1,0:T(1,128)S(1)}, f32[128,1024]{1,0:T(8,128)S(1)}) custom-call(bf16[1024,128]{1,0:T(8,128)(2,1)S(1)} %get-tuple-element.24.qh_ref, f32[8,128]{1,0:T(8,128)S(1)} %get-tuple-element.25.hide_ref, bf16[1,192,128]{2,1,0:T(8,128)(2,1)S(1)} %bitcast.12, bf16[1,192,128]{2,1,0:T(8,128)(2,1)S(1)} %bitcast.16, ...), custom_call_target="tpu_custom_call" | custom-call | flops 150994944 | bytes 946176 | tf_op jit(solution)/shard_map/pallas_call | solution.py:31
  13.3 0.0 collective-permute-done.4
  13.3 0.9 %shard_map.85 = (f32[1,1024]{1,0:T(1,128)S(1)}, f32[1,1024]{1,0:T(1,128)S(1)}, f32[128,1024]{1,0:T(8,128)S(1)}) custom-call(bf16[1024,128]{1,0:T(8,128)(2,1)S(1)} %get-tuple-element.24.qh_ref, f32[8,128]{1,0:T(8,128)S(1)} %get-tuple-element.25.hide_ref, bf16[1,192,128]{2,1,0:T(8,128)(2,1)S(1)} %bitcast.15, bf16[2,192,128]{2,1,0:T(8,128)(2,1)S(1)} %bitcast.11, ...), custom_call_target="tpu_custom_call" | custom-call | flops 150994944 | bytes 946176 | tf_op jit(solution)/shard_map/pallas_call | solution.py:31
  14.3 0.0 collective-permute-done.2
  14.3 1.2 %shard_map.86 = (bf16[1024,128]{1,0:T(8,128)(2,1)S(1)}, bf16[640,128]{1,0:T(8,128)(2,1)S(1)}, bf16[384,128]{1,0:T(8,128)(2,1)S(1)}) custom-call(bf16[1024,128]{1,0:T(8,128)(2,1)S(1)} %get-tuple-element.24.qh_ref, f32[8,128]{1,0:T(8,128)S(1)} %get-tuple-element.25.hide_ref, bf16[2,192,128]{2,1,0:T(8,128)(2,1)S(1)} %bitcast.13, ...), custom_call_target="tpu_custom_call" | custom-call | flops 234881024 | bytes 3780608 | tf_op jit(solution)/shard_map/pallas_call | solution.py:31
  15.5 1.6 %collective-permute-start.7 = (bf16[640,128]{1,0:T(8,128)(2,1)S(1)}, bf16[640,128]{1,0:T(8,128)(2,1)S(1)}, u32[]{:S(2)}, u32[]{:S(2)}) collective-permute-start(bf16[640,128]{1,0:T(8,128)(2,1)S(1)} %get-tuple-element.40), channel_id=1, source_target_pairs={{0,1},{1,0},{2,3},{3,2},{4,5},{5,4},{6,7},{7,6},{8,9},{9,8},{10,11... | collective-permute-start | bytes 491528 | tf_op jit(solution)/shard_map/ppermute | solution.py:318
  17.2 3.0 %shard_map.88 = (bf16[640,128]{1,0:T(8,128)(2,1)S(1)}, bf16[640,128]{1,0:T(8,128)(2,1)S(1)}, bf16[384,128]{1,0:T(8,128)(2,1)S(1)}) custom-call(bf16[1024,128]{1,0:T(8,128)(2,1)S(1)} %get-tuple-element.37.att_ref, bf16[4096,1024]{1,0:T(8,128)(2,1)} %w_hbm.5), custom_call_target="tpu_custom_call" | custom-call | flops 268435456 | bytes 8650752 | tf_op jit(solution)/shard_map/pallas_call | solution.py:31
  20.2 0.5 %collective-permute-start.6 = (bf16[640,128]{1,0:T(8,128)(2,1)S(1)}, bf16[640,128]{1,0:T(8,128)(2,1)S(1)}, u32[]{:S(2)}, u32[]{:S(2)}) collective-permute-start(bf16[640,128]{1,0:T(8,128)(2,1)S(1)} %get-tuple-element.38), channel_id=1, source_target_pairs={{0,1},{1,0},{2,3},{3,2},{4,5},{5,4},{6,7},{7,6},{8,9},{9,8},{10,11... | collective-permute-start | bytes 491528 | tf_op jit(solution)/shard_map/ppermute | solution.py:318
  20.7 1.6 %collective-permute-start.9 = (bf16[384,128]{1,0:T(8,128)(2,1)S(1)}, bf16[384,128]{1,0:T(8,128)(2,1)S(1)}, u32[]{:S(2)}, u32[]{:S(2)}) collective-permute-start(bf16[384,128]{1,0:T(8,128)(2,1)S(1)} %get-tuple-element.41), channel_id=1, source_target_pairs={{0,1},{1,0},{2,3},{3,2},{4,5},{5,4},{6,7},{7,6},{8,9},{9,8},{10,11... | collective-permute-start | bytes 294920 | tf_op jit(solution)/shard_map/ppermute | solution.py:318
  22.3 0.4 shard_map.89
  22.7 2.5 %collective-permute-start.11 = (bf16[384,128]{1,0:T(8,128)(2,1)S(1)}, bf16[384,128]{1,0:T(8,128)(2,1)S(1)}, u32[]{:S(2)}, u32[]{:S(2)}) collective-permute-start(bf16[384,128]{1,0:T(8,128)(2,1)S(1)} %shard_map.89), channel_id=1, source_target_pairs={{0,3},{1,2},{2,1},{3,0},{4,7},{5,6},{6,5},{7,4},{8,11},{9,10},{10,... | collective-permute-start | bytes 294920 | tf_op jit(solution)/shard_map/ppermute | solution.py:318
  25.2 0.2 collective-permute-start.10
  25.4 2.3 %shard_map.87 = bf16[1024,128]{1,0:T(8,128)(2,1)S(1)} custom-call(bf16[1024,128]{1,0:T(8,128)(2,1)S(1)} %get-tuple-element.37.att_ref, bf16[4096,1024]{1,0:T(8,128)(2,1)} %w_hbm.5), custom_call_target="tpu_custom_call" | custom-call | flops 268435456 | bytes 8650752 | tf_op jit(solution)/shard_map/pallas_call | solution.py:31
  27.7 0.0 collective-permute-done.7
  27.7 2.8 %collective-permute-start.8 = (bf16[640,128]{1,0:T(8,128)(2,1)S(1)}, bf16[640,128]{1,0:T(8,128)(2,1)S(1)}, u32[]{:S(2)}, u32[]{:S(2)}) collective-permute-start(bf16[640,128]{1,0:T(8,128)(2,1)S(1)} %add_convert_fusion.1), channel_id=1, source_target_pairs={{0,2},{1,3},{2,0},{3,1},{4,6},{5,7},{6,4},{7,5},{8,10},{9,11},{10,... | collective-permute-start | bytes 491528 | tf_op jit(solution)/shard_map/ppermute | solution.py:318
  30.5 0.0 collective-permute-done.9
  30.5 3.2 %collective-permute-done.11 = bf16[384,128]{1,0:T(8,128)(2,1)S(1)} collective-permute-done((bf16[384,128]{1,0:T(8,128)(2,1)S(1)}, bf16[384,128]{1,0:T(8,128)(2,1)S(1)}, u32[]{:S(2)}, u32[]{:S(2)}) %collective-permute-start.11) | collective-permute-done | bytes 98336 | tf_op jit(solution)/shard_map/ppermute | solution.py:318
  33.7 5.2 %collective-permute-done.10 = bf16[384,128]{1,0:T(8,128)(2,1)S(1)} collective-permute-done((bf16[384,128]{1,0:T(8,128)(2,1)S(1)}, bf16[384,128]{1,0:T(8,128)(2,1)S(1)}, u32[]{:S(2)}, u32[]{:S(2)}) %collective-permute-start.10) | collective-permute-done | bytes 98336 | tf_op jit(solution)/shard_map/ppermute | solution.py:318
  38.9 0.1 add_convert_fusion.2
  39.0 0.0 collective-permute-done.6
  39.0 2.9 %collective-permute-done.8 = bf16[640,128]{1,0:T(8,128)(2,1)S(1)} collective-permute-done((bf16[640,128]{1,0:T(8,128)(2,1)S(1)}, bf16[640,128]{1,0:T(8,128)(2,1)S(1)}, u32[]{:S(2)}, u32[]{:S(2)}) %collective-permute-start.8) | collective-permute-done | bytes 163872 | tf_op jit(solution)/shard_map/ppermute | solution.py:318
  42.0 0.1 add_convert_fusion
  42.0 0.7 %pad_maximum_fusion = bf16[1024,128]{1,0:T(8,128)(2,1)} fusion(bf16[384,128]{1,0:T(8,128)(2,1)S(1)} %add_convert_fusion.2, bf16[640,128]{1,0:T(8,128)(2,1)S(1)} %add_convert_fusion), kind=kLoop, calls=%fused_computation.2 | loop fusion | flops 524288 | bytes 524288 | tf_op jit(solution)/shard_map/concatenate | solution.py:345
  (3 shorter events, 0.1 us)
Async XLA Ops:
  1.0 5.1 %collective-permute-start = (bf16[192,128]{1,0:T(8,128)(2,1)S(1)}, bf16[192,128]{1,0:T(8,128)(2,1)S(1)}, u32[]{:S(2)}, u32[]{:S(2)}) collective-permute-start(bf16[192,128]{1,0:T(8,128)(2,1)S(1)} %shard_map.83), channel_id=1, source_target_pairs={{0,16},{4,20},{8,24},{12,28},{16,0},{20,4},{24,8},{28,12},{1,17},{... | collective-permute-start | bytes 147464 | tf_op jit(solution)/shard_map/ppermute | solution.py:280
  4.1 6.1 %collective-permute-start.3 = (bf16[192,128]{1,0:T(8,128)(2,1)S(1)}, bf16[192,128]{1,0:T(8,128)(2,1)S(1)}, u32[]{:S(2)}, u32[]{:S(2)}) collective-permute-start(bf16[192,128]{1,0:T(8,128)(2,1)S(1)} %shard_map.83), channel_id=1, source_target_pairs={{0,24},{4,28},{8,16},{12,20},{16,8},{20,12},{24,0},{28,4},{1,25},{... | collective-permute-start | bytes 147464 | tf_op jit(solution)/shard_map/ppermute | solution.py:280
  5.5 4.1 %collective-permute-start.1 = (bf16[192,128]{1,0:T(8,128)(2,1)S(1)}, bf16[192,128]{1,0:T(8,128)(2,1)S(1)}, u32[]{:S(2)}, u32[]{:S(2)}) collective-permute-start(bf16[192,128]{1,0:T(8,128)(2,1)S(1)} %shard_map.83), channel_id=1, source_target_pairs={{0,8},{4,12},{8,0},{12,4},{16,24},{20,28},{24,16},{28,20},{1,9},{5... | collective-permute-start | bytes 147464 | tf_op jit(solution)/shard_map/ppermute | solution.py:280
  9.6 4.6 %collective-permute-start.2 = (bf16[384,128]{1,0:T(8,128)(2,1)S(1)}, bf16[384,128]{1,0:T(8,128)(2,1)S(1)}, u32[]{:S(2)}, u32[]{:S(2)}) collective-permute-start(bf16[384,128]{1,0:T(8,128)(2,1)S(1)} %constant_dynamic-update-slice_fusion), channel_id=1, source_target_pairs={{0,4},{4,0},{8,12},{12,8},{16,20},{20,16},{24,28},{28,24},{1,5},{5... | collective-permute-start | bytes 294920 | tf_op jit(solution)/shard_map/ppermute | solution.py:280
  9.7 2.5 %collective-permute-start.5 = (bf16[192,128]{1,0:T(8,128)(2,1)S(1)}, bf16[192,128]{1,0:T(8,128)(2,1)S(1)}, u32[]{:S(2)}, u32[]{:S(2)}) collective-permute-start(bf16[192,128]{1,0:T(8,128)(2,1)S(1)} %shard_map.83), channel_id=1, source_target_pairs={{0,4},{4,0},{8,12},{12,8},{16,20},{20,16},{24,28},{28,24},{1,5},{5... | collective-permute-start | bytes 147464 | tf_op jit(solution)/shard_map/ppermute | solution.py:280
  10.2 3.1 %collective-permute-start.4 = (bf16[192,128]{1,0:T(8,128)(2,1)S(1)}, bf16[192,128]{1,0:T(8,128)(2,1)S(1)}, u32[]{:S(2)}, u32[]{:S(2)}) collective-permute-start(bf16[192,128]{1,0:T(8,128)(2,1)S(1)} %collective-permute-done.3), channel_id=1, source_target_pairs={{0,4},{4,0},{8,12},{12,8},{16,20},{20,16},{24,28},{28,24},{1,5},{5... | collective-permute-start | bytes 147464 | tf_op jit(solution)/shard_map/ppermute | solution.py:280
  15.5 12.2 %collective-permute-start.7 = (bf16[640,128]{1,0:T(8,128)(2,1)S(1)}, bf16[640,128]{1,0:T(8,128)(2,1)S(1)}, u32[]{:S(2)}, u32[]{:S(2)}) collective-permute-start(bf16[640,128]{1,0:T(8,128)(2,1)S(1)} %get-tuple-element.40), channel_id=1, source_target_pairs={{0,1},{1,0},{2,3},{3,2},{4,5},{5,4},{6,7},{7,6},{8,9},{9,8},{10,11... | collective-permute-start | bytes 491528 | tf_op jit(solution)/shard_map/ppermute | solution.py:318
  20.2 18.8 %collective-permute-start.6 = (bf16[640,128]{1,0:T(8,128)(2,1)S(1)}, bf16[640,128]{1,0:T(8,128)(2,1)S(1)}, u32[]{:S(2)}, u32[]{:S(2)}) collective-permute-start(bf16[640,128]{1,0:T(8,128)(2,1)S(1)} %get-tuple-element.38), channel_id=1, source_target_pairs={{0,1},{1,0},{2,3},{3,2},{4,5},{5,4},{6,7},{7,6},{8,9},{9,8},{10,11... | collective-permute-start | bytes 491528 | tf_op jit(solution)/shard_map/ppermute | solution.py:318
  20.7 9.8 %collective-permute-start.9 = (bf16[384,128]{1,0:T(8,128)(2,1)S(1)}, bf16[384,128]{1,0:T(8,128)(2,1)S(1)}, u32[]{:S(2)}, u32[]{:S(2)}) collective-permute-start(bf16[384,128]{1,0:T(8,128)(2,1)S(1)} %get-tuple-element.41), channel_id=1, source_target_pairs={{0,1},{1,0},{2,3},{3,2},{4,5},{5,4},{6,7},{7,6},{8,9},{9,8},{10,11... | collective-permute-start | bytes 294920 | tf_op jit(solution)/shard_map/ppermute | solution.py:318
  22.7 11.0 %collective-permute-start.11 = (bf16[384,128]{1,0:T(8,128)(2,1)S(1)}, bf16[384,128]{1,0:T(8,128)(2,1)S(1)}, u32[]{:S(2)}, u32[]{:S(2)}) collective-permute-start(bf16[384,128]{1,0:T(8,128)(2,1)S(1)} %shard_map.89), channel_id=1, source_target_pairs={{0,3},{1,2},{2,1},{3,0},{4,7},{5,6},{6,5},{7,4},{8,11},{9,10},{10,... | collective-permute-start | bytes 294920 | tf_op jit(solution)/shard_map/ppermute | solution.py:318
  25.2 13.7 %collective-permute-start.10 = (bf16[384,128]{1,0:T(8,128)(2,1)S(1)}, bf16[384,128]{1,0:T(8,128)(2,1)S(1)}, u32[]{:S(2)}, u32[]{:S(2)}) collective-permute-start(bf16[384,128]{1,0:T(8,128)(2,1)S(1)} %get-tuple-element.42), channel_id=1, source_target_pairs={{0,2},{1,3},{2,0},{3,1},{4,6},{5,7},{6,4},{7,5},{8,10},{9,11},{10,... | collective-permute-start | bytes 294920 | tf_op jit(solution)/shard_map/ppermute | solution.py:318
  27.7 14.2 %collective-permute-start.8 = (bf16[640,128]{1,0:T(8,128)(2,1)S(1)}, bf16[640,128]{1,0:T(8,128)(2,1)S(1)}, u32[]{:S(2)}, u32[]{:S(2)}) collective-permute-start(bf16[640,128]{1,0:T(8,128)(2,1)S(1)} %add_convert_fusion.1), channel_id=1, source_target_pairs={{0,2},{1,3},{2,0},{3,1},{4,6},{5,7},{6,4},{7,5},{8,10},{9,11},{10,... | collective-permute-start | bytes 491528 | tf_op jit(solution)/shard_map/ppermute | solution.py:318

commit v6 on v5

--- a/solution.py
+++ b/solution.py
@@ -17,7 +17,7 @@
 DMA = pltpu.SemaphoreType.DMA
 GROUP = 8
 PARTS = 4
-RELAY_PARTS, ALL_PARTS = 10, 16
+RELAY_PARTS, ALL_PARTS = 12, 16
 
 
 def dot(a, b, a_dim, b_dim):
@@ -183,8 +183,8 @@
         out_ref[start:stop, :] = part.astype(out_ref.dtype)
 
 
-def late_kernel(orders, anchors, retained, qh_ref, hide_ref, block_ref, top0, total0, summed0, w_ref, far_w,
-                att_ref, first_ref, far_ref):
+def late_kernel(orders, anchors, retained, qh_ref, hide_ref, block_ref, top0, total0, summed0, w_ref,
+                att_ref, first_ref):
     tok_rows = hide_ref.shape[1]
     size = qh_ref.shape[1]
 
@@ -196,10 +196,10 @@
 
     fold_blocks(orders, anchors, retained, qh_ref, hide_ref, (block_ref,), (top0, total0, summed0), finish)
     project(w_ref, 0, att_ref, first_ref)
+
+
+def direct_kernel(att_ref, farther_w, far_w, far_ref, farther_ref):
     project(far_w, 0, att_ref, far_ref)
-
-
-def direct_kernel(att_ref, farther_w, farther_ref):
     project(farther_w, farther_w.shape[0] - farther_ref.shape[0], att_ref, farther_ref)
 
 
@@ -307,10 +307,10 @@
     other = exchange(1)
     state = attend(state, (across_chip(diagonal_order, 1), diagonal_partner), (side_order, held))
     late_order = across_chip(side_order, 1)
-    att, first, far = call(
+    att, first = call(
         functools.partial(late_kernel, (late_order,), anchors, retained),
-        (qh, hide, blocks(other), *state, w_farther, w_far),
-        (shape((features, tok_rows), BF16), relayed, direct),
+        (qh, hide, blocks(other), *state, w_farther),
+        (shape((features, tok_rows), BF16), relayed),
         fold_flops(len(late_order)) + chunk_flops // 2,
     )
 
@@ -318,7 +318,7 @@
         return lax.ppermute(x, "tp", [(i, i ^ mask) for i in range(tp)])
 
     relay = send(first, 1)
-    farther = call(direct_kernel, (att, w_farther), direct, chunk_flops)
+    far, farther = call(direct_kernel, (att, w_farther, w_far), (direct, direct), chunk_flops)
     far = send(far, 2)
     farther = send(farther, 3)
     across, near_top, near_low = call(

time: 43 us -> 42.4 us (0.986)
  starting transfers between devices: 14.5 us -> 13.6 us
    ppermute x6, starting transfers between devices: 9.26 us -> 8.37 us  [send(): return lax.ppermute(x, 'tp', [(i, i ^ mask) for i in range(tp)])]
  transfers between devices with their start and end apart: 12 -> 12, of which waited for: 5 -> 5; matrix products, arithmetic and copies ran while one was open for 0% -> 0% of each run, Pallas kernels for 22% -> 23%
where the time goes in v6:
time: 42.4 us; the launch traced here: 42.2 us
  waiting for transfers between devices  15.7 us (37%)
  starting transfers between devices  13.6 us (32%)
  Pallas kernels  11.8 us (28%)
  other arithmetic  0.9 us (2%)
    pallas_call x8, Pallas kernels, call(): pl.pallas_call(kernel, out_shape=out_shape, in_specs=in_specs or [VMEM] *...  11.8 us
    ppermute x6, waiting for transfers between devices, send(): return lax.ppermute(x, 'tp', [(i, i ^ mask) for i in range(tp)])  11.7 us
    ppermute x6, starting transfers between devices, send(): return lax.ppermute(x, 'tp', [(i, i ^ mask) for i in range(tp)])  8.37 us
    ppermute x6, starting transfers between devices, exchange(): return lax.ppermute(held, 'ctx', [(i, i ^ mask) for i in range(slots)])  5.25 us
    ppermute x6, waiting for transfers between devices, exchange(): return lax.ppermute(held, 'ctx', [(i, i ^ mask) for i in range(slots)])  3.99 us
  transfers between devices with their start and end apart: 12, of which 5 were waited for; matrix products, arithmetic and copies ran while one was open for 0% of the time, Pallas kernels for 23%

profile of v6, /device:TPU:0, one launch (start us, length us, event | category | flops | bytes accessed | tf_op | source)
XLA Modules:
  0.0 42.2 jit_solution(1913932040267367047)
XLA Ops:
  0.0 1.0 %shard_map.83 = bf16[192,128]{1,0:T(8,128)(2,1)S(1)} custom-call(s32[8,32]{1,0:T(8,128)} %rows_hbm.1, bf16[128,128]{1,0:T(8,128)(2,1)} %bitcast.18, bf16[128,128]{1,0:T(8,128)(2,1)} %bitcast.20, bf16[64,128]{1,0:T(8,128)(2,1)} %bitcast.22, bf16[64,128]{1,0:T(8,128)(2,1)} %bitcast.23), custom_call_target="tpu_custom_call" | custom-call | flops 2097152 | bytes 99328 | tf_op jit(solution)/shard_map/pallas_call | solution.py:31
  1.0 3.1 %collective-permute-start = (bf16[192,128]{1,0:T(8,128)(2,1)S(1)}, bf16[192,128]{1,0:T(8,128)(2,1)S(1)}, u32[]{:S(2)}, u32[]{:S(2)}) collective-permute-start(bf16[192,128]{1,0:T(8,128)(2,1)S(1)} %shard_map.83), channel_id=1, source_target_pairs={{0,16},{4,20},{8,24},{12,28},{16,0},{20,4},{24,8},{28,12},{1,17},{... | collective-permute-start | bytes 147464 | tf_op jit(solution)/shard_map/ppermute | solution.py:280
  4.1 1.4 %collective-permute-start.3 = (bf16[192,128]{1,0:T(8,128)(2,1)S(1)}, bf16[192,128]{1,0:T(8,128)(2,1)S(1)}, u32[]{:S(2)}, u32[]{:S(2)}) collective-permute-start(bf16[192,128]{1,0:T(8,128)(2,1)S(1)} %shard_map.83), channel_id=1, source_target_pairs={{0,24},{4,28},{8,16},{12,20},{16,8},{20,12},{24,0},{28,4},{1,25},{... | collective-permute-start | bytes 147464 | tf_op jit(solution)/shard_map/ppermute | solution.py:280
  5.5 0.1 collective-permute-start.1
  5.6 0.5 %collective-permute-done = bf16[192,128]{1,0:T(8,128)(2,1)S(1)} collective-permute-done((bf16[192,128]{1,0:T(8,128)(2,1)S(1)}, bf16[192,128]{1,0:T(8,128)(2,1)S(1)}, u32[]{:S(2)}, u32[]{:S(2)}) %collective-permute-start) | collective-permute-done | bytes 49184 | tf_op jit(solution)/shard_map/ppermute | solution.py:280
  6.2 3.4 %collective-permute-done.1 = bf16[192,128]{1,0:T(8,128)(2,1)S(1)} collective-permute-done((bf16[192,128]{1,0:T(8,128)(2,1)S(1)}, bf16[192,128]{1,0:T(8,128)(2,1)S(1)}, u32[]{:S(2)}, u32[]{:S(2)}) %collective-permute-start.1) | collective-permute-done | bytes 49184 | tf_op jit(solution)/shard_map/ppermute | solution.py:280
  9.6 0.1 collective-permute-start.2
  9.7 0.5 %collective-permute-start.5 = (bf16[192,128]{1,0:T(8,128)(2,1)S(1)}, bf16[192,128]{1,0:T(8,128)(2,1)S(1)}, u32[]{:S(2)}, u32[]{:S(2)}) collective-permute-start(bf16[192,128]{1,0:T(8,128)(2,1)S(1)} %shard_map.83), channel_id=1, source_target_pairs={{0,4},{4,0},{8,12},{12,8},{16,20},{20,16},{24,28},{28,24},{1,5},{5... | collective-permute-start | bytes 147464 | tf_op jit(solution)/shard_map/ppermute | solution.py:280
  10.2 0.0 collective-permute-done.3
  10.2 0.1 collective-permute-start.4
  10.3 1.9 %shard_map.82 = (bf16[1024,128]{1,0:T(8,128)(2,1)S(1)}, f32[8,128]{1,0:T(8,128)S(1)}, bf16[1024,1024]{1,0:T(8,128)(2,1)S(1)}, bf16[256,1024]{1,0:T(8,128)(2,1)S(...) custom-call(s32[8]{0:T(128)} %blocks_hbm.1, bf16[1024,128]{1,0:T(8,128)(2,1)} %bitcast.17, ...), custom_call_target="tpu_custom_call" | custom-call | flops 67108864 | bytes 8716320 | tf_op jit(solution)/shard_map/pallas_call | solution.py:31
  12.2 0.0 collective-permute-done.5
  12.2 1.1 %shard_map.84 = (f32[1,1024]{1,0:T(1,128)S(1)}, f32[1,1024]{1,0:T(1,128)S(1)}, f32[128,1024]{1,0:T(8,128)S(1)}) custom-call(bf16[1024,128]{1,0:T(8,128)(2,1)S(1)} %get-tuple-element.25.qh_ref, f32[8,128]{1,0:T(8,128)S(1)} %get-tuple-element.26.hide_ref, bf16[1,192,128]{2,1,0:T(8,128)(2,1)S(1)} %bitcast.12, bf16[1,192,128]{2,1,0:T(8,128)(2,1)S(1)} %bitcast.16, ...), custom_call_target="tpu_custom_call" | custom-call | flops 150994944 | bytes 946176 | tf_op jit(solution)/shard_map/pallas_call | solution.py:31
  13.3 0.0 collective-permute-done.4
  13.3 0.9 %shard_map.85 = (f32[1,1024]{1,0:T(1,128)S(1)}, f32[1,1024]{1,0:T(1,128)S(1)}, f32[128,1024]{1,0:T(8,128)S(1)}) custom-call(bf16[1024,128]{1,0:T(8,128)(2,1)S(1)} %get-tuple-element.25.qh_ref, f32[8,128]{1,0:T(8,128)S(1)} %get-tuple-element.26.hide_ref, bf16[1,192,128]{2,1,0:T(8,128)(2,1)S(1)} %bitcast.15, bf16[2,192,128]{2,1,0:T(8,128)(2,1)S(1)} %bitcast.11, ...), custom_call_target="tpu_custom_call" | custom-call | flops 150994944 | bytes 946176 | tf_op jit(solution)/shard_map/pallas_call | solution.py:31
  14.2 0.0 collective-permute-done.2
  14.2 1.1 %shard_map.86 = (bf16[1024,128]{1,0:T(8,128)(2,1)S(1)}, bf16[768,128]{1,0:T(8,128)(2,1)S(1)}) custom-call(bf16[1024,128]{1,0:T(8,128)(2,1)S(1)} %get-tuple-element.25.qh_ref, f32[8,128]{1,0:T(8,128)S(1)} %get-tuple-element.26.hide_ref, bf16[2,192,128]{2,1,0:T(8,128)(2,1)S(1)} %bitcast.13, f32[1,1024]{1,0:T(1,128)S(1)} %get-tuple-element.33.top0, ...), custom_call_target="tpu_custom_call" | custom-call | flops 234881024 | bytes 2994176 | tf_op jit(solution)/shard_map/pallas_call | solution.py:31
  15.3 1.6 %collective-permute-start.7 = (bf16[768,128]{1,0:T(8,128)(2,1)S(1)}, bf16[768,128]{1,0:T(8,128)(2,1)S(1)}, u32[]{:S(2)}, u32[]{:S(2)}) collective-permute-start(bf16[768,128]{1,0:T(8,128)(2,1)S(1)} %get-tuple-element.40), channel_id=1, source_target_pairs={{0,1},{1,0},{2,3},{3,2},{4,5},{5,4},{6,7},{7,6},{8,9},{9,8},{10,11... | collective-permute-start | bytes 589832 | tf_op jit(solution)/shard_map/ppermute | solution.py:318
  16.9 3.2 %shard_map.88 = (bf16[768,128]{1,0:T(8,128)(2,1)S(1)}, bf16[768,128]{1,0:T(8,128)(2,1)S(1)}, bf16[256,128]{1,0:T(8,128)(2,1)S(1)}) custom-call(bf16[1024,128]{1,0:T(8,128)(2,1)S(1)} %get-tuple-element.37.att_ref, bf16[4096,1024]{1,0:T(8,128)(2,1)} %w_hbm.5), custom_call_target="tpu_custom_call" | custom-call | flops 268435456 | bytes 8650752 | tf_op jit(solution)/shard_map/pallas_call | solution.py:31
  20.1 0.5 %collective-permute-start.6 = (bf16[768,128]{1,0:T(8,128)(2,1)S(1)}, bf16[768,128]{1,0:T(8,128)(2,1)S(1)}, u32[]{:S(2)}, u32[]{:S(2)}) collective-permute-start(bf16[768,128]{1,0:T(8,128)(2,1)S(1)} %get-tuple-element.38), channel_id=1, source_target_pairs={{0,1},{1,0},{2,3},{3,2},{4,5},{5,4},{6,7},{7,6},{8,9},{9,8},{10,11... | collective-permute-start | bytes 589832 | tf_op jit(solution)/shard_map/ppermute | solution.py:318
  20.6 1.6 %collective-permute-start.9 = (bf16[256,128]{1,0:T(8,128)(2,1)S(1)}, bf16[256,128]{1,0:T(8,128)(2,1)S(1)}, u32[]{:S(2)}, u32[]{:S(2)}) collective-permute-start(bf16[256,128]{1,0:T(8,128)(2,1)S(1)} %get-tuple-element.41), channel_id=1, source_target_pairs={{0,1},{1,0},{2,3},{3,2},{4,5},{5,4},{6,7},{7,6},{8,9},{9,8},{10,11... | collective-permute-start | bytes 196616 | tf_op jit(solution)/shard_map/ppermute | solution.py:318
  22.2 0.4 %shard_map.89 = (bf16[256,128]{1,0:T(8,128)(2,1)S(1)}, bf16[256,128]{1,0:T(8,128)(2,1)S(1)}) custom-call(bf16[1024,128]{1,0:T(8,128)(2,1)S(1)} %get-tuple-element.37.att_ref, bf16[1024,1024]{1,0:T(8,128)(2,1)S(1)} %get-tuple-element.36.w_ref.farther_w, bf16[256,1024]{1,0:T(8,128)(2,1)S(1)} %get-tuple-element.42.far_w), custom_call_target="tpu_custom_call" | custom-call | flops 268435456 | bytes 2883584 | tf_op jit(solution)/shard_map/pallas_call | solution.py:31
  22.6 2.6 %collective-permute-start.10 = (bf16[256,128]{1,0:T(8,128)(2,1)S(1)}, bf16[256,128]{1,0:T(8,128)(2,1)S(1)}, u32[]{:S(2)}, u32[]{:S(2)}) collective-permute-start(bf16[256,128]{1,0:T(8,128)(2,1)S(1)} %get-tuple-element.43), channel_id=1, source_target_pairs={{0,2},{1,3},{2,0},{3,1},{4,6},{5,7},{6,4},{7,5},{8,10},{9,11},{10,... | collective-permute-start | bytes 196616 | tf_op jit(solution)/shard_map/ppermute | solution.py:318
  25.3 0.2 collective-permute-start.11
  25.5 2.2 %shard_map.87 = bf16[1024,128]{1,0:T(8,128)(2,1)S(1)} custom-call(bf16[1024,128]{1,0:T(8,128)(2,1)S(1)} %get-tuple-element.37.att_ref, bf16[4096,1024]{1,0:T(8,128)(2,1)} %w_hbm.5), custom_call_target="tpu_custom_call" | custom-call | flops 268435456 | bytes 8650752 | tf_op jit(solution)/shard_map/pallas_call | solution.py:31
  27.8 0.0 collective-permute-done.7
  27.8 0.1 add_convert_fusion.1
  27.8 1.8 %collective-permute-start.8 = (bf16[768,128]{1,0:T(8,128)(2,1)S(1)}, bf16[768,128]{1,0:T(8,128)(2,1)S(1)}, u32[]{:S(2)}, u32[]{:S(2)}) collective-permute-start(bf16[768,128]{1,0:T(8,128)(2,1)S(1)} %add_convert_fusion.1), channel_id=1, source_target_pairs={{0,2},{1,3},{2,0},{3,1},{4,6},{5,7},{6,4},{7,5},{8,10},{9,11},{10,... | collective-permute-start | bytes 589832 | tf_op jit(solution)/shard_map/ppermute | solution.py:318
  29.6 0.3 collective-permute-done.9
  29.9 0.0 collective-permute-done.10
  30.0 4.3 %collective-permute-done.11 = bf16[256,128]{1,0:T(8,128)(2,1)S(1)} collective-permute-done((bf16[256,128]{1,0:T(8,128)(2,1)S(1)}, bf16[256,128]{1,0:T(8,128)(2,1)S(1)}, u32[]{:S(2)}, u32[]{:S(2)}) %collective-permute-start.11) | collective-permute-done | bytes 65568 | tf_op jit(solution)/shard_map/ppermute | solution.py:318
  34.3 0.0 collective-permute-done.6
  34.3 7.0 %collective-permute-done.8 = bf16[768,128]{1,0:T(8,128)(2,1)S(1)} collective-permute-done((bf16[768,128]{1,0:T(8,128)(2,1)S(1)}, bf16[768,128]{1,0:T(8,128)(2,1)S(1)}, u32[]{:S(2)}, u32[]{:S(2)}) %collective-permute-start.8) | collective-permute-done | bytes 196640 | tf_op jit(solution)/shard_map/ppermute | solution.py:318
  41.4 0.1 add_convert_fusion
  41.4 0.7 %pad_maximum_fusion = bf16[1024,128]{1,0:T(8,128)(2,1)} fusion(bf16[256,128]{1,0:T(8,128)(2,1)S(1)} %add_convert_fusion.2, bf16[768,128]{1,0:T(8,128)(2,1)S(1)} %add_convert_fusion), kind=kLoop, calls=%fused_computation.2 | loop fusion | flops 524288 | bytes 524288 | tf_op jit(solution)/shard_map/concatenate | solution.py:345
  (3 shorter events, 0.1 us)
Async XLA Ops:
  1.0 5.1 %collective-permute-start = (bf16[192,128]{1,0:T(8,128)(2,1)S(1)}, bf16[192,128]{1,0:T(8,128)(2,1)S(1)}, u32[]{:S(2)}, u32[]{:S(2)}) collective-permute-start(bf16[192,128]{1,0:T(8,128)(2,1)S(1)} %shard_map.83), channel_id=1, source_target_pairs={{0,16},{4,20},{8,24},{12,28},{16,0},{20,4},{24,8},{28,12},{1,17},{... | collective-permute-start | bytes 147464 | tf_op jit(solution)/shard_map/ppermute | solution.py:280
  4.1 6.1 %collective-permute-start.3 = (bf16[192,128]{1,0:T(8,128)(2,1)S(1)}, bf16[192,128]{1,0:T(8,128)(2,1)S(1)}, u32[]{:S(2)}, u32[]{:S(2)}) collective-permute-start(bf16[192,128]{1,0:T(8,128)(2,1)S(1)} %shard_map.83), channel_id=1, source_target_pairs={{0,24},{4,28},{8,16},{12,20},{16,8},{20,12},{24,0},{28,4},{1,25},{... | collective-permute-start | bytes 147464 | tf_op jit(solution)/shard_map/ppermute | solution.py:280
  5.5 4.1 %collective-permute-start.1 = (bf16[192,128]{1,0:T(8,128)(2,1)S(1)}, bf16[192,128]{1,0:T(8,128)(2,1)S(1)}, u32[]{:S(2)}, u32[]{:S(2)}) collective-permute-start(bf16[192,128]{1,0:T(8,128)(2,1)S(1)} %shard_map.83), channel_id=1, source_target_pairs={{0,8},{4,12},{8,0},{12,4},{16,24},{20,28},{24,16},{28,20},{1,9},{5... | collective-permute-start | bytes 147464 | tf_op jit(solution)/shard_map/ppermute | solution.py:280
  9.6 4.6 %collective-permute-start.2 = (bf16[384,128]{1,0:T(8,128)(2,1)S(1)}, bf16[384,128]{1,0:T(8,128)(2,1)S(1)}, u32[]{:S(2)}, u32[]{:S(2)}) collective-permute-start(bf16[384,128]{1,0:T(8,128)(2,1)S(1)} %constant_dynamic-update-slice_fusion), channel_id=1, source_target_pairs={{0,4},{4,0},{8,12},{12,8},{16,20},{20,16},{24,28},{28,24},{1,5},{5... | collective-permute-start | bytes 294920 | tf_op jit(solution)/shard_map/ppermute | solution.py:280
  9.7 2.5 %collective-permute-start.5 = (bf16[192,128]{1,0:T(8,128)(2,1)S(1)}, bf16[192,128]{1,0:T(8,128)(2,1)S(1)}, u32[]{:S(2)}, u32[]{:S(2)}) collective-permute-start(bf16[192,128]{1,0:T(8,128)(2,1)S(1)} %shard_map.83), channel_id=1, source_target_pairs={{0,4},{4,0},{8,12},{12,8},{16,20},{20,16},{24,28},{28,24},{1,5},{5... | collective-permute-start | bytes 147464 | tf_op jit(solution)/shard_map/ppermute | solution.py:280
  10.2 3.1 %collective-permute-start.4 = (bf16[192,128]{1,0:T(8,128)(2,1)S(1)}, bf16[192,128]{1,0:T(8,128)(2,1)S(1)}, u32[]{:S(2)}, u32[]{:S(2)}) collective-permute-start(bf16[192,128]{1,0:T(8,128)(2,1)S(1)} %collective-permute-done.3), channel_id=1, source_target_pairs={{0,4},{4,0},{8,12},{12,8},{16,20},{20,16},{24,28},{28,24},{1,5},{5... | collective-permute-start | bytes 147464 | tf_op jit(solution)/shard_map/ppermute | solution.py:280
  15.3 12.5 %collective-permute-start.7 = (bf16[768,128]{1,0:T(8,128)(2,1)S(1)}, bf16[768,128]{1,0:T(8,128)(2,1)S(1)}, u32[]{:S(2)}, u32[]{:S(2)}) collective-permute-start(bf16[768,128]{1,0:T(8,128)(2,1)S(1)} %get-tuple-element.40), channel_id=1, source_target_pairs={{0,1},{1,0},{2,3},{3,2},{4,5},{5,4},{6,7},{7,6},{8,9},{9,8},{10,11... | collective-permute-start | bytes 589832 | tf_op jit(solution)/shard_map/ppermute | solution.py:318
  20.1 14.2 %collective-permute-start.6 = (bf16[768,128]{1,0:T(8,128)(2,1)S(1)}, bf16[768,128]{1,0:T(8,128)(2,1)S(1)}, u32[]{:S(2)}, u32[]{:S(2)}) collective-permute-start(bf16[768,128]{1,0:T(8,128)(2,1)S(1)} %get-tuple-element.38), channel_id=1, source_target_pairs={{0,1},{1,0},{2,3},{3,2},{4,5},{5,4},{6,7},{7,6},{8,9},{9,8},{10,11... | collective-permute-start | bytes 589832 | tf_op jit(solution)/shard_map/ppermute | solution.py:318
  20.6 9.3 %collective-permute-start.9 = (bf16[256,128]{1,0:T(8,128)(2,1)S(1)}, bf16[256,128]{1,0:T(8,128)(2,1)S(1)}, u32[]{:S(2)}, u32[]{:S(2)}) collective-permute-start(bf16[256,128]{1,0:T(8,128)(2,1)S(1)} %get-tuple-element.41), channel_id=1, source_target_pairs={{0,1},{1,0},{2,3},{3,2},{4,5},{5,4},{6,7},{7,6},{8,9},{9,8},{10,11... | collective-permute-start | bytes 196616 | tf_op jit(solution)/shard_map/ppermute | solution.py:318
  22.6 7.3 %collective-permute-start.10 = (bf16[256,128]{1,0:T(8,128)(2,1)S(1)}, bf16[256,128]{1,0:T(8,128)(2,1)S(1)}, u32[]{:S(2)}, u32[]{:S(2)}) collective-permute-start(bf16[256,128]{1,0:T(8,128)(2,1)S(1)} %get-tuple-element.43), channel_id=1, source_target_pairs={{0,2},{1,3},{2,0},{3,1},{4,6},{5,7},{6,4},{7,5},{8,10},{9,11},{10,... | collective-permute-start | bytes 196616 | tf_op jit(solution)/shard_map/ppermute | solution.py:318
  25.3 9.0 %collective-permute-start.11 = (bf16[256,128]{1,0:T(8,128)(2,1)S(1)}, bf16[256,128]{1,0:T(8,128)(2,1)S(1)}, u32[]{:S(2)}, u32[]{:S(2)}) collective-permute-start(bf16[256,128]{1,0:T(8,128)(2,1)S(1)} %get-tuple-element.44), channel_id=1, source_target_pairs={{0,3},{1,2},{2,1},{3,0},{4,7},{5,6},{6,5},{7,4},{8,11},{9,10},{10,... | collective-permute-start | bytes 196616 | tf_op jit(solution)/shard_map/ppermute | solution.py:318
  27.8 13.5 %collective-permute-start.8 = (bf16[768,128]{1,0:T(8,128)(2,1)S(1)}, bf16[768,128]{1,0:T(8,128)(2,1)S(1)}, u32[]{:S(2)}, u32[]{:S(2)}) collective-permute-start(bf16[768,128]{1,0:T(8,128)(2,1)S(1)} %add_convert_fusion.1), channel_id=1, source_target_pairs={{0,2},{1,3},{2,0},{3,1},{4,6},{5,7},{6,4},{7,5},{8,10},{9,11},{10,... | collective-permute-start | bytes 589832 | tf_op jit(solution)/shard_map/ppermute | solution.py:318

commit v7 on v6

--- a/solution.py
+++ b/solution.py
@@ -18,6 +18,7 @@
 GROUP = 8
 PARTS = 4
 RELAY_PARTS, ALL_PARTS = 12, 16
+NEAR_PARTS = 8
 
 
 def dot(a, b, a_dim, b_dim):
@@ -236,6 +237,8 @@
     weights = lambda n: shape((n, features), BF16)
     relay_rows = chunk_rows * RELAY_PARTS // ALL_PARTS
     relayed = shape((relay_rows, tok_rows), BF16)
+    near_first = shape((chunk_rows * NEAR_PARTS // ALL_PARTS, tok_rows), BF16)
+    near_rest = shape((chunk_rows - near_first.shape[0], tok_rows), BF16)
     direct = shape((chunk_rows - relay_rows, tok_rows), BF16)
     chunk_flops = 2 * chunk_rows * tok_rows * features
     block = call(
@@ -324,7 +327,7 @@
     across, near_top, near_low = call(
         later_kernel,
         (att, out_weight),
-        (relayed, relayed, direct),
+        (relayed, near_first, near_rest),
         chunk_flops,
         in_specs=[VMEM, HBM],
         scratch=[pltpu.VMEM((relay_rows, features), BF16), pltpu.VMEM((chunk_rows, features), BF16), DMA((2 * PARTS,))],
@@ -340,8 +343,9 @@
         in_specs=[VMEM, HBM],
         scratch=[pltpu.VMEM((chunk_rows, features), BF16), DMA((PARTS,))],
     )
-    top = add(own[:relay_rows], near_top, across)
-    low = add(own[relay_rows:], near_low, far, farther)
+    near = jnp.concatenate([near_top, near_low], axis=0)
+    top = add(own[:relay_rows], near[:relay_rows], across)
+    low = add(own[relay_rows:], near[relay_rows:], far, farther)
     return jnp.concatenate([top, low], axis=0)
 
 

time: 42.4 us -> 42.4 us (level)
  transfers between devices with their start and end apart: 12 -> 12, of which waited for: 5 -> 4; matrix products, arithmetic and copies ran while one was open for 0% -> 0% of each run, Pallas kernels for 23% -> 23%
where the time goes in v7:
time: 42.4 us; the launch traced here: 42.2 us
  waiting for transfers between devices  15.7 us (37%)
  starting transfers between devices  13.6 us (32%)
  Pallas kernels  11.8 us (28%)
  other arithmetic  0.9 us (2%)
    pallas_call x8, Pallas kernels, call(): pl.pallas_call(kernel, out_shape=out_shape, in_specs=in_specs or [VMEM] *...  11.8 us
    ppermute x6, waiting for transfers between devices, send(): return lax.ppermute(x, 'tp', [(i, i ^ mask) for i in range(tp)])  11.7 us
    ppermute x6, starting transfers between devices, send(): return lax.ppermute(x, 'tp', [(i, i ^ mask) for i in range(tp)])  8.37 us
    ppermute x6, starting transfers between devices, exchange(): return lax.ppermute(held, 'ctx', [(i, i ^ mask) for i in range(slots)])  5.25 us
    ppermute x6, waiting for transfers between devices, exchange(): return lax.ppermute(held, 'ctx', [(i, i ^ mask) for i in range(slots)])  3.99 us
  transfers between devices with their start and end apart: 12, of which 4 were waited for; matrix products, arithmetic and copies ran while one was open for 0% of the time, Pallas kernels for 23%

profile of v7, /device:TPU:0, one launch (start us, length us, event | category | flops | bytes accessed | tf_op | source)
XLA Modules:
  0.0 42.2 jit_solution(8311819926613196033)
XLA Ops:
  0.0 1.0 %shard_map.83 = bf16[192,128]{1,0:T(8,128)(2,1)S(1)} custom-call(s32[8,32]{1,0:T(8,128)} %rows_hbm.1, bf16[128,128]{1,0:T(8,128)(2,1)} %bitcast.18, bf16[128,128]{1,0:T(8,128)(2,1)} %bitcast.20, bf16[64,128]{1,0:T(8,128)(2,1)} %bitcast.22, bf16[64,128]{1,0:T(8,128)(2,1)} %bitcast.23), custom_call_target="tpu_custom_call" | custom-call | flops 2097152 | bytes 99328 | tf_op jit(solution)/shard_map/pallas_call | solution.py:32
  1.0 3.1 %collective-permute-start = (bf16[192,128]{1,0:T(8,128)(2,1)S(1)}, bf16[192,128]{1,0:T(8,128)(2,1)S(1)}, u32[]{:S(2)}, u32[]{:S(2)}) collective-permute-start(bf16[192,128]{1,0:T(8,128)(2,1)S(1)} %shard_map.83), channel_id=1, source_target_pairs={{0,16},{4,20},{8,24},{12,28},{16,0},{20,4},{24,8},{28,12},{1,17},{... | collective-permute-start | bytes 147464 | tf_op jit(solution)/shard_map/ppermute | solution.py:283
  4.1 1.4 %collective-permute-start.3 = (bf16[192,128]{1,0:T(8,128)(2,1)S(1)}, bf16[192,128]{1,0:T(8,128)(2,1)S(1)}, u32[]{:S(2)}, u32[]{:S(2)}) collective-permute-start(bf16[192,128]{1,0:T(8,128)(2,1)S(1)} %shard_map.83), channel_id=1, source_target_pairs={{0,24},{4,28},{8,16},{12,20},{16,8},{20,12},{24,0},{28,4},{1,25},{... | collective-permute-start | bytes 147464 | tf_op jit(solution)/shard_map/ppermute | solution.py:283
  5.5 0.1 collective-permute-start.1
  5.6 0.5 %collective-permute-done = bf16[192,128]{1,0:T(8,128)(2,1)S(1)} collective-permute-done((bf16[192,128]{1,0:T(8,128)(2,1)S(1)}, bf16[192,128]{1,0:T(8,128)(2,1)S(1)}, u32[]{:S(2)}, u32[]{:S(2)}) %collective-permute-start) | collective-permute-done | bytes 49184 | tf_op jit(solution)/shard_map/ppermute | solution.py:283
  6.2 3.4 %collective-permute-done.1 = bf16[192,128]{1,0:T(8,128)(2,1)S(1)} collective-permute-done((bf16[192,128]{1,0:T(8,128)(2,1)S(1)}, bf16[192,128]{1,0:T(8,128)(2,1)S(1)}, u32[]{:S(2)}, u32[]{:S(2)}) %collective-permute-start.1) | collective-permute-done | bytes 49184 | tf_op jit(solution)/shard_map/ppermute | solution.py:283
  9.6 0.1 collective-permute-start.2
  9.7 0.5 %collective-permute-start.5 = (bf16[192,128]{1,0:T(8,128)(2,1)S(1)}, bf16[192,128]{1,0:T(8,128)(2,1)S(1)}, u32[]{:S(2)}, u32[]{:S(2)}) collective-permute-start(bf16[192,128]{1,0:T(8,128)(2,1)S(1)} %shard_map.83), channel_id=1, source_target_pairs={{0,4},{4,0},{8,12},{12,8},{16,20},{20,16},{24,28},{28,24},{1,5},{5... | collective-permute-start | bytes 147464 | tf_op jit(solution)/shard_map/ppermute | solution.py:283
  10.2 0.0 collective-permute-done.3
  10.2 0.1 collective-permute-start.4
  10.3 1.9 %shard_map.82 = (bf16[1024,128]{1,0:T(8,128)(2,1)S(1)}, f32[8,128]{1,0:T(8,128)S(1)}, bf16[1024,1024]{1,0:T(8,128)(2,1)S(1)}, bf16[256,1024]{1,0:T(8,128)(2,1)S(...) custom-call(s32[8]{0:T(128)} %blocks_hbm.1, bf16[1024,128]{1,0:T(8,128)(2,1)} %bitcast.17, ...), custom_call_target="tpu_custom_call" | custom-call | flops 67108864 | bytes 8716320 | tf_op jit(solution)/shard_map/pallas_call | solution.py:32
  12.2 0.0 collective-permute-done.5
  12.2 1.1 %shard_map.84 = (f32[1,1024]{1,0:T(1,128)S(1)}, f32[1,1024]{1,0:T(1,128)S(1)}, f32[128,1024]{1,0:T(8,128)S(1)}) custom-call(bf16[1024,128]{1,0:T(8,128)(2,1)S(1)} %get-tuple-element.25.qh_ref, f32[8,128]{1,0:T(8,128)S(1)} %get-tuple-element.26.hide_ref, bf16[1,192,128]{2,1,0:T(8,128)(2,1)S(1)} %bitcast.12, bf16[1,192,128]{2,1,0:T(8,128)(2,1)S(1)} %bitcast.16, ...), custom_call_target="tpu_custom_call" | custom-call | flops 150994944 | bytes 946176 | tf_op jit(solution)/shard_map/pallas_call | solution.py:32
  13.3 0.0 collective-permute-done.4
  13.3 0.9 %shard_map.85 = (f32[1,1024]{1,0:T(1,128)S(1)}, f32[1,1024]{1,0:T(1,128)S(1)}, f32[128,1024]{1,0:T(8,128)S(1)}) custom-call(bf16[1024,128]{1,0:T(8,128)(2,1)S(1)} %get-tuple-element.25.qh_ref, f32[8,128]{1,0:T(8,128)S(1)} %get-tuple-element.26.hide_ref, bf16[1,192,128]{2,1,0:T(8,128)(2,1)S(1)} %bitcast.15, bf16[2,192,128]{2,1,0:T(8,128)(2,1)S(1)} %bitcast.11, ...), custom_call_target="tpu_custom_call" | custom-call | flops 150994944 | bytes 946176 | tf_op jit(solution)/shard_map/pallas_call | solution.py:32
  14.2 0.0 collective-permute-done.2
  14.2 1.1 %shard_map.86 = (bf16[1024,128]{1,0:T(8,128)(2,1)S(1)}, bf16[768,128]{1,0:T(8,128)(2,1)S(1)}) custom-call(bf16[1024,128]{1,0:T(8,128)(2,1)S(1)} %get-tuple-element.25.qh_ref, f32[8,128]{1,0:T(8,128)S(1)} %get-tuple-element.26.hide_ref, bf16[2,192,128]{2,1,0:T(8,128)(2,1)S(1)} %bitcast.13, f32[1,1024]{1,0:T(1,128)S(1)} %get-tuple-element.33.top0, ...), custom_call_target="tpu_custom_call" | custom-call | flops 234881024 | bytes 2994176 | tf_op jit(solution)/shard_map/pallas_call | solution.py:32
  15.3 1.6 %collective-permute-start.8 = (bf16[768,128]{1,0:T(8,128)(2,1)S(1)}, bf16[768,128]{1,0:T(8,128)(2,1)S(1)}, u32[]{:S(2)}, u32[]{:S(2)}) collective-permute-start(bf16[768,128]{1,0:T(8,128)(2,1)S(1)} %get-tuple-element.41), channel_id=1, source_target_pairs={{0,1},{1,0},{2,3},{3,2},{4,5},{5,4},{6,7},{7,6},{8,9},{9,8},{10,11... | collective-permute-start | bytes 589832 | tf_op jit(solution)/shard_map/ppermute | solution.py:321
  16.9 3.2 %shard_map.88 = (bf16[768,128]{1,0:T(8,128)(2,1)S(1)}, bf16[512,128]{1,0:T(8,128)(2,1)S(1)}, bf16[512,128]{1,0:T(8,128)(2,1)S(1)}) custom-call(bf16[1024,128]{1,0:T(8,128)(2,1)S(1)} %get-tuple-element.37.att_ref, bf16[4096,1024]{1,0:T(8,128)(2,1)} %w_hbm.5), custom_call_target="tpu_custom_call" | custom-call | flops 268435456 | bytes 8650752 | tf_op jit(solution)/shard_map/pallas_call | solution.py:32
  20.1 0.5 %collective-permute-start.6 = (bf16[512,128]{1,0:T(8,128)(2,1)S(1)}, bf16[512,128]{1,0:T(8,128)(2,1)S(1)}, u32[]{:S(2)}, u32[]{:S(2)}) collective-permute-start(bf16[512,128]{1,0:T(8,128)(2,1)S(1)} %get-tuple-element.38), channel_id=1, source_target_pairs={{0,1},{1,0},{2,3},{3,2},{4,5},{5,4},{6,7},{7,6},{8,9},{9,8},{10,11... | collective-permute-start | bytes 393224 | tf_op jit(solution)/shard_map/ppermute | solution.py:321
  20.6 1.6 %collective-permute-start.7 = (bf16[512,128]{1,0:T(8,128)(2,1)S(1)}, bf16[512,128]{1,0:T(8,128)(2,1)S(1)}, u32[]{:S(2)}, u32[]{:S(2)}) collective-permute-start(bf16[512,128]{1,0:T(8,128)(2,1)S(1)} %get-tuple-element.39), channel_id=1, source_target_pairs={{0,1},{1,0},{2,3},{3,2},{4,5},{5,4},{6,7},{7,6},{8,9},{9,8},{10,11... | collective-permute-start | bytes 393224 | tf_op jit(solution)/shard_map/ppermute | solution.py:321
  22.2 0.4 %shard_map.89 = (bf16[256,128]{1,0:T(8,128)(2,1)S(1)}, bf16[256,128]{1,0:T(8,128)(2,1)S(1)}) custom-call(bf16[1024,128]{1,0:T(8,128)(2,1)S(1)} %get-tuple-element.37.att_ref, bf16[1024,1024]{1,0:T(8,128)(2,1)S(1)} %get-tuple-element.36.w_ref.farther_w, bf16[256,1024]{1,0:T(8,128)(2,1)S(1)} %get-tuple-element.42.far_w), custom_call_target="tpu_custom_call" | custom-call | flops 268435456 | bytes 2883584 | tf_op jit(solution)/shard_map/pallas_call | solution.py:32
  22.6 2.6 %collective-permute-start.10 = (bf16[256,128]{1,0:T(8,128)(2,1)S(1)}, bf16[256,128]{1,0:T(8,128)(2,1)S(1)}, u32[]{:S(2)}, u32[]{:S(2)}) collective-permute-start(bf16[256,128]{1,0:T(8,128)(2,1)S(1)} %get-tuple-element.43), channel_id=1, source_target_pairs={{0,2},{1,3},{2,0},{3,1},{4,6},{5,7},{6,4},{7,5},{8,10},{9,11},{10,... | collective-permute-start | bytes 196616 | tf_op jit(solution)/shard_map/ppermute | solution.py:321
  25.3 0.2 collective-permute-start.11
  25.5 2.2 %shard_map.87 = bf16[1024,128]{1,0:T(8,128)(2,1)S(1)} custom-call(bf16[1024,128]{1,0:T(8,128)(2,1)S(1)} %get-tuple-element.37.att_ref, bf16[4096,1024]{1,0:T(8,128)(2,1)} %w_hbm.5), custom_call_target="tpu_custom_call" | custom-call | flops 268435456 | bytes 8650752 | tf_op jit(solution)/shard_map/pallas_call | solution.py:32
  27.8 0.0 collective-permute-done.8
  27.8 0.1 add_convert_fusion.1
  27.8 1.8 %collective-permute-start.9 = (bf16[768,128]{1,0:T(8,128)(2,1)S(1)}, bf16[768,128]{1,0:T(8,128)(2,1)S(1)}, u32[]{:S(2)}, u32[]{:S(2)}) collective-permute-start(bf16[768,128]{1,0:T(8,128)(2,1)S(1)} %add_convert_fusion.1), channel_id=1, source_target_pairs={{0,2},{1,3},{2,0},{3,1},{4,6},{5,7},{6,4},{7,5},{8,10},{9,11},{10,... | collective-permute-start | bytes 589832 | tf_op jit(solution)/shard_map/ppermute | solution.py:321
  29.6 0.0 collective-permute-done.10
  29.6 4.7 %collective-permute-done.11 = bf16[256,128]{1,0:T(8,128)(2,1)S(1)} collective-permute-done((bf16[256,128]{1,0:T(8,128)(2,1)S(1)}, bf16[256,128]{1,0:T(8,128)(2,1)S(1)}, u32[]{:S(2)}, u32[]{:S(2)}) %collective-permute-start.11) | collective-permute-done | bytes 65568 | tf_op jit(solution)/shard_map/ppermute | solution.py:321
  34.3 0.0 collective-permute-done.7
  34.3 0.0 collective-permute-done.6
  34.3 7.0 %collective-permute-done.9 = bf16[768,128]{1,0:T(8,128)(2,1)S(1)} collective-permute-done((bf16[768,128]{1,0:T(8,128)(2,1)S(1)}, bf16[768,128]{1,0:T(8,128)(2,1)S(1)}, u32[]{:S(2)}, u32[]{:S(2)}) %collective-permute-start.9) | collective-permute-done | bytes 196640 | tf_op jit(solution)/shard_map/ppermute | solution.py:321
  41.4 0.1 add_convert_fusion
  41.4 0.7 %pad_maximum_fusion = bf16[1024,128]{1,0:T(8,128)(2,1)} fusion(bf16[256,128]{1,0:T(8,128)(2,1)S(1)} %add_convert_fusion.2, bf16[768,128]{1,0:T(8,128)(2,1)S(1)} %add_convert_fusion), kind=kLoop, calls=%fused_computation.2 | loop fusion | flops 524288 | bytes 524288 | tf_op jit(solution)/shard_map/concatenate | solution.py:349
  (3 shorter events, 0.1 us)
Async XLA Ops:
  1.0 5.1 %collective-permute-start = (bf16[192,128]{1,0:T(8,128)(2,1)S(1)}, bf16[192,128]{1,0:T(8,128)(2,1)S(1)}, u32[]{:S(2)}, u32[]{:S(2)}) collective-permute-start(bf16[192,128]{1,0:T(8,128)(2,1)S(1)} %shard_map.83), channel_id=1, source_target_pairs={{0,16},{4,20},{8,24},{12,28},{16,0},{20,4},{24,8},{28,12},{1,17},{... | collective-permute-start | bytes 147464 | tf_op jit(solution)/shard_map/ppermute | solution.py:283
  4.1 6.1 %collective-permute-start.3 = (bf16[192,128]{1,0:T(8,128)(2,1)S(1)}, bf16[192,128]{1,0:T(8,128)(2,1)S(1)}, u32[]{:S(2)}, u32[]{:S(2)}) collective-permute-start(bf16[192,128]{1,0:T(8,128)(2,1)S(1)} %shard_map.83), channel_id=1, source_target_pairs={{0,24},{4,28},{8,16},{12,20},{16,8},{20,12},{24,0},{28,4},{1,25},{... | collective-permute-start | bytes 147464 | tf_op jit(solution)/shard_map/ppermute | solution.py:283
  5.5 4.1 %collective-permute-start.1 = (bf16[192,128]{1,0:T(8,128)(2,1)S(1)}, bf16[192,128]{1,0:T(8,128)(2,1)S(1)}, u32[]{:S(2)}, u32[]{:S(2)}) collective-permute-start(bf16[192,128]{1,0:T(8,128)(2,1)S(1)} %shard_map.83), channel_id=1, source_target_pairs={{0,8},{4,12},{8,0},{12,4},{16,24},{20,28},{24,16},{28,20},{1,9},{5... | collective-permute-start | bytes 147464 | tf_op jit(solution)/shard_map/ppermute | solution.py:283
  9.6 4.6 %collective-permute-start.2 = (bf16[384,128]{1,0:T(8,128)(2,1)S(1)}, bf16[384,128]{1,0:T(8,128)(2,1)S(1)}, u32[]{:S(2)}, u32[]{:S(2)}) collective-permute-start(bf16[384,128]{1,0:T(8,128)(2,1)S(1)} %constant_dynamic-update-slice_fusion), channel_id=1, source_target_pairs={{0,4},{4,0},{8,12},{12,8},{16,20},{20,16},{24,28},{28,24},{1,5},{5... | collective-permute-start | bytes 294920 | tf_op jit(solution)/shard_map/ppermute | solution.py:283
  9.7 2.5 %collective-permute-start.5 = (bf16[192,128]{1,0:T(8,128)(2,1)S(1)}, bf16[192,128]{1,0:T(8,128)(2,1)S(1)}, u32[]{:S(2)}, u32[]{:S(2)}) collective-permute-start(bf16[192,128]{1,0:T(8,128)(2,1)S(1)} %shard_map.83), channel_id=1, source_target_pairs={{0,4},{4,0},{8,12},{12,8},{16,20},{20,16},{24,28},{28,24},{1,5},{5... | collective-permute-start | bytes 147464 | tf_op jit(solution)/shard_map/ppermute | solution.py:283
  10.2 3.1 %collective-permute-start.4 = (bf16[192,128]{1,0:T(8,128)(2,1)S(1)}, bf16[192,128]{1,0:T(8,128)(2,1)S(1)}, u32[]{:S(2)}, u32[]{:S(2)}) collective-permute-start(bf16[192,128]{1,0:T(8,128)(2,1)S(1)} %collective-permute-done.3), channel_id=1, source_target_pairs={{0,4},{4,0},{8,12},{12,8},{16,20},{20,16},{24,28},{28,24},{1,5},{5... | collective-permute-start | bytes 147464 | tf_op jit(solution)/shard_map/ppermute | solution.py:283
  15.3 12.5 %collective-permute-start.8 = (bf16[768,128]{1,0:T(8,128)(2,1)S(1)}, bf16[768,128]{1,0:T(8,128)(2,1)S(1)}, u32[]{:S(2)}, u32[]{:S(2)}) collective-permute-start(bf16[768,128]{1,0:T(8,128)(2,1)S(1)} %get-tuple-element.41), channel_id=1, source_target_pairs={{0,1},{1,0},{2,3},{3,2},{4,5},{5,4},{6,7},{7,6},{8,9},{9,8},{10,11... | collective-permute-start | bytes 589832 | tf_op jit(solution)/shard_map/ppermute | solution.py:321
  20.1 14.2 %collective-permute-start.6 = (bf16[512,128]{1,0:T(8,128)(2,1)S(1)}, bf16[512,128]{1,0:T(8,128)(2,1)S(1)}, u32[]{:S(2)}, u32[]{:S(2)}) collective-permute-start(bf16[512,128]{1,0:T(8,128)(2,1)S(1)} %get-tuple-element.38), channel_id=1, source_target_pairs={{0,1},{1,0},{2,3},{3,2},{4,5},{5,4},{6,7},{7,6},{8,9},{9,8},{10,11... | collective-permute-start | bytes 393224 | tf_op jit(solution)/shard_map/ppermute | solution.py:321
  20.6 13.7 %collective-permute-start.7 = (bf16[512,128]{1,0:T(8,128)(2,1)S(1)}, bf16[512,128]{1,0:T(8,128)(2,1)S(1)}, u32[]{:S(2)}, u32[]{:S(2)}) collective-permute-start(bf16[512,128]{1,0:T(8,128)(2,1)S(1)} %get-tuple-element.39), channel_id=1, source_target_pairs={{0,1},{1,0},{2,3},{3,2},{4,5},{5,4},{6,7},{7,6},{8,9},{9,8},{10,11... | collective-permute-start | bytes 393224 | tf_op jit(solution)/shard_map/ppermute | solution.py:321
  22.6 7.0 %collective-permute-start.10 = (bf16[256,128]{1,0:T(8,128)(2,1)S(1)}, bf16[256,128]{1,0:T(8,128)(2,1)S(1)}, u32[]{:S(2)}, u32[]{:S(2)}) collective-permute-start(bf16[256,128]{1,0:T(8,128)(2,1)S(1)} %get-tuple-element.43), channel_id=1, source_target_pairs={{0,2},{1,3},{2,0},{3,1},{4,6},{5,7},{6,4},{7,5},{8,10},{9,11},{10,... | collective-permute-start | bytes 196616 | tf_op jit(solution)/shard_map/ppermute | solution.py:321
  25.3 9.0 %collective-permute-start.11 = (bf16[256,128]{1,0:T(8,128)(2,1)S(1)}, bf16[256,128]{1,0:T(8,128)(2,1)S(1)}, u32[]{:S(2)}, u32[]{:S(2)}) collective-permute-start(bf16[256,128]{1,0:T(8,128)(2,1)S(1)} %get-tuple-element.44), channel_id=1, source_target_pairs={{0,3},{1,2},{2,1},{3,0},{4,7},{5,6},{6,5},{7,4},{8,11},{9,10},{10,... | collective-permute-start | bytes 196616 | tf_op jit(solution)/shard_map/ppermute | solution.py:321
  27.8 13.5 %collective-permute-start.9 = (bf16[768,128]{1,0:T(8,128)(2,1)S(1)}, bf16[768,128]{1,0:T(8,128)(2,1)S(1)}, u32[]{:S(2)}, u32[]{:S(2)}) collective-permute-start(bf16[768,128]{1,0:T(8,128)(2,1)S(1)} %add_convert_fusion.1), channel_id=1, source_target_pairs={{0,2},{1,3},{2,0},{3,1},{4,6},{5,7},{6,4},{7,5},{8,10},{9,11},{10,... | collective-permute-start | bytes 589832 | tf_op jit(solution)/shard_map/ppermute | solution.py:321
